TPU v7x, 32 devices: a whole 2x2x4 slice. The times are simulated.
32 devices in a mesh: ctx: 8 (over y, x, core), fsdp: 4 (over z).
Axes of the slice: x: 2, y: 2, z: 4, core: 2. Of those that a mesh axis runs over, the one named last changes fastest.
Arguments:
- patches: bfloat16 [4, 2048, 1024], P('fsdp', 'ctx'), may hold values from -6 to 6
- cotangent: bfloat16 [4, 2048, 1024], P('fsdp', 'ctx'), may hold values from -6 to 6
- deal_table: int32 [16], replicated, may hold values from 0 to 15, each once
- prompt_len: int32 [4], P('fsdp'), may hold values from 256 to 1024, as said below
- w_query: bfloat16 [1024, 1024], P('fsdp'), may hold values from -0.375 to 0.375
- w_key: bfloat16 [1024, 1024], P('fsdp'), may hold values from -0.1875 to 0.1875
- w_value: bfloat16 [1024, 1024], P('fsdp'), may hold values from -0.1875 to 0.1875
- w_output: bfloat16 [1024, 1024], P('fsdp'), may hold values from -1.5 to 1.5
- w_gate: bfloat16 [1024, 2816], P('fsdp'), may hold values from -0.1875 to 0.1875
- w_up: bfloat16 [1024, 2816], P('fsdp'), may hold values from -0.1875 to 0.1875
- w_down: bfloat16 [2816, 1024], P('fsdp'), may hold values from -0.109375 to 0.109375
- gain_attn: bfloat16 [1024], P('fsdp'), may hold values from 0.5 to 1.5
- gain_ffn: bfloat16 [1024], P('fsdp'), may hold values from 0.5 to 1.5
Outputs:
- layer_out: bfloat16 [4, 2048, 1024], P('fsdp', 'ctx')
- grad_patches: float32 [4, 2048, 1024], P('fsdp', 'ctx')
- grad_w_query: float32 [1024, 1024], P('fsdp')
- grad_w_key: float32 [1024, 1024], P('fsdp')
- grad_w_value: float32 [1024, 1024], P('fsdp')
- grad_w_output: float32 [1024, 1024], P('fsdp')
- grad_w_gate: float32 [1024, 2816], P('fsdp')
- grad_w_up: float32 [1024, 2816], P('fsdp')
- grad_w_down: float32 [2816, 1024], P('fsdp')
- grad_gain_attn: float32 [1024], P('fsdp')
- grad_gain_ffn: float32 [1024], P('fsdp')
Inputs may be any that keep to these rules, and one draw needn't show every extreme that they name: A permutation: stored block s of every group holds the group's patch block deal_table[s]. `prompt_len`: one group's continuations see its whole prompt.
All inputs are finite; a program needn't handle non-finite values.
Results may differ from a plain program's by a relative error of at most 0.025.
Values may be sent and summed in bfloat16 or wider, within the bound.
A program may use at most 384 MiB of HBM per device.

v0:
```python
import math

import jax
import jax.numpy as jnp
from jax import lax
from jax.sharding import PartitionSpec as P

HEADS = 16
HEAD = 64
CONT_LEN = 1024


epsilon = 1e-05
score_scale = 0.125
masked_value = -1e30


def rms_forward(values, gain):
    factor = lax.rsqrt(jnp.mean(values * values, axis=-1, keepdims=True) + epsilon)
    return (values * factor * gain, factor)


def rms_backward(values, factor, gain, grad_normed):
    scaled = grad_normed * gain
    grad_gain = jnp.sum(grad_normed * values * factor, axis=0)
    cubed = factor * factor * factor
    grad_values = factor * scaled - values * cubed * jnp.mean(
        scaled * values, axis=-1, keepdims=True
    )
    return (grad_values, grad_gain)


def segment_of(position, prompt):
    return jnp.where(position < prompt, -1, (position - prompt) // CONT_LEN)


def visible(query_pos, key_pos, prompt, length):
    same = (segment_of(query_pos, prompt)[:, None] == segment_of(key_pos, prompt)[None, :]) & (
        key_pos[None, :] <= query_pos[:, None]
    )
    shared = (query_pos[:, None] >= prompt) & (key_pos[None, :] < length)
    return same | shared


def per_device(
    patches,
    cotangent,
    deal_table,
    prompt_len,
    w_query,
    w_key,
    w_value,
    w_output,
    w_gate,
    w_up,
    w_down,
    gain_attn,
    gain_ffn,
):
    local_rows = patches.shape[1]
    width = patches.shape[2]
    devices_ctx = lax.axis_size("ctx")
    group_tok = local_rows * devices_ctx
    cont_count = group_tok // (2 * CONT_LEN)
    prompt = group_tok - cont_count * CONT_LEN
    block_len = local_rows // 2
    slot_count = 2 * devices_ctx
    key_rows = math.gcd(512, group_tok)
    block_count = group_tok // key_rows
    length = prompt_len[0]

    def positions_of(first_row, count):
        stored = first_row + jnp.arange(count, dtype=jnp.int32)
        slot_ids = stored // block_len
        picked = jnp.where(
            slot_ids[:, None] == jnp.arange(slot_count, dtype=jnp.int32)[None, :],
            deal_table[None, :],
            0,
        )
        return jnp.sum(picked, axis=1) * block_len + stored % block_len

    query_pos = positions_of(lax.axis_index("ctx") * local_rows, local_rows)
    key_pos = positions_of(0, group_tok).reshape(block_count, key_rows)
    (
        full_query,
        full_key,
        full_value,
        full_output,
        full_gate,
        full_up,
        full_down,
        full_gain_attn,
        full_gain_ffn,
    ) = (
        lax.all_gather(w_query, "fsdp", axis=0, tiled=True),
        lax.all_gather(w_key, "fsdp", axis=0, tiled=True),
        lax.all_gather(w_value, "fsdp", axis=0, tiled=True),
        lax.all_gather(w_output, "fsdp", axis=0, tiled=True),
        lax.all_gather(w_gate, "fsdp", axis=0, tiled=True),
        lax.all_gather(w_up, "fsdp", axis=0, tiled=True),
        lax.all_gather(w_down, "fsdp", axis=0, tiled=True),
        lax.all_gather(gain_attn, "fsdp", axis=0, tiled=True),
        lax.all_gather(gain_ffn, "fsdp", axis=0, tiled=True),
    )
    rows_f32 = patches[0].astype(jnp.float32)
    gain_one = full_gain_attn.astype(jnp.float32)
    normed, factor_attn = rms_forward(rows_f32, gain_one)
    normed_low = normed.astype(jnp.bfloat16)
    queries = jnp.dot(normed_low, full_query, preferred_element_type=jnp.float32).astype(
        jnp.bfloat16
    )
    keys_local = jnp.dot(normed_low, full_key, preferred_element_type=jnp.float32).astype(
        jnp.bfloat16
    )
    values_local = jnp.dot(normed_low, full_value, preferred_element_type=jnp.float32).astype(
        jnp.bfloat16
    )
    key_all, value_all = (
        lax.all_gather(keys_local, "ctx", axis=0, tiled=True),
        lax.all_gather(values_local, "ctx", axis=0, tiled=True),
    )
    query_heads = queries.reshape(local_rows, HEADS, HEAD)

    def split_blocks(array):
        return array.reshape(block_count, key_rows, HEADS, HEAD)

    def forward_block(state, block):
        key_block, value_block, block_pos = block
        visible_mask = visible(query_pos, block_pos, prompt, length)

        def forward_update(inner_state):
            maxima, totals, accum = inner_state
            scores = (
                jnp.einsum(
                    "qhe,khe->hqk", query_heads, key_block, preferred_element_type=jnp.float32
                )
                * score_scale
            )
            scores = jnp.where(visible_mask[None], scores, masked_value)
            new_max = jnp.maximum(maxima, jnp.max(scores, axis=-1))
            rescale = jnp.exp(maxima - new_max)
            probs = jnp.where(visible_mask[None], jnp.exp(scores - new_max[:, :, None]), 0.0)
            totals = totals * rescale + jnp.sum(probs, axis=-1)
            accum = accum * rescale.T[:, :, None] + jnp.einsum(
                "hqk,khe->qhe",
                probs.astype(jnp.bfloat16),
                value_block,
                preferred_element_type=jnp.float32,
            )
            return (new_max, totals, accum)

        return (
            lax.cond(jnp.any(visible_mask), forward_update, lambda inner_state: inner_state, state),
            None,
        )

    start_state = (
        jnp.full((HEADS, local_rows), masked_value, jnp.float32),
        jnp.zeros((HEADS, local_rows), jnp.float32),
        jnp.zeros((local_rows, HEADS, HEAD), jnp.float32),
    )
    (maxima, totals, accum), unused = lax.scan(
        forward_block, start_state, (split_blocks(key_all), split_blocks(value_all), key_pos)
    )
    attn_f32 = accum / totals.T[:, :, None]
    log_total = maxima + jnp.log(totals)
    attn_low = attn_f32.astype(jnp.bfloat16).reshape(local_rows, width)
    hidden = rows_f32 + jnp.dot(attn_low, full_output, preferred_element_type=jnp.float32)
    gain_two = full_gain_ffn.astype(jnp.float32)
    normed_ffn, factor_ffn = rms_forward(hidden, gain_two)
    ffn_low = normed_ffn.astype(jnp.bfloat16)
    gate = jnp.dot(ffn_low, full_gate, preferred_element_type=jnp.float32)
    up_proj = jnp.dot(ffn_low, full_up, preferred_element_type=jnp.float32)
    sigmoid = jax.nn.sigmoid(gate)
    activated = gate * sigmoid
    inner_low = (activated * up_proj).astype(jnp.bfloat16)
    layer = hidden + jnp.dot(inner_low, full_down, preferred_element_type=jnp.float32)
    grad_out = cotangent[0].astype(jnp.float32)
    grad_down_in = cotangent[0]
    grad_w_down = jnp.dot(inner_low.T, grad_down_in, preferred_element_type=jnp.float32)
    grad_inner = jnp.dot(grad_down_in, full_down.T, preferred_element_type=jnp.float32)
    grad_gate = (grad_inner * up_proj * sigmoid * (1.0 + gate * (1.0 - sigmoid))).astype(
        jnp.bfloat16
    )
    grad_up = (grad_inner * activated).astype(jnp.bfloat16)
    grad_w_gate = jnp.dot(ffn_low.T, grad_gate, preferred_element_type=jnp.float32)
    grad_w_up = jnp.dot(ffn_low.T, grad_up, preferred_element_type=jnp.float32)
    grad_normed_ffn = jnp.dot(grad_gate, full_gate.T, preferred_element_type=jnp.float32) + jnp.dot(
        grad_up, full_up.T, preferred_element_type=jnp.float32
    )
    grad_hidden_norm, grad_gain_ffn = rms_backward(hidden, factor_ffn, gain_two, grad_normed_ffn)
    grad_hidden = grad_out + grad_hidden_norm
    grad_branch = grad_hidden.astype(jnp.bfloat16)
    grad_w_output = jnp.dot(attn_low.T, grad_branch, preferred_element_type=jnp.float32)
    grad_attn = (
        jnp.dot(grad_branch, full_output.T, preferred_element_type=jnp.float32)
        .astype(jnp.bfloat16)
        .reshape(local_rows, HEADS, HEAD)
    )
    delta = jnp.einsum("qhe,qhe->hq", grad_attn.astype(jnp.float32), attn_f32)
    key_back, value_back = (key_all, value_all)

    def backward_block(grad_query, block):
        key_block, value_block, block_pos = block
        visible_mask = visible(query_pos, block_pos, prompt, length)

        def backward_update(grad_state):
            scores = (
                jnp.einsum(
                    "qhe,khe->hqk", query_heads, key_block, preferred_element_type=jnp.float32
                )
                * score_scale
            )
            probs = jnp.where(visible_mask[None], jnp.exp(scores - log_total[:, :, None]), 0.0)
            grad_probs = jnp.einsum(
                "qhe,khe->hqk", grad_attn, value_block, preferred_element_type=jnp.float32
            )
            grad_scores = (probs * (grad_probs - delta[:, :, None])).astype(jnp.bfloat16)
            grad_state = (
                grad_state
                + jnp.einsum(
                    "hqk,khe->qhe", grad_scores, key_block, preferred_element_type=jnp.float32
                )
                * score_scale
            )
            grad_keys = (
                jnp.einsum(
                    "hqk,qhe->khe", grad_scores, query_heads, preferred_element_type=jnp.float32
                )
                * score_scale
            )
            grad_values = jnp.einsum(
                "hqk,qhe->khe",
                probs.astype(jnp.bfloat16),
                grad_attn,
                preferred_element_type=jnp.float32,
            )
            return (grad_state, (grad_keys, grad_values))

        def skipped(grad_state):
            empty = jnp.zeros((key_rows, HEADS, HEAD), jnp.float32)
            return (grad_state, (empty, empty))

        return lax.cond(jnp.any(visible_mask), backward_update, skipped, grad_query)

    zero_query = jnp.zeros((local_rows, HEADS, HEAD), jnp.float32)
    grad_query, (grad_key_blocks, grad_value_blocks) = lax.scan(
        backward_block, zero_query, (split_blocks(key_back), split_blocks(value_back), key_pos)
    )
    grad_key_sum, grad_value_sum = (
        lax.psum_scatter(
            grad_key_blocks.reshape(group_tok, width).astype(jnp.bfloat16),
            "ctx",
            scatter_dimension=0,
            tiled=True,
        ).astype(jnp.float32),
        lax.psum_scatter(
            grad_value_blocks.reshape(group_tok, width).astype(jnp.bfloat16),
            "ctx",
            scatter_dimension=0,
            tiled=True,
        ).astype(jnp.float32),
    )
    grad_key_low = grad_key_sum.astype(jnp.bfloat16)
    grad_value_low = grad_value_sum.astype(jnp.bfloat16)
    grad_query_low = grad_query.reshape(local_rows, width).astype(jnp.bfloat16)
    grad_w_query = jnp.dot(normed_low.T, grad_query_low, preferred_element_type=jnp.float32)
    grad_w_key = jnp.dot(normed_low.T, grad_key_low, preferred_element_type=jnp.float32)
    grad_w_value = jnp.dot(normed_low.T, grad_value_low, preferred_element_type=jnp.float32)
    grad_normed = (
        jnp.dot(grad_query_low, full_query.T, preferred_element_type=jnp.float32)
        + jnp.dot(grad_key_low, full_key.T, preferred_element_type=jnp.float32)
        + jnp.dot(grad_value_low, full_value.T, preferred_element_type=jnp.float32)
    )
    grad_rows_norm, grad_gain_attn = rms_backward(rows_f32, factor_attn, gain_one, grad_normed)
    grad_rows = grad_hidden + grad_rows_norm
    shards = (
        lax.psum_scatter(
            grad_w_query.astype(jnp.bfloat16), "fsdp", scatter_dimension=0, tiled=True
        ).astype(jnp.float32),
        lax.psum_scatter(
            grad_w_key.astype(jnp.bfloat16), "fsdp", scatter_dimension=0, tiled=True
        ).astype(jnp.float32),
        lax.psum_scatter(
            grad_w_value.astype(jnp.bfloat16), "fsdp", scatter_dimension=0, tiled=True
        ).astype(jnp.float32),
        lax.psum_scatter(
            grad_w_output.astype(jnp.bfloat16), "fsdp", scatter_dimension=0, tiled=True
        ).astype(jnp.float32),
        lax.psum_scatter(
            grad_w_gate.astype(jnp.bfloat16), "fsdp", scatter_dimension=0, tiled=True
        ).astype(jnp.float32),
        lax.psum_scatter(
            grad_w_up.astype(jnp.bfloat16), "fsdp", scatter_dimension=0, tiled=True
        ).astype(jnp.float32),
        lax.psum_scatter(
            grad_w_down.astype(jnp.bfloat16), "fsdp", scatter_dimension=0, tiled=True
        ).astype(jnp.float32),
        lax.psum_scatter(
            grad_gain_attn.astype(jnp.bfloat16), "fsdp", scatter_dimension=0, tiled=True
        ).astype(jnp.float32),
        lax.psum_scatter(
            grad_gain_ffn.astype(jnp.bfloat16), "fsdp", scatter_dimension=0, tiled=True
        ).astype(jnp.float32),
    )
    summed = (
        lax.psum(shards[0].astype(jnp.bfloat16), "ctx").astype(jnp.float32),
        lax.psum(shards[1].astype(jnp.bfloat16), "ctx").astype(jnp.float32),
        lax.psum(shards[2].astype(jnp.bfloat16), "ctx").astype(jnp.float32),
        lax.psum(shards[3].astype(jnp.bfloat16), "ctx").astype(jnp.float32),
        lax.psum(shards[4].astype(jnp.bfloat16), "ctx").astype(jnp.float32),
        lax.psum(shards[5].astype(jnp.bfloat16), "ctx").astype(jnp.float32),
        lax.psum(shards[6].astype(jnp.bfloat16), "ctx").astype(jnp.float32),
        lax.psum(shards[7].astype(jnp.bfloat16), "ctx").astype(jnp.float32),
        lax.psum(shards[8].astype(jnp.bfloat16), "ctx").astype(jnp.float32),
    )
    return (
        layer.astype(jnp.bfloat16)[None],
        grad_rows[None],
        summed[0],
        summed[1],
        summed[2],
        summed[3],
        summed[4],
        summed[5],
        summed[6],
        summed[7],
        summed[8],
    )


def solution(mesh):
    placed = (
        P("fsdp", "ctx", None),
        P("fsdp", "ctx", None),
        P(),
        P("fsdp"),
        P("fsdp", None),
        P("fsdp", None),
        P("fsdp", None),
        P("fsdp", None),
        P("fsdp", None),
        P("fsdp", None),
        P("fsdp", None),
        P("fsdp"),
        P("fsdp"),
    )
    return jax.shard_map(
        per_device,
        mesh=mesh,
        in_specs=placed,
        out_specs=(
            P("fsdp", "ctx", None),
            P("fsdp", "ctx", None),
            P("fsdp", None),
            P("fsdp", None),
            P("fsdp", None),
            P("fsdp", None),
            P("fsdp", None),
            P("fsdp", None),
            P("fsdp", None),
            P("fsdp"),
            P("fsdp"),
        ),
        check_vma=False,
    )
```

profile of v0, /device:TPU:0, one launch (start us, length us, event | category | flops | bytes accessed | tf_op | source)
XLA Modules:
  0.0 1433.3 jit_solution(15015941853190533655)
XLA Ops:
  10.1 12.6 all-gather
  24.6 33.4 %all-gather.12.cloned.1.call-done = bf16[1024,1024]{1,0:T(8,128)(2,1)} async-done(((bf16[256,1024]{1,0:T(8,128)(2,1)}), bf16[1024,1024]{1,0:T(8,128)(2,1)}) %all-gather.12.cloned.1.call-update) | async-done | bytes 2097168 | tf_op jit(solution)/shard_map/all_gather | solution.py:96
  61.4 42.6 %all-gather.18.cloned.1.call-done = bf16[1024,1024]{1,0:T(8,128)(2,1)} async-done(((bf16[256,1024]{1,0:T(8,128)(2,1)}), bf16[1024,1024]{1,0:T(8,128)(2,1)}) %all-gather.18.cloned.1.call-update) | async-done | bytes 2097168 | tf_op jit(solution)/shard_map/all_gather | solution.py:97
  110.3 9.3 all-gather.1
  119.7 30.4 %all-gather.16.cloned.1.call-done = bf16[1024,1024]{1,0:T(8,128)(2,1)} async-done(((bf16[256,1024]{1,0:T(8,128)(2,1)}), bf16[1024,1024]{1,0:T(8,128)(2,1)}) %all-gather.16.cloned.1.call-update) | async-done | bytes 2097168 | tf_op jit(solution)/shard_map/all_gather | solution.py:95
  152.7 35.1 %all-gather.14.cloned.1.call-done = bf16[2048,1024]{1,0:T(8,128)(2,1)} async-done(((bf16[256,1024]{1,0:T(8,128)(2,1)}), bf16[2048,1024]{1,0:T(8,128)(2,1)}) %all-gather.14.cloned.1.call-update) | async-done | bytes 4194320 | tf_op jit(solution)/shard_map/all_gather | solution.py:119
  187.8 12.0 reshape.215
  199.8 9.8 copy.70
  209.6 17.1 %all-gather.20.cloned.1.call-done = bf16[2048,1024]{1,0:T(8,128)(2,1)} async-done(((bf16[256,1024]{1,0:T(8,128)(2,1)}), bf16[2048,1024]{1,0:T(8,128)(2,1)}) %all-gather.20.cloned.1.call-update) | async-done | bytes 4194320 | tf_op jit(solution)/shard_map/all_gather | solution.py:120
  226.7 11.7 reshape.216
  238.5 9.8 copy.71
  248.3 25.8 %while.37 = (s32[]{:T(128)}, f32[16,256]{1,0:T(8,128)S(1)}, f32[16,256]{1,0:T(8,128)S(1)}, f32[256,16,64]{0,2,1:T(8,128)S(1)}, s32[256]{0:T(256)S(1)}, /*index=5...) while((s32[]{:T(128)}, f32[16,256]{1,0:T(8,128)S(1)}, ...), condition=%wide.region_9.10_spmd, body=%wide.region_3.9_spmd.sunk | while | flops 565471488 | bytes 30691068 | solution.py:162
  250.6 8.3 conditional.4
  255.4 3.5 fusion.9
  265.9 8.2 conditional.4
  270.6 3.5 fusion.9
  278.0 102.9 %all-gather.24.cloned.1.call-done = bf16[1024,2816]{1,0:T(8,128)(2,1)} async-done(((bf16[256,2816]{1,0:T(8,128)(2,1)}), bf16[1024,2816]{1,0:T(8,128)(2,1)}) %all-gather.24.cloned.1.call-update) | async-done | bytes 5767184 | tf_op jit(solution)/shard_map/all_gather | solution.py:99
  381.0 5.9 fusion.93
  386.8 100.7 %all-gather.26.cloned.1.call-done = bf16[1024,2816]{1,0:T(8,128)(2,1)} async-done(((bf16[256,2816]{1,0:T(8,128)(2,1)}), bf16[1024,2816]{1,0:T(8,128)(2,1)}) %all-gather.26.cloned.1.call-update) | async-done | bytes 5767184 | tf_op jit(solution)/shard_map/all_gather | solution.py:100
  487.5 5.9 fusion.94
  493.4 100.7 %all-gather.28.cloned.1.call-done = bf16[2816,1024]{1,0:T(8,128)(2,1)} async-done(((bf16[704,1024]{1,0:T(8,128)(2,1)}), bf16[2816,1024]{1,0:T(8,128)(2,1)}) %all-gather.28.cloned.1.call-update) | async-done | bytes 5767184 | tf_op jit(solution)/shard_map/all_gather | solution.py:101
  594.1 20.8 %multiply_convert_fusion = (bf16[256,2816]{1,0:T(8,128)(2,1)S(1)}, bf16[256,2816]{1,0:T(8,128)(2,1)S(1)}, bf16[256,2816]{1,0:T(8,128)(2,1)}) fusion(f32[256,2816]{1,0:T(8,128)} %fusion.93, f32[256,2816]{1,0:T(8,128)} %fusion.94, bf16[2816,1024]{1,0:T(8,128)(2,1)} %all-gather.28.cloned.1.call-done, bf16[1,256,1024]{2,1,0:T(8,128)(2,1)S(1)} %copy-done.21), kind=kOutput, calls=%fused_computation.81 | convolution fusion | flops 1487208448 | bytes 16384000 | tf_op jit(solution)/shard_map/dot_general | solution.py:181
  614.9 5.4 fusion.95
  628.5 40.4 %while.38 = (s32[]{:T(128)}, f32[256,16,64]{0,2,1:T(8,128)}, bf16[4,512,16,64]{1,3,2,0:T(8,128)(2,1)}, bf16[4,512,16,64]{1,3,2,0:T(8,128)(2,1)}, s32[256]{0:T(25...) while((s32[]{:T(128)}, f32[256,16,64]{0,2,1:T(8,128)}, ...), condition=%wide.region_16.17_spmd, body=%wide.region_12.16_spmd.sunk | while | flops 1365522688 | bytes 62329680 | solution.py:247
  630.8 12.4 conditional.5
  633.4 4.6 fusion.23
  655.0 12.4 conditional.5
  657.7 4.6 fusion.23
  668.9 5.7 copy.75
  674.7 3.4 copy.94
  678.5 5.7 copy.76
  684.2 3.4 copy.95
  694.1 57.8 %reduce-scatter.10.cloned.1.call-done = bf16[256,1024]{0,1:T(8,128)(2,1)} async-done(((bf16[2048,1024]{0,1:T(8,128)(2,1)}), bf16[256,1024]{0,1:T(8,128)(2,1)}) %reduce-scatter.10.cloned.1.call-update) | async-done | bytes 524304 | tf_op jit(solution)/shard_map/reduce_scatter | solution.py:251
  755.1 51.2 %reduce-scatter.12.cloned.1.call-done = bf16[256,1024]{0,1:T(8,128)(2,1)} async-done(((bf16[2048,1024]{0,1:T(8,128)(2,1)}), bf16[256,1024]{0,1:T(8,128)(2,1)}) %reduce-scatter.12.cloned.1.call-update) | async-done | bytes 524304 | tf_op jit(solution)/shard_map/reduce_scatter | solution.py:257
  809.6 5.6 convolution_convert_fusion.2
  815.4 5.5 convolution_convert_fusion.1
  822.0 5.5 convolution_convert_fusion
  827.6 25.1 %reduce-scatter.14.cloned.1.call-done = bf16[256,1024]{1,0:T(8,128)(2,1)} async-done(((bf16[1024,1024]{1,0:T(8,128)(2,1)}), bf16[256,1024]{1,0:T(8,128)(2,1)}) %reduce-scatter.14.cloned.1.call-update) | async-done | bytes 524304 | tf_op jit(solution)/shard_map/reduce_scatter | solution.py:278
  852.7 45.1 %reduce-scatter.20.cloned.1.call-done = bf16[256,1024]{1,0:T(8,128)(2,1)} async-done(((bf16[1024,1024]{1,0:T(8,128)(2,1)}), bf16[256,1024]{1,0:T(8,128)(2,1)}) %reduce-scatter.20.cloned.1.call-update) | async-done | bytes 524304 | tf_op jit(solution)/shard_map/reduce_scatter | solution.py:287
  897.8 45.6 %reduce-scatter.16.cloned.1.call-done = bf16[256,1024]{1,0:T(8,128)(2,1)} async-done(((bf16[1024,1024]{1,0:T(8,128)(2,1)}), bf16[256,1024]{1,0:T(8,128)(2,1)}) %reduce-scatter.16.cloned.1.call-update) | async-done | bytes 524304 | tf_op jit(solution)/shard_map/reduce_scatter | solution.py:281
  943.4 45.6 %reduce-scatter.18.cloned.1.call-done = bf16[256,1024]{1,0:T(8,128)(2,1)} async-done(((bf16[1024,1024]{1,0:T(8,128)(2,1)}), bf16[256,1024]{1,0:T(8,128)(2,1)}) %reduce-scatter.18.cloned.1.call-update) | async-done | bytes 524304 | tf_op jit(solution)/shard_map/reduce_scatter | solution.py:284
  989.0 103.6 %reduce-scatter.22.cloned.1.call-done = bf16[256,2816]{1,0:T(8,128)(2,1)} async-done(((bf16[1024,2816]{1,0:T(8,128)(2,1)}), bf16[256,2816]{1,0:T(8,128)(2,1)}) %reduce-scatter.22.cloned.1.call-update) | async-done | bytes 1441808 | tf_op jit(solution)/shard_map/reduce_scatter | solution.py:290
  1092.7 105.0 %reduce-scatter.24.cloned.1.call-done = bf16[256,2816]{1,0:T(8,128)(2,1)} async-done(((bf16[1024,2816]{1,0:T(8,128)(2,1)}), bf16[256,2816]{1,0:T(8,128)(2,1)}) %reduce-scatter.24.cloned.1.call-update) | async-done | bytes 1441808 | tf_op jit(solution)/shard_map/reduce_scatter | solution.py:293
  1197.6 105.0 %reduce-scatter.26.cloned.1.call-done = bf16[704,1024]{1,0:T(8,128)(2,1)} async-done(((bf16[2816,1024]{1,0:T(8,128)(2,1)}), bf16[704,1024]{1,0:T(8,128)(2,1)}) %reduce-scatter.26.cloned.1.call-update) | async-done | bytes 1441808 | tf_op jit(solution)/shard_map/reduce_scatter | solution.py:296
  1306.3 5.7 fusion.55
  1315.5 10.2 all-reduce.4
  1325.8 12.7 all-reduce.2
  1340.9 72.4 %all-reduce.7.cloned.1.call-done = (bf16[256,1024]{1,0:T(8,128)(2,1)}, bf16[256,1024]{1,0:T(8,128)(2,1)}, bf16[256,1024]{1,0:T(8,128)(2,1)}, bf16[256,1024]{1,0:...) async-done(((bf16[256,1024]{1,0:T(8,128)(2,1)}, bf16[256,1024]{1,0:T(8,128)(2,1)}, bf16[256,1024]{1,0:T(8,128)(2,1)}, ...) | async-done | bytes 6422544 | tf_op jit(solution)/shard_map/psum | solution.py:307
  (250 shorter events, 110.5 us)
Async XLA Ops:
  7.2 96.9 %copy-start.3 = (bf16[1,256,1024]{2,1,0:T(8,128)(2,1)S(1)}, bf16[1,256,1024]{2,1,0:T(8,128)(2,1)}, u32[]{:S(2)}) copy-start(bf16[1,256,1024]{2,1,0:T(8,128)(2,1)} %param.21) | copy-start | bytes 1572868
  7.2 50.8 %all-gather.12.cloned.1.call-start = ((), (), s32[]{:S(2)}) async-start(), calls=%async_computation.9 | async-start | bytes 2621440 | tf_op jit(solution)/shard_map/all_gather | solution.py:96
  7.9 96.1 %all-gather.18.cloned.1.call-start = ((), (), s32[]{:S(2)}) async-start(), calls=%async_computation.12 | async-start | bytes 2621440 | tf_op jit(solution)/shard_map/all_gather | solution.py:97
  8.7 141.5 %all-gather.16.cloned.1.call-start = ((), (), s32[]{:S(2)}) async-start(), calls=%async_computation.11 | async-start | bytes 2621440 | tf_op jit(solution)/shard_map/all_gather | solution.py:95
  9.4 178.4 %all-gather.14.cloned.1.call-start = ((), (), s32[]{:S(2)}) async-start(), calls=%async_computation.10 | async-start | bytes 4718592 | tf_op jit(solution)/shard_map/all_gather | solution.py:119
  22.8 127.4 %copy-start.30 = (f32[4,1,256]{2,1,0:T(1,128)}, f32[4,1,256]{2,1,0:T(1,128)S(1)}, u32[]{:S(2)}) copy-start(f32[4,1,256]{2,1,0:T(1,128)S(1)} %convert_element_type.229) | copy-start | bytes 12292
  24.6 125.6 %copy-start.32 = (f32[256]{0:T(256)}, f32[256]{0:T(256)S(1)}, u32[]{:S(2)}) copy-start(f32[256]{0:T(256)S(1)} %get-tuple-element.728) | copy-start | bytes 3076
  61.3 48.8 %copy-start.35 = (s32[16]{0:T(128)S(1)}, s32[16]{0:T(128)}, u32[]{:S(2)}) copy-start(s32[16]{0:T(128)} %param.23) | copy-start | bytes 196
  61.3 48.9 %copy-start.37 = (bf16[256]{0:T(256)(128)(2,1)S(1)}, bf16[256]{0:T(256)(128)(2,1)}, u32[]{:S(2)}) copy-start(bf16[256]{0:T(256)(128)(2,1)} %param.33) | copy-start | bytes 1540
  61.4 165.4 %all-gather.20.cloned.1.call-start = ((), (), s32[]{:S(2)}) async-start(), calls=%async_computation.13 | async-start | bytes 4718592 | tf_op jit(solution)/shard_map/all_gather | solution.py:120
  107.2 167.9 %all-gather.22.cloned.1.call-start = ((), (), s32[]{:S(2)}) async-start(), calls=%async_computation.14 | async-start | bytes 2621440 | tf_op jit(solution)/shard_map/all_gather | solution.py:98
  107.8 273.2 %all-gather.24.cloned.1.call-start = ((), (), s32[]{:S(2)}) async-start(), calls=%async_computation.15 | async-start | bytes 7208960 | tf_op jit(solution)/shard_map/all_gather | solution.py:99
  108.5 379.0 %all-gather.26.cloned.1.call-start = ((), (), s32[]{:S(2)}) async-start(), calls=%async_computation.16 | async-start | bytes 7208960 | tf_op jit(solution)/shard_map/all_gather | solution.py:100
  109.3 484.8 %all-gather.28.cloned.1.call-start = ((), (), s32[]{:S(2)}) async-start(), calls=%async_computation.17 | async-start | bytes 7208960 | tf_op jit(solution)/shard_map/all_gather | solution.py:101
  110.0 641.8 %reduce-scatter.10.cloned.1.call-start = ((), (), s32[]{:S(2)}) async-start(), calls=%async_computation.18 | async-start | bytes 4718592 | tf_op jit(solution)/shard_map/reduce_scatter | solution.py:251
  277.8 344.4 %copy-start.6 = (f32[256,1024]{1,0:T(8,128)}, f32[256,1024]{1,0:T(8,128)S(1)}, u32[]{:S(2)}) copy-start(f32[256,1024]{1,0:T(8,128)S(1)} %get-tuple-element.732) | copy-start | bytes 3145732
  278.0 209.5 %copy-start.11 = (bf16[256,1024]{1,0:T(8,128)(2,1)}, bf16[256,1024]{1,0:T(8,128)(2,1)S(1)}, u32[]{:S(2)}) copy-start(bf16[256,1024]{1,0:T(8,128)(2,1)S(1)} %multiply_convert_fusion.3) | copy-start | bytes 1572868
  386.8 207.2 %copy-start.21 = (bf16[1,256,1024]{2,1,0:T(8,128)(2,1)S(1)}, bf16[1,256,1024]{2,1,0:T(8,128)(2,1)}, u32[]{:S(2)}) copy-start(bf16[1,256,1024]{2,1,0:T(8,128)(2,1)} %param.22) | copy-start | bytes 1572868
  614.9 5.4 copy-start.25
  614.9 5.4 copy-start.24
  614.9 5.4 copy-start.36
  622.6 6.0 copy-start.4
  622.6 3.6 copy-start.9
  633.4 4.6 copy-start
  640.1 3.1 copy-start.1
  657.7 4.6 copy-start
  678.0 128.3 %reduce-scatter.12.cloned.1.call-start = ((), (), s32[]{:S(2)}) async-start(), calls=%async_computation.19 | async-start | bytes 4718592 | tf_op jit(solution)/shard_map/reduce_scatter | solution.py:257
  687.7 4.3 copy-start.5
  687.7 4.3 copy-start.13
  687.7 165.0 %reduce-scatter.14.cloned.1.call-start = ((), (), s32[]{:S(2)}) async-start(), calls=%async_computation.20 | async-start | bytes 2621440 | tf_op jit(solution)/shard_map/reduce_scatter | solution.py:278
  691.9 205.9 %reduce-scatter.20.cloned.1.call-start = ((), (), s32[]{:S(2)}) async-start(), calls=%async_computation.23 | async-start | bytes 2621440 | tf_op jit(solution)/shard_map/reduce_scatter | solution.py:287
  694.0 249.4 %reduce-scatter.16.cloned.1.call-start = ((), (), s32[]{:S(2)}) async-start(), calls=%async_computation.21 | async-start | bytes 2621440 | tf_op jit(solution)/shard_map/reduce_scatter | solution.py:281
  755.1 54.5 %copy-start.12 = (bf16[256,1024]{1,0:T(8,128)(2,1)S(1)}, bf16[256,1024]{1,0:T(8,128)(2,1)}, u32[]{:S(2)}) copy-start(bf16[256,1024]{1,0:T(8,128)(2,1)} %copy-done.11) | copy-start | bytes 1572868
  755.1 233.9 %reduce-scatter.18.cloned.1.call-start = ((), (), s32[]{:S(2)}) async-start(), calls=%async_computation.22 | async-start | bytes 2621440 | tf_op jit(solution)/shard_map/reduce_scatter | solution.py:284
  809.5 283.1 %reduce-scatter.22.cloned.1.call-start = ((), (), s32[]{:S(2)}) async-start(), calls=%async_computation.24 | async-start | bytes 7208960 | tf_op jit(solution)/shard_map/reduce_scatter | solution.py:290
  815.2 382.4 %reduce-scatter.24.cloned.1.call-start = ((), (), s32[]{:S(2)}) async-start(), calls=%async_computation.25 | async-start | bytes 7208960 | tf_op jit(solution)/shard_map/reduce_scatter | solution.py:293
  821.0 481.7 %reduce-scatter.26.cloned.1.call-start = ((), (), s32[]{:S(2)}) async-start(), calls=%async_computation.26 | async-start | bytes 7208960 | tf_op jit(solution)/shard_map/reduce_scatter | solution.py:296
  827.5 475.1 %copy-start.38 = (u32[32]{0:T(128)S(1)}, u32[32]{0:T(128)}, u32[]{:S(2)}) copy-start(u32[32]{0:T(128)} %constant.286) | copy-start | bytes 388
  827.6 476.3 %copy-start.15 = (bf16[256,16,64]{0,2,1:T(8,128)(2,1)S(1)}, bf16[256,16,64]{0,2,1:T(8,128)(2,1)}, u32[]{:S(2)}) copy-start(bf16[256,16,64]{0,2,1:T(8,128)(2,1)} %copy-done.14) | copy-start | bytes 1572868
  827.6 585.8 %all-reduce.7.cloned.1.call-start = ((), (), s32[]{:S(2)}) async-start(), calls=%async_computation.27 | async-start | bytes 12845056 | tf_op jit(solution)/shard_map/psum | solution.py:307
  1302.6 3.6 copy-start.7
  1306.3 5.7 copy-start.18
  1306.3 5.7 copy-start.19
  1312.0 27.6 %copy-start.34 = (f32[256]{0:T(256)S(1)}, f32[256]{0:T(256)}, u32[]{:S(2)}) copy-start(f32[256]{0:T(256)} %get-tuple-element.727) | copy-start | bytes 3076
  1413.3 6.6 copy-start.29
  1413.3 7.7 copy-start.28
  1415.6 7.2 copy-start.27
  1421.1 3.5 copy-start.26
  (13 other events, 25.5 us)
Sparse Core Ops, SparseCore 0:
  9.6 48.3 all-gather.11
  59.5 44.4 all-gather.17
  105.6 44.4 all-gather.15
  152.5 35.3 all-gather.13
  190.1 36.5 all-gather.19
  228.2 45.6 all-gather.21
  275.4 105.4 all-gather.23
  382.5 104.9 all-gather.25
  489.1 104.9 all-gather.27
  678.2 73.6 reduce-scatter.9
  755.2 51.0 reduce-scatter.11
  809.0 43.6 reduce-scatter.13
  855.0 42.8 reduce-scatter.19
  900.6 42.8 reduce-scatter.15
  946.1 42.8 reduce-scatter.17
  991.2 101.4 reduce-scatter.21
  1094.8 102.7 reduce-scatter.23
  1199.8 102.7 reduce-scatter.25
  1306.8 106.5 all-reduce.6
where the time goes:
time: 1430 us
  waiting for transfers between devices  1120 us (78%)
  matrix products  127 us (9%)
  local copies, waits for them, and re-layouts  77.5 us (5%)
  blocking collectives  44.8 us (3%)
  other arithmetic  37.4 us (3%)
  between operations  15.3 us (1%)
    reduce_scatter x1, waiting for transfers between devices, per_device(): lax.psum_scatter(grad_w_down.astype(jnp.bfloat16), 'fsdp', scatter_dimens...  105 us
    reduce_scatter x1, waiting for transfers between devices, per_device(): lax.psum_scatter(grad_w_up.astype(jnp.bfloat16), 'fsdp', scatter_dimensio...  105 us
    reduce_scatter x1, waiting for transfers between devices, per_device(): lax.psum_scatter(grad_w_gate.astype(jnp.bfloat16), 'fsdp', scatter_dimens...  104 us
    all_gather x1, waiting for transfers between devices, per_device(): lax.all_gather(w_gate, 'fsdp', axis=0, tiled=True)  103 us
    all_gather x1, waiting for transfers between devices, per_device(): lax.all_gather(w_down, 'fsdp', axis=0, tiled=True)  101 us
    all_gather x1, waiting for transfers between devices, per_device(): lax.all_gather(w_up, 'fsdp', axis=0, tiled=True)  101 us
    psum x1, waiting for transfers between devices, per_device(): lax.psum(shards[0].astype(jnp.bfloat16), 'ctx').astype(jnp.float32)  72.4 us
    reduce_scatter x1, waiting for transfers between devices, per_device(): lax.psum_scatter(grad_key_blocks.reshape(group_tok, width).astype(jnp.bfl...  57.8 us
  transfers between devices with their start and end apart: 19, of which 18 were waited for; matrix products, arithmetic and copies ran while one was open for 10% of the time, Pallas kernels for 0%

commit v1 on v0

--- a/solution.py
+++ b/solution.py
@@ -1,8 +1,11 @@
+import functools
 import math
 
 import jax
 import jax.numpy as jnp
 from jax import lax
+from jax.experimental import pallas as pl
+from jax.experimental.pallas import tpu as pltpu
 from jax.sharding import PartitionSpec as P
 
 HEADS = 16
@@ -42,7 +45,7 @@
     return same | shared
 
 
-def per_device(
+def rows_plan(
     patches,
     cotangent,
     deal_table,
@@ -329,7 +332,394 @@
     )
 
 
+TILE = 256
+
+
+def dot_f32(left, right, left_dim, right_dim):
+    return lax.dot_general(
+        left,
+        right,
+        (((left_dim,), (right_dim,)), ((), ())),
+        preferred_element_type=jnp.float32,
+    )
+
+
+def head_masks():
+    lane = lax.broadcasted_iota(jnp.int32, (TILE, 2 * HEAD), 1)
+    first = (lane < HEAD).astype(jnp.bfloat16)
+    return first, (1 - first).astype(jnp.bfloat16)
+
+
+def stack_heads(tile, masks):
+    return jnp.concatenate([tile * masks[0], tile * masks[1]], axis=0)
+
+
+def tile_mask(kind, tile, length):
+    row = lax.broadcasted_iota(jnp.int32, (TILE, 2 * TILE), 0)
+    if kind == "diagonal":
+        column = lax.broadcasted_iota(jnp.int32, (TILE, 2 * TILE), 1)
+        return row <= jnp.where(column < TILE, column, column - TILE)
+    return row + tile * TILE < length
+
+
+def over_keys(tile, per_segment, step, state):
+    base = tile // per_segment * per_segment
+    state = lax.fori_loop(0, base, lambda key, kept: step(key, kept, "prompt"), state)
+    state = lax.fori_loop(base, tile, lambda key, kept: step(key, kept, "full"), state)
+    return step(tile, state, "diagonal")
+
+
+def to_logical(slot_of, source, column, target, blocks, block_len, scale=None):
+    for block in range(blocks):
+        first = pl.multiple_of(slot_of[block] * block_len, block_len)
+        picked = source[pl.ds(first, block_len), column : column + 2 * HEAD]
+        if scale is not None:
+            picked = picked * scale
+        target[block * block_len : (block + 1) * block_len, :] = picked
+
+
+def to_stored(block_of, source, target, column, blocks, block_len):
+    for slot in range(blocks):
+        first = pl.multiple_of(block_of[slot] * block_len, block_len)
+        target[slot * block_len : (slot + 1) * block_len, column : column + 2 * HEAD] = source[
+            pl.ds(first, block_len), :
+        ]
+
+
+def attend_forward(
+    per_segment, slot_of, block_of, length_ref, qkv, attn, attn_t, lse, query, key, value_t, kept
+):
+    rows = qkv.shape[0]
+    blocks = slot_of.shape[0]
+    block_len = rows // blocks
+    length = length_ref[0]
+    to_logical(slot_of, qkv, 0, query, blocks, block_len, jnp.bfloat16(score_scale))
+    to_logical(slot_of, qkv, 2 * HEAD, key, blocks, block_len)
+    to_logical(slot_of, qkv, 4 * HEAD, kept, blocks, block_len)
+    for tile in range(rows // TILE):
+        value_t[tile] = kept[tile * TILE : (tile + 1) * TILE, :].T
+    masks = head_masks()
+
+    def one_tile(tile, unused):
+        rows_at = pl.ds(pl.multiple_of(tile * TILE, TILE), TILE)
+        both = stack_heads(query[rows_at, :], masks)
+
+        def step(key_tile, state, kind):
+            maxima, totals, accum = state
+            keys_at = pl.ds(pl.multiple_of(key_tile * TILE, TILE), TILE)
+            scores = dot_f32(key[keys_at, :], both, 1, 1)
+            if kind != "full":
+                scores = jnp.where(tile_mask(kind, key_tile, length), scores, masked_value)
+            new_max = jnp.maximum(maxima, jnp.max(scores, axis=0, keepdims=True))
+            probs = jnp.exp(scores - new_max)
+            rescale = jnp.exp(maxima - new_max)
+            totals = totals * rescale + jnp.sum(probs, axis=0, keepdims=True)
+            accum = accum * rescale + dot_f32(
+                value_t[key_tile], probs.astype(jnp.bfloat16), 1, 0
+            )
+            return new_max, totals, accum
+
+        maxima, totals, accum = over_keys(
+            tile,
+            per_segment,
+            step,
+            (
+                jnp.full((1, 2 * TILE), masked_value, jnp.float32),
+                jnp.zeros((1, 2 * TILE), jnp.float32),
+                jnp.zeros((2 * HEAD, 2 * TILE), jnp.float32),
+            ),
+        )
+        accum = accum / totals
+        feature = lax.broadcasted_iota(jnp.int32, (2 * HEAD, TILE), 0)
+        picked = jnp.where(feature < HEAD, accum[:, :TILE], accum[:, TILE:])
+        attn_t[tile] = picked
+        lse[tile] = maxima + jnp.log(totals)
+        kept[rows_at, :] = picked.T.astype(jnp.bfloat16)
+        return unused
+
+    lax.fori_loop(0, rows // TILE, one_tile, 0)
+    to_stored(block_of, kept, attn, 0, blocks, block_len)
+
+
+def attend_backward(
+    per_segment,
+    slot_of,
+    block_of,
+    length_ref,
+    qkv,
+    grad_attn,
+    attn_t,
+    lse,
+    grad_qkv,
+    query,
+    key,
+    value,
+    grad,
+    key_t,
+    grad_key,
+    grad_value,
+):
+    rows = qkv.shape[0]
+    blocks = slot_of.shape[0]
+    block_len = rows // blocks
+    length = length_ref[0]
+    to_logical(slot_of, qkv, 0, query, blocks, block_len, jnp.bfloat16(score_scale))
+    to_logical(slot_of, qkv, 2 * HEAD, key, blocks, block_len)
+    to_logical(slot_of, qkv, 4 * HEAD, value, blocks, block_len)
+    to_logical(slot_of, grad_attn, 0, grad, blocks, block_len)
+    for tile in range(rows // TILE):
+        key_t[tile] = key[tile * TILE : (tile + 1) * TILE, :].T
+    grad_key[...] = jnp.zeros_like(grad_key)
+    grad_value[...] = jnp.zeros_like(grad_value)
+    masks = head_masks()
+
+    def one_tile(tile, unused):
+        rows_at = pl.ds(pl.multiple_of(tile * TILE, TILE), TILE)
+        both = stack_heads(query[rows_at, :], masks)
+        grad_tile = grad[rows_at, :]
+        both_grad = stack_heads(grad_tile, masks)
+        product = grad_tile.astype(jnp.float32).T * attn_t[tile]
+        delta = jnp.concatenate(
+            [
+                jnp.sum(product[:HEAD], axis=0, keepdims=True),
+                jnp.sum(product[HEAD:], axis=0, keepdims=True),
+            ],
+            axis=1,
+        )
+        log_total = lse[tile]
+
+        def step(key_tile, grad_query, kind):
+            keys_at = pl.ds(pl.multiple_of(key_tile * TILE, TILE), TILE)
+            scores = dot_f32(key[keys_at, :], both, 1, 1)
+            if kind != "full":
+                scores = jnp.where(tile_mask(kind, key_tile, length), scores, masked_value)
+            probs = jnp.exp(scores - log_total)
+            grad_probs = dot_f32(value[keys_at, :], both_grad, 1, 1)
+            grad_scores = (probs * (grad_probs - delta)).astype(jnp.bfloat16)
+            grad_value[keys_at, :] += dot_f32(probs.astype(jnp.bfloat16), both_grad, 1, 0)
+            grad_key[keys_at, :] += dot_f32(grad_scores, both, 1, 0)
+            return grad_query + dot_f32(key_t[key_tile], grad_scores, 1, 0)
+
+        grad_query = over_keys(
+            tile, per_segment, step, jnp.zeros((2 * HEAD, 2 * TILE), jnp.float32)
+        )
+        feature = lax.broadcasted_iota(jnp.int32, (2 * HEAD, TILE), 0)
+        picked = jnp.where(feature < HEAD, grad_query[:, :TILE], grad_query[:, TILE:])
+        query[rows_at, :] = (picked * score_scale).T.astype(jnp.bfloat16)
+        return unused
+
+    lax.fori_loop(0, rows // TILE, one_tile, 0)
+    key[...] = grad_key[...].astype(jnp.bfloat16)
+    value[...] = grad_value[...].astype(jnp.bfloat16)
+    to_stored(block_of, query, grad_qkv, 0, blocks, block_len)
+    to_stored(block_of, key, grad_qkv, 2 * HEAD, blocks, block_len)
+    to_stored(block_of, value, grad_qkv, 4 * HEAD, blocks, block_len)
+
+
+def heads_plan(
+    patches,
+    cotangent,
+    deal_table,
+    prompt_len,
+    w_query,
+    w_key,
+    w_value,
+    w_output,
+    w_gate,
+    w_up,
+    w_down,
+    gain_attn,
+    gain_ffn,
+):
+    local_rows = patches.shape[1]
+    width = patches.shape[2]
+    devices_ctx = lax.axis_size("ctx")
+    devices_fsdp = lax.axis_size("fsdp")
+    me = lax.axis_index("ctx")
+    group_tok = local_rows * devices_ctx
+    slot_count = deal_table.shape[0]
+    cols = width // devices_ctx
+    part = w_down.shape[0] // devices_ctx
+    hidden_units = part * devices_fsdp
+    slots = jnp.arange(slot_count, dtype=jnp.int32)
+    slot_of = jnp.sum(
+        jnp.where(deal_table[None, :] == slots[:, None], slots[None, :], 0), axis=1
+    ).astype(jnp.int32)
+
+    def columns_of(weight):
+        return lax.dynamic_slice_in_dim(weight, me * cols, cols, 1)
+
+    def units_of(weight):
+        split = weight.reshape(weight.shape[0], devices_fsdp, devices_ctx, part)
+        return lax.dynamic_index_in_dim(split, me, 2, keepdims=False).reshape(
+            weight.shape[0], hidden_units
+        )
+
+    def rows_gathered(array):
+        return lax.all_gather(array, "fsdp", axis=0, tiled=True)
+
+    w_qkv = rows_gathered(
+        jnp.concatenate([columns_of(w_query), columns_of(w_key), columns_of(w_value)], axis=1)
+    )
+    full_output = rows_gathered(w_output)
+    gate_up = rows_gathered(jnp.concatenate([units_of(w_gate), units_of(w_up)], axis=1))
+    my_gate, my_up = gate_up[:, :hidden_units], gate_up[:, hidden_units:]
+    my_down = rows_gathered(lax.dynamic_slice_in_dim(w_down, me * part, part, 0))
+    gains = lax.all_gather(jnp.stack([gain_attn, gain_ffn]), "fsdp", axis=1, tiled=True)
+    gain_one = gains[0].astype(jnp.float32)
+    gain_two = gains[1].astype(jnp.float32)
+
+    rows_f32 = patches[0].astype(jnp.float32)
+    all_rows = lax.all_gather(patches[0], "ctx", axis=0, tiled=True)
+    normed, unused = rms_forward(all_rows.astype(jnp.float32), gain_one)
+    normed_low = normed.astype(jnp.bfloat16)
+    qkv = jnp.dot(normed_low, w_qkv, preferred_element_type=jnp.float32).astype(jnp.bfloat16)
+
+    tiles = group_tok // TILE
+    per_segment = CONT_LEN // TILE
+    smem = pl.BlockSpec(memory_space=pltpu.SMEM)
+    vmem = pl.BlockSpec(memory_space=pltpu.VMEM)
+    attn, attn_t, lse = pl.pallas_call(
+        functools.partial(attend_forward, per_segment),
+        out_shape=(
+            jax.ShapeDtypeStruct((group_tok, cols), jnp.bfloat16),
+            jax.ShapeDtypeStruct((tiles, cols, TILE), jnp.float32),
+            jax.ShapeDtypeStruct((tiles, 1, 2 * TILE), jnp.float32),
+        ),
+        in_specs=[smem, smem, smem, vmem],
+        out_specs=(vmem, vmem, vmem),
+        scratch_shapes=[
+            pltpu.VMEM((group_tok, cols), jnp.bfloat16),
+            pltpu.VMEM((group_tok, cols), jnp.bfloat16),
+            pltpu.VMEM((tiles, cols, TILE), jnp.bfloat16),
+            pltpu.VMEM((group_tok, cols), jnp.bfloat16),
+        ],
+        name="attend_forward",
+    )(slot_of, deal_table, prompt_len, qkv)
+
+    def to_rows(array):
+        moved = lax.all_to_all(
+            array.reshape(devices_ctx, local_rows, cols), "ctx", split_axis=0, concat_axis=0
+        )
+        return moved.transpose(1, 0, 2).reshape(local_rows, width)
+
+    def to_heads(array):
+        moved = array.reshape(local_rows, devices_ctx, cols).transpose(1, 0, 2)
+        return lax.all_to_all(moved, "ctx", split_axis=0, concat_axis=0).reshape(group_tok, cols)
+
+    attn_rows = to_rows(attn)
+    hidden = rows_f32 + jnp.dot(attn_rows, full_output, preferred_element_type=jnp.float32)
+    normed_ffn, factor_ffn = rms_forward(hidden, gain_two)
+    ffn_low = lax.all_gather(normed_ffn.astype(jnp.bfloat16), "ctx", axis=0, tiled=True)
+    grad_down_in = lax.all_gather(cotangent[0], "ctx", axis=0, tiled=True)
+    gate = jnp.dot(ffn_low, my_gate, preferred_element_type=jnp.float32)
+    up_proj = jnp.dot(ffn_low, my_up, preferred_element_type=jnp.float32)
+    sigmoid = jax.nn.sigmoid(gate)
+    activated = gate * sigmoid
+    inner_low = (activated * up_proj).astype(jnp.bfloat16)
+
+    def summed_rows(array):
+        return lax.psum_scatter(
+            array.astype(jnp.bfloat16), "ctx", scatter_dimension=0, tiled=True
+        ).astype(jnp.float32)
+
+    grad_inner = jnp.dot(grad_down_in, my_down.T, preferred_element_type=jnp.float32)
+    grad_gate = (grad_inner * up_proj * sigmoid * (1.0 + gate * (1.0 - sigmoid))).astype(
+        jnp.bfloat16
+    )
+    grad_up = (grad_inner * activated).astype(jnp.bfloat16)
+    grad_normed_ffn = summed_rows(
+        jnp.dot(grad_gate, my_gate.T, preferred_element_type=jnp.float32)
+        + jnp.dot(grad_up, my_up.T, preferred_element_type=jnp.float32)
+    )
+    layer = hidden + summed_rows(jnp.dot(inner_low, my_down, preferred_element_type=jnp.float32))
+    grad_w_gate = jnp.dot(ffn_low.T, grad_gate, preferred_element_type=jnp.float32)
+    grad_w_up = jnp.dot(ffn_low.T, grad_up, preferred_element_type=jnp.float32)
+    grad_w_down = jnp.dot(inner_low.T, grad_down_in, preferred_element_type=jnp.float32)
+
+    grad_hidden_norm, grad_gain_ffn = rms_backward(hidden, factor_ffn, gain_two, grad_normed_ffn)
+    grad_hidden = cotangent[0].astype(jnp.float32) + grad_hidden_norm
+    grad_branch = grad_hidden.astype(jnp.bfloat16)
+    grad_w_output = jnp.dot(attn_rows.T, grad_branch, preferred_element_type=jnp.float32)
+    grad_attn = to_heads(
+        jnp.dot(grad_branch, full_output.T, preferred_element_type=jnp.float32).astype(
+            jnp.bfloat16
+        )
+    )
+    grad_qkv = pl.pallas_call(
+        functools.partial(attend_backward, per_segment),
+        out_shape=jax.ShapeDtypeStruct((group_tok, 3 * cols), jnp.bfloat16),
+        in_specs=[smem, smem, smem, vmem, vmem, vmem, vmem],
+        out_specs=vmem,
+        scratch_shapes=[
+            pltpu.VMEM((group_tok, cols), jnp.bfloat16),
+            pltpu.VMEM((group_tok, cols), jnp.bfloat16),
+            pltpu.VMEM((group_tok, cols), jnp.bfloat16),
+            pltpu.VMEM((group_tok, cols), jnp.bfloat16),
+            pltpu.VMEM((tiles, cols, TILE), jnp.bfloat16),
+            pltpu.VMEM((group_tok, cols), jnp.float32),
+            pltpu.VMEM((group_tok, cols), jnp.float32),
+        ],
+        name="attend_backward",
+    )(slot_of, deal_table, prompt_len, qkv, grad_attn, attn_t, lse)
+    grad_w_qkv = jnp.dot(normed_low.T, grad_qkv, preferred_element_type=jnp.float32)
+    grad_normed = summed_rows(jnp.dot(grad_qkv, w_qkv.T, preferred_element_type=jnp.float32))
+    factor_attn = lax.rsqrt(jnp.mean(rows_f32 * rows_f32, axis=-1, keepdims=True) + epsilon)
+    grad_rows_norm, grad_gain_attn = rms_backward(rows_f32, factor_attn, gain_one, grad_normed)
+    grad_rows = grad_hidden + grad_rows_norm
+
+    def scattered(array, axis=0):
+        return lax.psum_scatter(
+            array.astype(jnp.bfloat16), "fsdp", scatter_dimension=axis, tiled=True
+        )
+
+    def spread(array):
+        return lax.all_gather(array, "ctx", axis=0, tiled=False)
+
+    qkv_shard = spread(scattered(grad_w_qkv))
+
+    def columns_back(index):
+        piece = qkv_shard[:, :, index * cols : (index + 1) * cols]
+        return piece.transpose(1, 0, 2).reshape(-1, width).astype(jnp.float32)
+
+    gate_up_shard = spread(scattered(jnp.concatenate([grad_w_gate, grad_w_up], axis=1)))
+
+    def units_back(index):
+        piece = gate_up_shard[:, :, index * hidden_units : (index + 1) * hidden_units]
+        piece = piece.reshape(devices_ctx, -1, devices_fsdp, part).transpose(1, 2, 0, 3)
+        return piece.reshape(-1, devices_fsdp * devices_ctx * part).astype(jnp.float32)
+
+    down_shard = spread(scattered(grad_w_down)).reshape(-1, width).astype(jnp.float32)
+    output_part = lax.psum_scatter(
+        grad_w_output.astype(jnp.bfloat16), "ctx", scatter_dimension=1, tiled=True
+    )
+    output_shard = spread(scattered(output_part)).transpose(1, 0, 2).reshape(-1, width)
+    gains_sum = lax.psum(
+        lax.psum_scatter(
+            jnp.stack([grad_gain_attn, grad_gain_ffn]), "fsdp", scatter_dimension=1, tiled=True
+        ),
+        "ctx",
+    )
+    return (
+        layer.astype(jnp.bfloat16)[None],
+        grad_rows[None],
+        columns_back(0),
+        columns_back(1),
+        columns_back(2),
+        output_shard.astype(jnp.float32),
+        units_back(0),
+        units_back(1),
+        down_shard,
+        gains_sum[0],
+        gains_sum[1],
+    )
+
+
 def solution(mesh):
+    if HEADS % mesh.shape["ctx"] == 0:
+        per_device = heads_plan
+    else:
+        per_device = rows_plan
     placed = (
         P("fsdp", "ctx", None),
         P("fsdp", "ctx", None),

time: 1430 us -> 683 us (0.48)
  waiting for transfers between devices: 1120 us -> 399 us
  matrix products: 127 us -> 64 us
  Pallas kernels: 0 us -> 44.5 us
  blocking collectives: 44.8 us -> 88.6 us
  local copies, waits for them, and re-layouts: 77.5 us -> 38.5 us
  other arithmetic: 37.4 us -> 21.7 us
    reduce_scatter x9 -> x7, waiting for transfers between devices: 584 us -> 171 us  [the longest x3 134 us: summed_rows(): lax.psum_scatter(array.astype(jnp.bfloat16), 'ctx', scatter_dimension=0,...]
    all_gather x9 -> x8, waiting for transfers between devices: 463 us -> 161 us  [the longest x3 63.6 us: spread(): return lax.all_gather(array, 'ctx', axis=0, tiled=False)]
    psum x1 -> x0, waiting for transfers between devices: 72.4 us -> none  [per_device(): lax.psum(shards[0].astype(jnp.bfloat16), 'ctx').astype(jnp.float32)]
    dot_general x35 -> x15, matrix products: 127 us -> 64 us  [the longest x1 7.79 us: heads_plan(): jnp.dot(grad_down_in, my_down.T, preferred_element_type=jnp.float32)]
    unnamed x19, waiting for transfers between devices: 4.85 us -> 65.8 us
    pallas_call x0 -> x2, Pallas kernels: none -> 44.5 us  [the longest x1 22.8 us: heads_plan(): pl.pallas_call(functools.partial(attend_backward, per_segment), out_shape...]
    all_gather x2 -> x4, blocking collectives: 22 us -> 63.8 us  [the longest x2 41 us: rows_gathered(): return lax.all_gather(array, 'fsdp', axis=0, tiled=True)]
    reshape x2, local copies, waits for them, and re-layouts: 23.7 us -> 2.13 us  [the longest x1 2.04 us: to_rows(): array.reshape(devices_ctx, local_rows, cols)]
  transfers between devices with their start and end apart: 19 -> 18, of which waited for: 18 -> 16; matrix products, arithmetic and copies ran while one was open for 10% -> 15% of each run, Pallas kernels for 0% -> 7%
where the time goes in v1:
time: 683 us; the launch traced here: 676 us
  waiting for transfers between devices  399 us (58%)
  blocking collectives  88.6 us (13%)
  matrix products  64 us (9%)
  Pallas kernels  44.5 us (7%)
  local copies, waits for them, and re-layouts  38.5 us (6%)
  other arithmetic  21.7 us (3%)
  between operations  15.4 us (2%)
    reduce_scatter x3, waiting for transfers between devices, summed_rows(): lax.psum_scatter(array.astype(jnp.bfloat16), 'ctx', scatter_dimension=0,...  134 us
    unnamed x19, waiting for transfers between devices  65.8 us
    all_gather x3, waiting for transfers between devices, spread(): return lax.all_gather(array, 'ctx', axis=0, tiled=False)  63.6 us
    all_gather x2, blocking collectives, rows_gathered(): return lax.all_gather(array, 'fsdp', axis=0, tiled=True)  41 us
    all_gather x1, waiting for transfers between devices, heads_plan(): lax.all_gather(normed_ffn.astype(jnp.bfloat16), 'ctx', axis=0, tiled=True)  38 us
    reduce_scatter x4, waiting for transfers between devices, scattered(): lax.psum_scatter(array.astype(jnp.bfloat16), 'fsdp', scatter_dimension=ax...  37.1 us
    all_gather x1, waiting for transfers between devices, heads_plan(): grad_down_in = lax.all_gather(cotangent[0], 'ctx', axis=0, tiled=True)  29.3 us
    all_gather x2, waiting for transfers between devices, rows_gathered(): return lax.all_gather(array, 'fsdp', axis=0, tiled=True)  28.4 us
  transfers between devices with their start and end apart: 18, of which 16 were waited for; matrix products, arithmetic and copies ran while one was open for 15% of the time, Pallas kernels for 7%

profile of v1, /device:TPU:0, one launch (start us, length us, event | category | flops | bytes accessed | tf_op | source)
XLA Modules:
  0.0 676.0 jit_solution(7262106074326721259)
XLA Ops:
  10.5 2.5 copy.71
  16.1 12.7 %all_gather.49 = bf16[2,1024]{1,0:T(2,128)(2,1)S(1)} all-gather(bf16[2,256]{1,0:T(2,128)(2,1)S(1)} %pad_maximum_fusion.4), channel_id=1, replica_groups=mesh['ctx'=8,'fsdp'=4] {'fsdp'}, dimensions={1}, use_global_device_ids=true | all-gather | bytes 5120 | tf_op jit(solution)/shard_map/all_gather | solution.py:568
  30.5 16.6 %all_gather.50 = bf16[1024,384]{1,0:T(8,128)(2,1)S(1)} all-gather(bf16[256,384]{1,0:T(8,128)(2,1)S(1)} %pad_maximum_fusion.2), channel_id=1, replica_groups=mesh['ctx'=8,'fsdp'=4] {'fsdp'}, dimensions={0}, use_global_device_ids=true | all-gather | bytes 983040 | tf_op jit(solution)/shard_map/all_gather | solution.py:559
  47.1 2.1 all-gather.21.cloned.1.call-done
  49.2 3.2 fusion
  52.7 3.6 convolution_convert_fusion.2.qkv
  56.2 21.7 %attend_forward.1 = (bf16[2048,128]{1,0:T(8,128)(2,1)}, f32[8,128,256]{2,1,0:T(8,128)}, f32[8,1,512]{2,1,0:T(1,128)}) custom-call(s32[16]{0:T(128)} %select_reduce_fusion.slot_of, s32[16]{0:T(128)} %block_of.3, s32[1]{0:T(128)S(6)} %copy.104.length_ref, bf16[2048,384]{1,0:T(8,128)(2,1)} %convolution_convert_fusion.2.qkv), custom_call_target="tpu_custom_call" | custom-call | tf_op jit(solution)/shard_map/attend_forward/pallas_call | solution.py:582
  78.0 2.0 copy.69
  80.0 3.5 all-to-all-start
  83.6 12.9 %all-gather.15.cloned.1.call-done = bf16[1024,1024]{1,0:T(8,128)(2,1)} async-done(((bf16[256,1024]{1,0:T(8,128)(2,1)}), bf16[1024,1024]{1,0:T(8,128)(2,1)}) %all-gather.15.cloned.1.call-update) | async-done | bytes 2097168 | tf_op jit(solution)/shard_map/all_gather | solution.py:559
  96.5 2.6 multiply_reduce_fusion
  101.3 24.4 %all_gather.54 = bf16[352,1024]{1,0:T(8,128)(2,1)S(1)} all-gather(bf16[88,1024]{1,0:T(8,128)(2,1)S(1)} %constant_dynamic-slice_fusion.5), channel_id=1, replica_groups=mesh['ctx'=8,'fsdp'=4] {'fsdp'}, dimensions={0}, use_global_device_ids=true | all-gather | bytes 901120 | tf_op jit(solution)/shard_map/all_gather | solution.py:559
  125.7 15.5 %all-gather.19.cloned.1.call-done = bf16[1024,704]{0,1:T(8,128)(2,1)} async-done(((bf16[256,704]{0,1:T(8,128)(2,1)}), bf16[1024,704]{0,1:T(8,128)(2,1)}) %all-gather.19.cloned.1.call-update) | async-done | bytes 1441808 | tf_op jit(solution)/shard_map/all_gather | solution.py:559
  141.3 38.0 %all-gather.17.cloned.1.call-done = bf16[2048,1024]{1,0:T(8,128)(2,1)} async-done(((bf16[256,1024]{1,0:T(8,128)(2,1)}), bf16[2048,1024]{1,0:T(8,128)(2,1)}) %all-gather.17.cloned.1.call-update) | async-done | bytes 4194320 | tf_op jit(solution)/shard_map/all_gather | solution.py:613
  179.2 5.8 fusion.34
  185.0 3.3 fusion.38
  188.3 29.3 %all-gather.23.cloned.1.call-done = bf16[1,2048,1024]{2,1,0:T(8,128)(2,1)} async-done(((bf16[1,256,1024]{2,1,0:T(8,128)(2,1)}), bf16[1,2048,1024]{2,1,0:T(8,128)(2,1)}) %all-gather.23.cloned.1.call-update) | async-done | bytes 4194320 | tf_op jit(solution)/shard_map/all_gather | solution.py:614
  217.6 7.8 %multiply_convert_fusion = (bf16[2048,352]{0,1:T(8,128)(2,1)S(1)}, bf16[2048,352]{0,1:T(8,128)(2,1)S(1)}, bf16[2048,352]{0,1:T(8,128)(2,1)}) fusion(f32[2048,352]{0,1:T(8,128)} %fusion.38, f32[2048,352]{0,1:T(8,128)} %fusion.34, bf16[352,1024]{1,0:T(8,128)(2,1)S(1)} %all_gather.54, bf16[1,2048,1024]{2,1,0:T(8,128)(2,1)} %all-gather.23.cloned.1.call-done), kind=kOutput, calls=%fused_computation.15 | convolution fusion | flops 1487208448 | bytes 15007744 | tf_op jit(solution)/shard_map/dot_general | solution.py:626
  225.4 2.4 fusion.36
  227.8 4.6 add_convert_fusion
  232.4 5.7 convolution_convert_fusion.1
  238.4 5.7 fusion.11
  244.2 4.7 convolution_convert_fusion.5
  252.0 31.7 %reduce-scatter.16.cloned.1.call-done = bf16[256,1024]{1,0:T(8,128)(2,1)} async-done(((bf16[2048,1024]{1,0:T(8,128)(2,1)}), bf16[256,1024]{1,0:T(8,128)(2,1)}) %reduce-scatter.16.cloned.1.call-update) | async-done | bytes 524304 | tf_op jit(solution)/shard_map/reduce_scatter | solution.py:622
  285.1 53.2 %reduce-scatter.14.cloned.1.call-done = bf16[256,1024]{1,0:T(8,128)(2,1)} async-done(((bf16[2048,1024]{1,0:T(8,128)(2,1)}), bf16[256,1024]{1,0:T(8,128)(2,1)}) %reduce-scatter.14.cloned.1.call-update) | async-done | bytes 524304 | tf_op jit(solution)/shard_map/reduce_scatter | solution.py:622
  338.2 2.4 fusion.24
  342.6 3.9 copy.83
  346.6 2.4 fusion.17
  349.1 12.8 %all_to_all.10 = bf16[8,256,128]{2,1,0:T(8,128)(2,1)} all-to-all(bf16[8,256,128]{2,1,0:T(8,128)(2,1)S(1)} %bitcast.132), channel_id=1, replica_groups=mesh['ctx'=8,'fsdp'=4] {'ctx'}, dimensions={0} | all-to-all | bytes 1048576 | tf_op jit(solution)/shard_map/all_to_all | solution.py:608
  361.9 22.8 %attend_backward.1 = bf16[2048,384]{1,0:T(8,128)(2,1)} custom-call(s32[16]{0:T(128)} %select_reduce_fusion.slot_of, s32[16]{0:T(128)} %block_of.3, s32[1]{0:T(128)S(6)} %copy.104.length_ref, bf16[2048,384]{1,0:T(8,128)(2,1)} %convolution_convert_fusion.2.qkv, bf16[2048,128]{1,0:T(8,128)(2,1)} %bitcast.133, f32[8,128,256]{2,1,0:T(8,128)} %get-tuple-element.15.attn_t, ...), custom_call_target="tpu_custom_call" | custom-call | tf_op jit(solution)/shard_map/attend_backward/pallas_call | solution.py:649
  384.7 6.1 convolution_convert_fusion.4
  391.5 7.3 %reduce-scatter.24.cloned.1.call-done = bf16[256,704]{0,1:T(8,128)(2,1)} async-done(((bf16[1024,704]{0,1:T(8,128)(2,1)}), bf16[256,704]{0,1:T(8,128)(2,1)}) %reduce-scatter.24.cloned.1.call-update) | async-done | bytes 360464 | tf_op jit(solution)/shard_map/reduce_scatter | solution.py:672
  399.0 43.5 %reduce-scatter.28.cloned.1.call-done = bf16[128,1024]{1,0:T(8,128)(2,1)} async-done(((bf16[1024,1024]{1,0:T(8,128)(2,1)}), bf16[128,1024]{1,0:T(8,128)(2,1)}) %reduce-scatter.28.cloned.1.call-update) | async-done | bytes 262160
  444.3 24.2 %reduce-scatter.20.cloned.1.call-done = bf16[256,384]{1,0:T(8,128)(2,1)} async-done(((bf16[1024,384]{1,0:T(8,128)(2,1)}), bf16[256,384]{1,0:T(8,128)(2,1)}) %reduce-scatter.20.cloned.1.call-update) | async-done | bytes 196624 | tf_op jit(solution)/shard_map/reduce_scatter | solution.py:672
  468.9 5.7 convolution_convert_fusion
  475.8 19.0 %all-gather.29.cloned.1.call-done = bf16[704,1024]{1,0:T(8,128)(2,1)} async-done(((bf16[88,1024]{1,0:T(8,128)(2,1)}), bf16[704,1024]{1,0:T(8,128)(2,1)}) %all-gather.29.cloned.1.call-update) | async-done | bytes 1441808 | tf_op jit(solution)/shard_map/all_gather | solution.py:677
  494.8 3.3 convert_element_type.195
  498.1 30.2 %all-gather.27.cloned.1.call-done = bf16[2048,704]{0,1:T(8,128)(2,1)} async-done(((bf16[256,704]{0,1:T(8,128)(2,1)}), bf16[2048,704]{0,1:T(8,128)(2,1)}) %all-gather.27.cloned.1.call-update) | async-done | bytes 2883600 | tf_op jit(solution)/shard_map/all_gather | solution.py:677
  528.3 2.8 copy.94
  534.9 3.4 copy.82
  542.1 3.4 copy.81
  545.5 5.6 reduce-scatter.22.cloned.1.call-done
  551.0 10.1 %all-gather.3 = bf16[2048,128]{1,0:T(8,128)(2,1)S(1)} all-gather(bf16[256,128]{1,0:T(8,128)(2,1)} %reduce-scatter.22.cloned.1.call-done), channel_id=5, replica_groups=mesh['ctx'=8,'fsdp'=4] {'ctx'}, dimensions={0}, use_global_device_ids=true | all-gather | bytes 589824 | tf_op jit(solution)/shard_map/all_gather | solution.py:677
  562.2 14.4 %all-gather.25.cloned.1.call-done = bf16[2048,384]{1,0:T(8,128)(2,1)} async-done(((bf16[256,384]{1,0:T(8,128)(2,1)}), bf16[2048,384]{1,0:T(8,128)(2,1)}) %all-gather.25.cloned.1.call-update) | async-done | bytes 1572880 | tf_op jit(solution)/shard_map/all_gather | solution.py:677
  581.6 49.4 %reduce-scatter.18.cloned.1.call-done = bf16[256,1024]{1,0:T(8,128)(2,1)} async-done(((bf16[2048,1024]{1,0:T(8,128)(2,1)}), bf16[256,1024]{1,0:T(8,128)(2,1)}) %reduce-scatter.18.cloned.1.call-update) | async-done | bytes 524304 | tf_op jit(solution)/shard_map/reduce_scatter | solution.py:622
  633.5 2.3 fusion.22
  635.8 19.6 %reduce-scatter.30.cloned.1.call-done = f32[256,2]{1,0:T(8,128)} async-done(((f32[1024,2]{1,0:T(8,128)}), f32[256,2]{1,0:T(8,128)}) %reduce-scatter.30.cloned.1.call-update) | async-done | bytes 2064
  656.4 12.0 %psum.7 = f32[2,256]{1,0:T(2,128)S(1)} all-reduce(f32[2,256]{1,0:T(2,128)S(1)} %copy.86), channel_id=1, replica_groups=mesh['ctx'=8,'fsdp'=4] {'ctx'}, use_global_device_ids=true, to_apply=%region_17.18 | all-reduce | flops 512 | bytes 4096 | tf_op jit(solution)/shard_map/psum | solution.py:697
  (120 shorter events, 38.4 us)
Async XLA Ops:
  7.2 94.1 %copy-start = (bf16[704,1024]{1,0:T(8,128)(2,1)S(1)}, bf16[704,1024]{1,0:T(8,128)(2,1)}, u32[]{:S(2)}) copy-start(bf16[704,1024]{1,0:T(8,128)(2,1)} %param.23) | copy-start | bytes 4325380
  7.2 42.0 %all-gather.21.cloned.1.call-start = ((), (), s32[]{:S(2)}) async-start(), calls=%async_computation.21 | async-start | bytes 4718592 | tf_op jit(solution)/shard_map/all_gather | solution.py:573
  7.9 88.6 %all-gather.15.cloned.1.call-start = ((), (), s32[]{:S(2)}) async-start(), calls=%async_computation.11 | async-start | bytes 2621440 | tf_op jit(solution)/shard_map/all_gather | solution.py:559
  8.7 132.6 %all-gather.19.cloned.1.call-start = ((), (), s32[]{:S(2)}) async-start(), calls=%async_computation.13 | async-start | bytes 1802240 | tf_op jit(solution)/shard_map/all_gather | solution.py:559
  10.4 5.0 copy-start.16
  10.4 5.6 copy-start.19
  10.4 5.6 copy-start.20
  47.1 5.4 copy-start.11
  49.2 3.4 copy-start.6
  52.5 3.8 copy-start.13
  56.2 40.3 %copy-start.2 = (bf16[1,256,1024]{2,1,0:T(8,128)(2,1)S(1)}, bf16[1,256,1024]{2,1,0:T(8,128)(2,1)}, u32[]{:S(2)}) copy-start(bf16[1,256,1024]{2,1,0:T(8,128)(2,1)} %param.13) | copy-start | bytes 1572868
  80.0 16.5 %all-to-all-start = ((bf16[8,256,128]{1,2,0:T(8,128)(2,1)}), bf16[8,256,128]{1,2,0:T(8,128)(2,1)S(1)}, u32[]{:S(2)}, u32[]{:S(2)}) async-start(bf16[8,256,128]{1,2,0:T(8,128)(2,1)} %copy.69), calls=%async_computation | async-start | bytes 1048576 | tf_op jit(solution)/shard_map/all_to_all | solution.py:601
  83.5 95.7 %all-gather.17.cloned.1.call-start = ((), (), s32[]{:S(2)}) async-start(), calls=%async_computation.12 | async-start | bytes 4718592 | tf_op jit(solution)/shard_map/all_gather | solution.py:613
  96.5 4.1 copy-start.4
  100.7 116.9 %all-gather.23.cloned.1.call-start = ((), (), s32[]{:S(2)}) async-start(), calls=%async_computation.22 | async-start | bytes 4718592 | tf_op jit(solution)/shard_map/all_gather | solution.py:614
  101.2 182.4 %reduce-scatter.16.cloned.1.call-start = ((), (), s32[]{:S(2)}) async-start(), calls=%async_computation.15 | async-start | bytes 4718592 | tf_op jit(solution)/shard_map/reduce_scatter | solution.py:622
  141.3 43.8 %copy-start.8 = (bf16[1024,704]{0,1:T(8,128)(2,1)S(1)}, bf16[1024,704]{0,1:T(8,128)(2,1)}, u32[]{:S(2)}) copy-start(bf16[1024,704]{0,1:T(8,128)(2,1)} %all-gather.19.cloned.1.call-done) | copy-start | bytes 4325380
  179.2 5.8 copy-start.17
  217.6 7.8 %copy-start.9 = (bf16[1024,704]{0,1:T(8,128)(2,1)S(1)}, bf16[1024,704]{0,1:T(8,128)(2,1)}, u32[]{:S(2)}) copy-start(bf16[1024,704]{0,1:T(8,128)(2,1)} %all-gather.19.cloned.1.call-done) | copy-start | bytes 4325380
  225.4 2.4 copy-start.10
  232.4 105.8 %reduce-scatter.14.cloned.1.call-start = ((), (), s32[]{:S(2)}) async-start(), calls=%async_computation.14 | async-start | bytes 4718592 | tf_op jit(solution)/shard_map/reduce_scatter | solution.py:622
  238.1 152.8 %reduce-scatter.26.cloned.1.call-start = ((), (), s32[]{:S(2)}) async-start(), calls=%async_computation.20 | async-start | bytes 901120 | tf_op jit(solution)/shard_map/reduce_scatter | solution.py:672
  244.1 154.8 %reduce-scatter.24.cloned.1.call-start = ((), (), s32[]{:S(2)}) async-start(), calls=%async_computation.19 | async-start | bytes 1802240 | tf_op jit(solution)/shard_map/reduce_scatter | solution.py:672
  244.2 4.7 copy-start.18
  250.6 87.6 %copy-start.7 = (bf16[1,256,1024]{2,1,0:T(8,128)(2,1)S(1)}, bf16[1,256,1024]{2,1,0:T(8,128)(2,1)}, u32[]{:S(2)}) copy-start(bf16[1,256,1024]{2,1,0:T(8,128)(2,1)} %param.14) | copy-start | bytes 1572868
  250.6 87.6 %copy-start.15 = (f32[256]{0:T(256)S(1)}, f32[256]{0:T(256)}, u32[]{:S(2)}) copy-start(f32[256]{0:T(256)} %get-tuple-element.81) | copy-start | bytes 3076
  251.9 88.7 %copy-start.5 = (bf16[8,256,128]{1,2,0:T(8,128)(2,1)S(1)}, bf16[8,256,128]{1,2,0:T(8,128)(2,1)}, u32[]{:S(2)}) copy-start(bf16[8,256,128]{1,2,0:T(8,128)(2,1)} %copy-done.4) | copy-start | bytes 1572868
  251.9 190.5 %reduce-scatter.28.cloned.1.call-start = ((), (), s32[]{:S(2)}) async-start(), calls=%async_computation.26 | async-start | bytes 2359296
  346.6 121.9 %reduce-scatter.20.cloned.1.call-start = ((), (), s32[]{:S(2)}) async-start(), calls=%async_computation.17 | async-start | bytes 983040 | tf_op jit(solution)/shard_map/reduce_scatter | solution.py:672
  349.1 35.6 %copy-start.14 = (f32[2048]{0:T(1024)S(1)}, f32[2048]{0:T(1024)}, u32[]{:S(2)}) copy-start(f32[2048]{0:T(1024)} %copy-done.13) | copy-start | bytes 24580
  384.7 84.1 %copy-start.12 = (bf16[1024,384]{1,0:T(8,128)(2,1)S(1)}, bf16[1024,384]{1,0:T(8,128)(2,1)}, u32[]{:S(2)}) copy-start(bf16[1024,384]{1,0:T(8,128)(2,1)} %copy-done.11) | copy-start | bytes 2359300
  390.9 103.9 %all-gather.29.cloned.1.call-start = ((), (), s32[]{:S(2)}) async-start(), calls=%async_computation.25 | async-start | bytes 1622016 | tf_op jit(solution)/shard_map/all_gather | solution.py:677
  391.5 136.8 %all-gather.27.cloned.1.call-start = ((), (), s32[]{:S(2)}) async-start(), calls=%async_computation.24 | async-start | bytes 3244032 | tf_op jit(solution)/shard_map/all_gather | solution.py:677
  398.9 152.1 %reduce-scatter.22.cloned.1.call-start = ((), (), s32[]{:S(2)}) async-start(), calls=%async_computation.18 | async-start | bytes 327680 | tf_op jit(solution)/shard_map/reduce_scatter | solution.py:672
  444.3 132.3 %all-gather.25.cloned.1.call-start = ((), (), s32[]{:S(2)}) async-start(), calls=%async_computation.23 | async-start | bytes 1769472 | tf_op jit(solution)/shard_map/all_gather | solution.py:677
  468.6 162.4 %reduce-scatter.18.cloned.1.call-start = ((), (), s32[]{:S(2)}) async-start(), calls=%async_computation.16 | async-start | bytes 4718592 | tf_op jit(solution)/shard_map/reduce_scatter | solution.py:622
  474.6 1.0 copy-start.3
  474.6 180.8 %reduce-scatter.30.cloned.1.call-start = ((), (), s32[]{:S(2)}) async-start(), calls=%async_computation.27 | async-start | bytes 655360
  580.5 88.5 %copy-start.1 = (bf16[704,1024]{1,0:T(8,128)(2,1)S(1)}, bf16[704,1024]{1,0:T(8,128)(2,1)}, u32[]{:S(2)}) copy-start(bf16[704,1024]{1,0:T(8,128)(2,1)} %param.23) | copy-start | bytes 4325380
Sparse Core Ops, SparseCore 0:
  9.9 39.2 all-gather.20
  50.8 45.6 all-gather.14
  98.6 42.5 all-gather.18
  143.6 35.6 all-gather.16
  181.0 36.5 all-gather.22
  232.5 51.1 reduce-scatter.15
  287.0 51.1 reduce-scatter.13
  341.1 22.9 reduce-scatter.25
  366.4 32.4 reduce-scatter.23
  402.6 39.8 reduce-scatter.27
  445.3 23.1 reduce-scatter.19
  470.3 24.5 all-gather.28
  496.7 31.5 all-gather.26
  531.0 19.9 reduce-scatter.21
  552.7 23.8 all-gather.24
  579.8 51.1 reduce-scatter.17
  633.6 21.8 reduce-scatter.29

commit v2 on v0

--- a/solution.py
+++ b/solution.py
@@ -1,8 +1,11 @@
+import functools
 import math
 
 import jax
 import jax.numpy as jnp
 from jax import lax
+from jax.experimental import pallas as pl
+from jax.experimental.pallas import tpu as pltpu
 from jax.sharding import PartitionSpec as P
 
 HEADS = 16
@@ -42,7 +45,7 @@
     return same | shared
 
 
-def per_device(
+def rows_plan(
     patches,
     cotangent,
     deal_table,
@@ -329,7 +332,1428 @@
     )
 
 
+TILE = 256
+
+
+def dot_f32(left, right, left_dim, right_dim):
+    return lax.dot_general(
+        left,
+        right,
+        (((left_dim,), (right_dim,)), ((), ())),
+        preferred_element_type=jnp.float32,
+    )
+
+
+def head_masks():
+    lane = lax.broadcasted_iota(jnp.int32, (TILE, 2 * HEAD), 1)
+    first = (lane < HEAD).astype(jnp.bfloat16)
+    return first, (1 - first).astype(jnp.bfloat16)
+
+
+def stack_heads(tile, masks):
+    return jnp.concatenate([tile * masks[0], tile * masks[1]], axis=0)
+
+
+def tile_mask(kind, tile, length):
+    row = lax.broadcasted_iota(jnp.int32, (TILE, 2 * TILE), 0)
+    if kind == "diagonal":
+        column = lax.broadcasted_iota(jnp.int32, (TILE, 2 * TILE), 1)
+        return row <= jnp.where(column < TILE, column, column - TILE)
+    return row + tile * TILE < length
+
+
+def over_keys(tile, per_segment, step, state):
+    base = tile // per_segment * per_segment
+    state = lax.fori_loop(0, base, lambda key, kept: step(key, kept, "prompt"), state)
+    state = lax.fori_loop(base, tile, lambda key, kept: step(key, kept, "full"), state)
+    return step(tile, state, "diagonal")
+
+
+def load_tile(ref, tile):
+    held = TILE // ref.shape[1]
+    return ref[pl.ds(tile * held, held)].reshape(TILE, ref.shape[2])
+
+
+def store_tile(ref, tile, values):
+    held = TILE // ref.shape[1]
+    ref[pl.ds(tile * held, held)] = values.reshape(held, ref.shape[1], ref.shape[2])
+
+
+def to_logical(slot_of, source, column, target, scale=None):
+    for block in range(target.shape[0]):
+        picked = source[slot_of[block], :, column : column + 2 * HEAD]
+        if scale is not None:
+            picked = picked * scale
+        target[block] = picked
+
+
+def to_stored(block_of, source, target, column):
+    block_len = source.shape[1]
+    for slot in range(source.shape[0]):
+        target[slot * block_len : (slot + 1) * block_len, column : column + 2 * HEAD] = source[
+            block_of[slot]
+        ]
+
+
+def tiles_between(count, one_tile, between):
+    first = 0
+    for stop in sorted(between):
+        lax.fori_loop(first, stop, one_tile, 0)
+        between[stop]()
+        first = stop
+    lax.fori_loop(first, count, one_tile, 0)
+
+
+def attend_forward(
+    per_segment,
+    slot_of,
+    block_of,
+    length_ref,
+    qkv,
+    attn,
+    attn_t,
+    lse,
+    query,
+    key,
+    value_t,
+    kept,
+    between,
+):
+    rows = qkv.shape[0] * qkv.shape[1]
+    length = length_ref[0]
+    to_logical(slot_of, qkv, 0, query, jnp.bfloat16(score_scale))
+    to_logical(slot_of, qkv, 2 * HEAD, key)
+    to_logical(slot_of, qkv, 4 * HEAD, kept)
+    for tile in range(rows // TILE):
+        value_t[tile] = load_tile(kept, tile).T
+    masks = head_masks()
+
+    def one_tile(tile, unused):
+        both = stack_heads(load_tile(query, tile), masks)
+
+        def step(key_tile, state, kind):
+            maxima, totals, accum = state
+            scores = dot_f32(load_tile(key, key_tile), both, 1, 1)
+            if kind != "full":
+                scores = jnp.where(tile_mask(kind, key_tile, length), scores, masked_value)
+            new_max = jnp.maximum(maxima, jnp.max(scores, axis=0, keepdims=True))
+            probs = jnp.exp(scores - new_max)
+            rescale = jnp.exp(maxima - new_max)
+            totals = totals * rescale + jnp.sum(probs, axis=0, keepdims=True)
+            accum = accum * rescale + dot_f32(
+                value_t[key_tile], probs.astype(jnp.bfloat16), 1, 0
+            )
+            return new_max, totals, accum
+
+        maxima, totals, accum = over_keys(
+            tile,
+            per_segment,
+            step,
+            (
+                jnp.full((1, 2 * TILE), masked_value, jnp.float32),
+                jnp.zeros((1, 2 * TILE), jnp.float32),
+                jnp.zeros((2 * HEAD, 2 * TILE), jnp.float32),
+            ),
+        )
+        accum = accum / totals
+        feature = lax.broadcasted_iota(jnp.int32, (2 * HEAD, TILE), 0)
+        picked = jnp.where(feature < HEAD, accum[:, :TILE], accum[:, TILE:])
+        attn_t[tile] = picked
+        lse[tile] = maxima + jnp.log(totals)
+        store_tile(kept, tile, picked.T.astype(jnp.bfloat16))
+        return unused
+
+    tiles_between(rows // TILE, one_tile, between)
+    to_stored(block_of, kept, attn, 0)
+
+
+def attend_backward(
+    per_segment,
+    slot_of,
+    block_of,
+    length_ref,
+    qkv,
+    grad_attn,
+    attn_t,
+    lse,
+    grad_qkv,
+    query,
+    key,
+    value,
+    grad,
+    key_t,
+    grad_key,
+    grad_value,
+    between,
+):
+    rows = qkv.shape[0] * qkv.shape[1]
+    length = length_ref[0]
+    to_logical(slot_of, qkv, 0, query, jnp.bfloat16(score_scale))
+    to_logical(slot_of, qkv, 2 * HEAD, key)
+    to_logical(slot_of, qkv, 4 * HEAD, value)
+    to_logical(slot_of, grad_attn, 0, grad)
+    for tile in range(rows // TILE):
+        key_t[tile] = load_tile(key, tile).T
+    grad_key[...] = jnp.zeros_like(grad_key)
+    grad_value[...] = jnp.zeros_like(grad_value)
+    masks = head_masks()
+
+    def one_tile(tile, unused):
+        both = stack_heads(load_tile(query, tile), masks)
+        grad_tile = load_tile(grad, tile)
+        both_grad = stack_heads(grad_tile, masks)
+        product = grad_tile.astype(jnp.float32).T * attn_t[tile]
+        delta = jnp.concatenate(
+            [
+                jnp.sum(product[:HEAD], axis=0, keepdims=True),
+                jnp.sum(product[HEAD:], axis=0, keepdims=True),
+            ],
+            axis=1,
+        )
+        log_total = lse[tile]
+
+        def step(key_tile, grad_query, kind):
+            keys_at = pl.ds(pl.multiple_of(key_tile * TILE, TILE), TILE)
+            scores = dot_f32(load_tile(key, key_tile), both, 1, 1)
+            if kind != "full":
+                scores = jnp.where(tile_mask(kind, key_tile, length), scores, masked_value)
+            probs = jnp.exp(scores - log_total)
+            grad_probs = dot_f32(load_tile(value, key_tile), both_grad, 1, 1)
+            grad_scores = (probs * (grad_probs - delta)).astype(jnp.bfloat16)
+            grad_value[keys_at, :] += dot_f32(probs.astype(jnp.bfloat16), both_grad, 1, 0)
+            grad_key[keys_at, :] += dot_f32(grad_scores, both, 1, 0)
+            return grad_query + dot_f32(key_t[key_tile], grad_scores, 1, 0)
+
+        grad_query = over_keys(
+            tile, per_segment, step, jnp.zeros((2 * HEAD, 2 * TILE), jnp.float32)
+        )
+        feature = lax.broadcasted_iota(jnp.int32, (2 * HEAD, TILE), 0)
+        picked = jnp.where(feature < HEAD, grad_query[:, :TILE], grad_query[:, TILE:])
+        store_tile(query, tile, (picked * score_scale).T.astype(jnp.bfloat16))
+        return unused
+
+    tiles_between(rows // TILE, one_tile, between)
+    key[...] = grad_key[...].astype(jnp.bfloat16).reshape(key.shape)
+    value[...] = grad_value[...].astype(jnp.bfloat16).reshape(value.shape)
+    to_stored(block_of, query, grad_qkv, 0)
+    to_stored(block_of, key, grad_qkv, 2 * HEAD)
+    to_stored(block_of, value, grad_qkv, 4 * HEAD)
+
+
+def dma(count):
+    return pltpu.SemaphoreType.DMA((count,))
+
+
+def flipped(bit, flip):
+    return bit + flip - 2 * bit * flip
+
+
+class Place:
+    def __init__(self, devices_fsdp):
+        self.me = lax.axis_index("ctx")
+        self.core = lax.rem(self.me, 2)
+        self.column = lax.rem(self.me // 2, 2)
+        self.row = self.me // 4
+        self.group = lax.axis_index("fsdp")
+        self.groups = devices_fsdp
+
+    def peer(self, flip):
+        low, middle, high = flip % 2, flip // 2 % 2, flip // 4
+        return (
+            flipped(self.row, high) * 4
+            + flipped(self.column, middle) * 2
+            + flipped(self.core, low)
+        )
+
+    def other_group(self, step):
+        return lax.rem(self.group + step, self.groups)
+
+    def meet(self):
+        barrier = pltpu.get_barrier_semaphore()
+        for flip in range(1, 8):
+            pl.semaphore_signal(barrier, inc=1, device_id={"ctx": self.peer(flip)})
+        for step in range(1, self.groups):
+            pl.semaphore_signal(barrier, inc=1, device_id={"fsdp": self.other_group(step)})
+        pl.semaphore_wait(barrier, 7 + self.groups - 1)
+
+
+def remote(source, target, send, recv, device):
+    return pltpu.make_async_remote_copy(
+        src_ref=source,
+        dst_ref=target,
+        send_sem=send,
+        recv_sem=recv,
+        device_id=device,
+        device_id_type=pl.DeviceIdType.MESH,
+    )
+
+
+class Spread:
+    def __init__(self, place, own, region, send, recv):
+        me, peer = place.me, place.peer
+
+        def copy(index, source, target, flip):
+            return remote(source, target, send.at[index], recv.at[index], {"ctx": peer(flip)})
+
+        self.copies = [
+            copy(0, own(None), region(me, None), 1),
+            copy(1, own(0), region(me, 0), 2),
+            copy(2, own(1), region(me, 1), 2),
+            copy(3, own(1), region(me, 1), 4),
+            copy(4, own(0), region(me, 0), 4),
+            copy(5, region(peer(2), 0), region(peer(2), 0), 4),
+            copy(6, region(peer(4), 1), region(peer(4), 1), 2),
+            copy(7, region(peer(2), None), region(peer(2), None), 1),
+            copy(8, region(peer(4), None), region(peer(4), None), 1),
+            copy(9, region(peer(6), None), region(peer(6), None), 1),
+        ]
+
+    def start(self):
+        for index in (1, 3, 0, 2, 4):
+            self.copies[index].start()
+
+    def arrived(self, *indices):
+        for index in indices:
+            self.copies[index].wait_recv()
+
+    def relay_first(self):
+        self.arrived(1)
+        self.copies[5].start()
+        self.arrived(3)
+        self.copies[6].start()
+
+    def relay_second(self):
+        self.arrived(2)
+        self.copies[7].start()
+        self.arrived(4)
+        self.copies[8].start()
+
+    def relay_third(self):
+        self.arrived(5, 6)
+        self.copies[9].start()
+
+    def sent(self):
+        for copy in self.copies:
+            copy.wait_send()
+
+
+class PairSum:
+    def __init__(self, place, stage, landed, sums, received, send, recv, out_send, out_recv):
+        self.place = place
+        self.stage, self.landed, self.sums, self.received = stage, landed, sums, received
+        self.send, self.recv, self.out_send, self.out_recv = send, recv, out_send, out_recv
+
+    def mine(self, pair):
+        place = self.place
+        return (
+            flipped(place.row, pair // 2) * 4
+            + flipped(place.column, lax.rem(pair, 2)) * 2
+            + place.core
+        )
+
+    def theirs(self, pair):
+        return self.mine(pair) + 1 - 2 * self.place.core
+
+    def exchange(self, pair):
+        return remote(
+            self.stage.at[pair],
+            self.landed.at[pair],
+            self.send.at[pair],
+            self.recv.at[pair],
+            {"ctx": self.place.peer(1)},
+        )
+
+    def deliver(self, pair):
+        return remote(
+            self.sums.at[pair],
+            self.received.at[pair],
+            self.out_send.at[pair],
+            self.out_recv.at[pair],
+            {"ctx": self.mine(pair)},
+        )
+
+    def sent(self):
+        for pair in range(4):
+            self.exchange(pair).wait_send()
+            if pair:
+                self.deliver(pair).wait_send()
+
+
+def halves(count):
+    return lambda half: pl.ds(0 if half in (None, 0) else count // 2, count if half is None else count // 2)
+
+
+def forward_kernel(
+    per_segment,
+    devices_fsdp,
+    slot_of,
+    block_of,
+    length_ref,
+    patches,
+    cotangent,
+    w_query,
+    w_key,
+    w_value,
+    w_output,
+    w_gate,
+    w_up,
+    w_down,
+    gain_attn,
+    gain_ffn,
+    qkv,
+    normed_out,
+    attn_t,
+    lse,
+    qkv_out,
+    gains_out,
+    grad_units,
+    grad_output,
+    layer_sums,
+    hidden,
+    grad_hidden,
+    gain_part,
+    grad_attn_out,
+    normed,
+    grads,
+    normed_ffn,
+    w_qkv,
+    output_all,
+    gate_t,
+    up_t,
+    down,
+    down_parts,
+    gate_stage,
+    up_stage,
+    gain_stage,
+    gains,
+    query,
+    key,
+    value_t,
+    kept,
+    attn,
+    attn_rows,
+    own_ffn,
+    inner_t,
+    grad_gate_t,
+    grad_up_t,
+    stage,
+    landed,
+    own_sum,
+    norm_sums,
+    norm_received,
+    down_tiles,
+    grad_branch,
+    grad_rows,
+    grad_attn,
+    local_sem,
+    group_send,
+    group_recv,
+    x_send,
+    x_recv,
+    g_send,
+    g_recv,
+    o_send,
+    o_recv,
+    f_send,
+    f_recv,
+    a_send,
+    a_recv,
+    b_send,
+    b_recv,
+    pair_send,
+    pair_recv,
+    out_send,
+    out_recv,
+):
+    place = Place(devices_fsdp)
+    me, group = place.me, place.group
+    local_rows, width = patches.shape
+    cols = width // 8
+    shard = w_query.shape[0]
+    part = w_down.shape[1]
+    units = part * devices_fsdp
+    place.meet()
+
+    def rows_of(block, count=local_rows):
+        return pl.ds(pl.multiple_of(block * count, count), count)
+
+    def rows_half(ref):
+        def region(block, half):
+            start = block * local_rows + (local_rows // 2 if half == 1 else 0)
+            count = local_rows if half is None else local_rows // 2
+            return ref.at[pl.ds(pl.multiple_of(start, local_rows // 2), count)]
+
+        return region
+
+    def own_half(ref):
+        return lambda half: ref.at[halves(local_rows)(half)]
+
+    spread_x = Spread(place, own_half(patches), rows_half(normed), x_send, x_recv)
+    spread_x.start()
+
+    my_cols = rows_of(me, cols)
+    my_shard = rows_of(group, shard)
+    group_items = [
+        (w_query.at[:, my_cols], w_qkv.at[my_shard, 0:cols]),
+        (w_key.at[:, my_cols], w_qkv.at[my_shard, cols : 2 * cols]),
+        (w_value.at[:, my_cols], w_qkv.at[my_shard, 2 * cols : 3 * cols]),
+        (gain_stage, gains.at[:, my_shard]),
+        (w_output.at[me], output_all.at[group, me]),
+        (gate_stage, gate_t.at[:, my_shard]),
+        (up_stage, up_t.at[:, my_shard]),
+        (w_down.at[me], down_parts.at[group]),
+    ]
+
+    def group_copies(index):
+        source, target = group_items[index]
+        return [
+            remote(
+                source,
+                target,
+                group_send.at[index, step - 1],
+                group_recv.at[index, step - 1],
+                {"fsdp": place.other_group(step)},
+            )
+            for step in range(1, devices_fsdp)
+        ]
+
+    def local_copy(index):
+        source, target = group_items[index]
+        return pltpu.make_async_copy(source, target, local_sem.at[index])
+
+    def send_group(index):
+        for copy in group_copies(index):
+            copy.start()
+        local_copy(index).start()
+
+    def group_arrived(index):
+        for copy in group_copies(index):
+            copy.wait_recv()
+        local_copy(index).wait()
+
+    for index in (0, 1, 2):
+        send_group(index)
+    gain_stage[0:8, :] = jnp.broadcast_to(gain_attn[...].astype(jnp.float32), (8, shard))
+    gain_stage[8:16, :] = jnp.broadcast_to(gain_ffn[...].astype(jnp.float32), (8, shard))
+    send_group(3)
+    send_group(4)
+
+    def pick_units(weight, target):
+        span = part * 8
+        pieces = []
+        for index in range(devices_fsdp):
+            low = span * index // 128 * 128
+            high = -(-span * (index + 1) // 128) * 128
+            unit = lax.broadcasted_iota(jnp.int32, (part, high - low), 0)
+            column = lax.broadcasted_iota(jnp.int32, (part, high - low), 1)
+            chosen = (column + low == unit + span * index + part * me).astype(jnp.bfloat16)
+            pieces.append(dot_f32(chosen, weight[:, low:high], 1, 1))
+        target[...] = jnp.concatenate(pieces, axis=0).astype(jnp.bfloat16)
+
+    pick_units(w_gate, gate_stage)
+    pick_units(w_up, up_stage)
+    send_group(5)
+    send_group(6)
+    send_group(7)
+
+    normed[rows_of(me), :] = patches[...]
+    grads[rows_of(me), :] = cotangent[...]
+    spread_x.relay_first()
+    spread_x.relay_second()
+    spread_g = Spread(place, own_half(cotangent), rows_half(grads), g_send, g_recv)
+    spread_g.start()
+    spread_x.relay_third()
+    spread_x.arrived(0, 7, 8, 9)
+    for index in (0, 1, 2, 3):
+        group_arrived(index)
+    gain_one = gains[0:1, :]
+
+    def project(block, unused):
+        at = rows_of(block)
+        values = normed[at, :].astype(jnp.float32)
+        low = rms_forward(values, gain_one)[0].astype(jnp.bfloat16)
+        normed[at, :] = low
+        store_tile(qkv, block, dot_f32(low, w_qkv[...], 1, 0).astype(jnp.bfloat16))
+        return unused
+
+    spread_x.sent()
+    lax.fori_loop(0, 8, project, 0)
+    save_normed = pltpu.make_async_copy(normed, normed_out, local_sem.at[8])
+    save_normed.start()
+
+    group_arrived(4)
+
+    def output_half(block, half):
+        if half is None:
+            return output_all.at[:, block]
+        lines = output_all.shape[2]
+        return output_all.at[:, block, halves(lines)(half)]
+
+    spread_o = Spread(place, lambda half: output_half(me, half), output_half, o_send, o_recv)
+
+    def after_prompt():
+        spread_g.relay_first()
+        spread_g.relay_second()
+        spread_o.start()
+
+    def after_half():
+        spread_g.relay_third()
+        spread_o.relay_first()
+        spread_o.relay_second()
+
+    attend_forward(
+        per_segment,
+        slot_of,
+        block_of,
+        length_ref,
+        qkv,
+        attn,
+        attn_t,
+        lse,
+        query,
+        key,
+        value_t,
+        kept,
+        {per_segment: after_prompt, per_segment + per_segment // 2: after_half},
+    )
+
+    def swap(source, target, send, recv):
+        return [
+            remote(source(flip), target, send.at[flip - 1], recv.at[flip - 1], {"ctx": place.peer(flip)})
+            for flip in range(1, 8)
+        ]
+
+    to_rows = swap(
+        lambda flip: attn.at[rows_of(place.peer(flip))], attn_rows.at[:, my_cols], a_send, a_recv
+    )
+    for copy in to_rows:
+        copy.start()
+    attn_rows[:, my_cols] = attn[rows_of(me), :]
+    spread_o.relay_third()
+    for index in (5, 6, 7):
+        group_arrived(index)
+    down[...] = jnp.concatenate(
+        [down_parts[index].astype(jnp.float32) for index in range(devices_fsdp)], axis=0
+    ).astype(jnp.bfloat16)
+    spread_g.arrived(0, 7, 8, 9)
+    spread_o.arrived(0, 7, 8, 9)
+    for copy in to_rows:
+        copy.wait_recv()
+
+    full_output = output_all[...].reshape(width, width)
+    gain_two = gains[8:9, :]
+    hidden[...] = patches[...].astype(jnp.float32) + dot_f32(attn_rows[...], full_output, 1, 0)
+    own_ffn[...] = rms_forward(hidden[...], gain_two)[0].astype(jnp.bfloat16)
+    spread_f = Spread(place, own_half(own_ffn), rows_half(normed_ffn), f_send, f_recv)
+    spread_f.start()
+    normed_ffn[rows_of(me), :] = own_ffn[...]
+
+    sums = PairSum(
+        place, stage, landed, norm_sums, norm_received, pair_send, pair_recv, out_send, out_recv
+    )
+
+    def feed(block):
+        at = rows_of(block)
+        low = normed_ffn[at, :]
+        grad_out = grads[at, :]
+        gate = dot_f32(low, gate_t[...], 1, 1)
+        up_proj = dot_f32(low, up_t[...], 1, 1)
+        grad_inner = dot_f32(grad_out, down[...], 1, 1)
+        sigmoid = jax.nn.sigmoid(gate)
+        activated = gate * sigmoid
+        inner = activated * up_proj
+        inner_low = inner.astype(jnp.bfloat16)
+        grad_gate = grad_inner * up_proj * sigmoid * (1.0 + gate * (1.0 - sigmoid))
+        grad_up = grad_inner * activated
+        gate_low = grad_gate.astype(jnp.bfloat16)
+        up_low = grad_up.astype(jnp.bfloat16)
+        inner_t[:, at] = inner.T.astype(jnp.bfloat16)
+        grad_gate_t[:, at] = grad_gate.T.astype(jnp.bfloat16)
+        grad_up_t[:, at] = grad_up.T.astype(jnp.bfloat16)
+        return (
+            dot_f32(inner_low, down[...], 1, 0),
+            dot_f32(gate_low, gate_t[...], 1, 0) + dot_f32(up_low, up_t[...], 1, 0),
+        )
+
+    def one_pair(pair, unused):
+        @pl.when(pair == 0)
+        def _():
+            spread_f.arrived(0)
+
+        @pl.when(pair == 1)
+        def _():
+            spread_f.relay_first()
+            spread_f.relay_second()
+            spread_f.arrived(7)
+
+        @pl.when(pair == 2)
+        def _():
+            spread_f.arrived(8)
+
+        @pl.when(pair == 3)
+        def _():
+            spread_f.relay_third()
+            spread_f.arrived(9)
+
+        layer, norm = feed(sums.theirs(pair))
+        stage[pair, 0] = layer.astype(jnp.bfloat16)
+        stage[pair, 1] = norm.astype(jnp.bfloat16)
+        sums.exchange(pair).start()
+        layer, norm = feed(sums.mine(pair))
+        own_sum[0] = layer
+        own_sum[1] = norm
+        sums.exchange(pair).wait_recv()
+        layer_sums[pair] = (own_sum[0] + landed[pair, 0].astype(jnp.float32)).astype(jnp.bfloat16)
+        norm_sums[pair] = (own_sum[1] + landed[pair, 1].astype(jnp.float32)).astype(jnp.bfloat16)
+
+        @pl.when(pair > 0)
+        def _():
+            sums.deliver(pair).start()
+
+        return unused
+
+    lax.fori_loop(0, 4, one_pair, 0)
+
+    def units_tile(tile, unused):
+        at = rows_of(tile, shard)
+        low = normed_ffn[:, at]
+        grad_units[tile, 0:units, :] = dot_f32(grad_gate_t[...], low, 1, 0).astype(jnp.bfloat16)
+        grad_units[tile, units : 2 * units, :] = dot_f32(grad_up_t[...], low, 1, 0).astype(
+            jnp.bfloat16
+        )
+        down_tiles[tile] = dot_f32(inner_t[...], grads[:, at], 1, 0)
+        return unused
+
+    lax.fori_loop(0, devices_fsdp, units_tile, 0)
+    for index in range(devices_fsdp):
+        grad_units[index, 2 * units : 3 * units, :] = jnp.concatenate(
+            [
+                down_tiles[tile, index * part : (index + 1) * part, :]
+                for tile in range(devices_fsdp)
+            ],
+            axis=0,
+        ).astype(jnp.bfloat16)
+
+    total = norm_sums[0].astype(jnp.float32)
+    for pair in range(1, 4):
+        sums.deliver(pair).wait_recv()
+        total = total + norm_received[pair].astype(jnp.float32)
+    values = hidden[...]
+    factor = lax.rsqrt(jnp.mean(values * values, axis=-1, keepdims=True) + epsilon)
+    scaled = total * gain_two
+    gain_part[...] = jnp.sum(total * values * factor, axis=0, keepdims=True)
+    whole = (
+        cotangent[...].astype(jnp.float32)
+        + factor * scaled
+        - values * (factor * factor * factor) * jnp.mean(scaled * values, axis=-1, keepdims=True)
+    )
+    grad_hidden[...] = whole
+    grad_branch[...] = whole.astype(jnp.bfloat16)
+    grad_rows[...] = dot_f32(grad_branch[...], output_all[...].reshape(width, width), 1, 1).astype(
+        jnp.bfloat16
+    )
+    to_heads = swap(
+        lambda flip: grad_rows.at[:, rows_of(place.peer(flip), cols)],
+        grad_attn.at[rows_of(me)],
+        b_send,
+        b_recv,
+    )
+    for copy in to_heads:
+        copy.start()
+    grad_attn[rows_of(me), :] = grad_rows[:, my_cols]
+
+    for index in range(devices_fsdp):
+        piece = attn_rows[:, index * shard : (index + 1) * shard].T
+        grad_output[index] = (
+            dot_f32(piece, grad_branch[...], 1, 0)
+            .astype(jnp.bfloat16)
+            .reshape(8, shard // 8, width)
+        )
+    qkv_out[...] = w_qkv[...]
+    gains_out[...] = gains[...]
+    for copy in to_heads:
+        copy.wait_recv()
+    grad_attn_out[...] = grad_attn[...].reshape(grad_attn_out.shape)
+
+    save_normed.wait()
+    for index in range(8):
+        for copy in group_copies(index):
+            copy.wait_send()
+    spread_g.sent()
+    spread_o.sent()
+    spread_f.sent()
+    for copy in to_rows + to_heads:
+        copy.wait_send()
+    sums.sent()
+
+
+def backward_kernel(
+    per_segment,
+    devices_fsdp,
+    slot_of,
+    block_of,
+    length_ref,
+    qkv,
+    grad_attn,
+    attn_t,
+    lse,
+    normed,
+    w_qkv,
+    gains,
+    patches,
+    grad_hidden,
+    hidden,
+    layer_sums,
+    grad_units,
+    grad_output,
+    gain_part,
+    layer,
+    grad_patches,
+    units_out,
+    columns_out,
+    gains_out,
+    grad_qkv,
+    query,
+    key,
+    value,
+    grad,
+    key_t,
+    grad_key,
+    grad_value,
+    units_landed,
+    units_stage,
+    units_all,
+    layer_received,
+    output_stage,
+    output_landed,
+    output_sums,
+    output_received,
+    output_total,
+    output_group,
+    stage,
+    landed,
+    own_sum,
+    norm_sums,
+    norm_received,
+    grad_qkv_t,
+    qkv_parts,
+    qkv_landed,
+    columns_stage,
+    columns_all,
+    gain_stage,
+    gain_landed,
+    gain_total,
+    gain_all,
+    local_sem,
+    units_send,
+    units_recv,
+    layer_send,
+    layer_recv,
+    wo_send,
+    wo_recv,
+    wo_out_send,
+    wo_out_recv,
+    group_send,
+    group_recv,
+    pair_send,
+    pair_recv,
+    out_send,
+    out_recv,
+    u_send,
+    u_recv,
+    c_send,
+    c_recv,
+    gain_send,
+    gain_recv,
+    gain_out_send,
+    gain_out_recv,
+):
+    place = Place(devices_fsdp)
+    me, group = place.me, place.group
+    local_rows, width = patches.shape
+    shard = width // devices_fsdp
+    cols = width // 8
+    units = grad_units.shape[1] // 3
+    place.meet()
+
+    def rows_of(block, count=local_rows):
+        return pl.ds(pl.multiple_of(block * count, count), count)
+
+    def over_groups(source, target, send, recv):
+        return [
+            remote(
+                source(place.other_group(step)),
+                target.at[group],
+                send.at[step - 1],
+                recv.at[step - 1],
+                {"fsdp": place.other_group(step)},
+            )
+            for step in range(1, devices_fsdp)
+        ]
+
+    units_copies = over_groups(lambda to: grad_units.at[to], units_landed, units_send, units_recv)
+    for copy in units_copies:
+        copy.start()
+    sums = PairSum(
+        place, stage, landed, norm_sums, norm_received, pair_send, pair_recv, out_send, out_recv
+    )
+    output_pairs = PairSum(
+        place,
+        output_stage,
+        output_landed,
+        output_sums,
+        output_received,
+        wo_send,
+        wo_recv,
+        wo_out_send,
+        wo_out_recv,
+    )
+    for pair in range(4):
+        output_stage[pair] = grad_output[:, output_pairs.theirs(pair)]
+        output_pairs.exchange(pair).start()
+    layer_copies = [
+        remote(
+            layer_sums.at[pair],
+            layer_received.at[pair],
+            layer_send.at[pair],
+            layer_recv.at[pair],
+            {"ctx": sums.mine(pair)},
+        )
+        for pair in range(1, 4)
+    ]
+    for copy in layer_copies:
+        copy.start()
+
+    def after_prompt():
+        for pair in range(4):
+            output_pairs.exchange(pair).wait_recv()
+            output_sums[pair] = (
+                grad_output[:, output_pairs.mine(pair)].astype(jnp.float32)
+                + output_landed[pair].astype(jnp.float32)
+            ).astype(jnp.bfloat16)
+            if pair:
+                output_pairs.deliver(pair).start()
+
+    attend_backward(
+        per_segment,
+        slot_of,
+        block_of,
+        length_ref,
+        qkv,
+        grad_attn,
+        attn_t,
+        lse,
+        grad_qkv,
+        query,
+        key,
+        value,
+        grad,
+        key_t,
+        grad_key,
+        grad_value,
+        {per_segment: after_prompt},
+    )
+
+    def one_pair(pair, unused):
+        stage[pair] = dot_f32(grad_qkv[rows_of(sums.theirs(pair)), :], w_qkv[...], 1, 1).astype(
+            jnp.bfloat16
+        )
+        sums.exchange(pair).start()
+        return unused
+
+    lax.fori_loop(0, 4, one_pair, 0)
+
+    def sum_pair(step, unused):
+        pair = 3 - step
+        own_sum[...] = dot_f32(grad_qkv[rows_of(sums.mine(pair)), :], w_qkv[...], 1, 1)
+        sums.exchange(pair).wait_recv()
+        norm_sums[pair] = (own_sum[...] + landed[pair].astype(jnp.float32)).astype(jnp.bfloat16)
+
+        @pl.when(pair > 0)
+        def _():
+            sums.deliver(pair).start()
+
+        return unused
+
+    lax.fori_loop(0, 4, sum_pair, 0)
+
+    def turn(tile, unused):
+        at = rows_of(tile, TILE)
+        grad_qkv_t[:, at] = grad_qkv[at, :].T
+        return unused
+
+    lax.fori_loop(0, grad_qkv.shape[0] // TILE, turn, 0)
+
+    def weight_tile(tile, unused):
+        qkv_parts[tile] = dot_f32(grad_qkv_t[...], normed[:, rows_of(tile, shard)], 1, 0).astype(
+            jnp.bfloat16
+        )
+        return unused
+
+    lax.fori_loop(0, devices_fsdp, weight_tile, 0)
+    qkv_copies = over_groups(
+        lambda to: qkv_parts.at[to], qkv_landed, group_send.at[0], group_recv.at[0]
+    )
+    for copy in qkv_copies:
+        copy.start()
+
+    total = output_sums[0].astype(jnp.float32)
+    for pair in range(1, 4):
+        output_pairs.deliver(pair).wait_recv()
+        total = total + output_received[pair].astype(jnp.float32)
+    output_total[...] = total.astype(jnp.bfloat16)
+    output_copies = over_groups(
+        lambda to: output_total.at[to], output_group, group_send.at[1], group_recv.at[1]
+    )
+    for copy in output_copies:
+        copy.start()
+
+    def group_sum(own, landed_ref, copies):
+        landed_ref[group] = own
+        for copy in copies:
+            copy.wait_recv()
+        total = landed_ref[0].astype(jnp.float32)
+        for index in range(1, devices_fsdp):
+            total = total + landed_ref[index].astype(jnp.float32)
+        return total
+
+    units_stage[...] = group_sum(grad_units[group], units_landed, units_copies).astype(
+        jnp.bfloat16
+    )
+
+    def half_of(ref, lines):
+        def region(block, half):
+            return ref.at[block] if half is None else ref.at[block, halves(lines)(half)]
+
+        return region
+
+    def own_of(ref, lines):
+        return lambda half: ref if half is None else ref.at[halves(lines)(half)]
+
+    spread_u = Spread(
+        place,
+        own_of(units_stage, 3 * units),
+        half_of(units_all, 3 * units),
+        u_send,
+        u_recv,
+    )
+    spread_u.start()
+    units_all[me] = units_stage[...]
+
+    total = layer_sums[0].astype(jnp.float32)
+    for pair, copy in enumerate(layer_copies):
+        copy.wait_recv()
+        total = total + layer_received[pair + 1].astype(jnp.float32)
+    layer[...] = (hidden[...] + total).astype(jnp.bfloat16)
+
+    total = norm_sums[0].astype(jnp.float32)
+    for pair in range(1, 4):
+        sums.deliver(pair).wait_recv()
+        total = total + norm_received[pair].astype(jnp.float32)
+    values = patches[...].astype(jnp.float32)
+    gain_one = gains[0:1, :]
+    factor = lax.rsqrt(jnp.mean(values * values, axis=-1, keepdims=True) + epsilon)
+    scaled = total * gain_one
+    gain_stage[...] = jnp.zeros_like(gain_stage)
+    attn_part = jnp.sum(total * values * factor, axis=0, keepdims=True)
+    ffn_part = gain_part[...]
+    for index in range(devices_fsdp):
+        at = slice(index * shard, (index + 1) * shard)
+        gain_stage[index, 0:1, :] = attn_part[:, at]
+        gain_stage[index, 1:2, :] = ffn_part[:, at]
+    gain_copies = over_groups(lambda to: gain_stage.at[to], gain_landed, gain_send, gain_recv)
+    for copy in gain_copies:
+        copy.start()
+    grad_patches[...] = (
+        grad_hidden[...]
+        + factor * scaled
+        - values * (factor * factor * factor) * jnp.mean(scaled * values, axis=-1, keepdims=True)
+    )
+    spread_u.relay_first()
+    spread_u.relay_second()
+    gain_total[...] = group_sum(gain_stage[group], gain_landed, gain_copies)
+    gain_out = [
+        remote(
+            gain_total,
+            gain_all.at[me],
+            gain_out_send.at[flip - 1],
+            gain_out_recv.at[flip - 1],
+            {"ctx": place.peer(flip)},
+        )
+        for flip in range(1, 8)
+    ]
+    for copy in gain_out:
+        copy.start()
+    gain_all[me] = gain_total[...]
+
+    turned = group_sum(qkv_parts[group], qkv_landed, qkv_copies).T.astype(jnp.bfloat16)
+    for index in range(3):
+        columns_stage[index * shard : (index + 1) * shard, :] = turned[
+            :, index * cols : (index + 1) * cols
+        ]
+    summed = group_sum(output_total[group], output_group, output_copies).astype(jnp.bfloat16)
+    lines = shard // 8
+    for index in range(8):
+        columns_stage[3 * shard + index * lines : 3 * shard + (index + 1) * lines, :] = summed[
+            :, index * cols : (index + 1) * cols
+        ]
+    spread_c = Spread(
+        place, own_of(columns_stage, 4 * shard), half_of(columns_all, 4 * shard), c_send, c_recv
+    )
+    spread_c.start()
+    columns_all[me] = columns_stage[...]
+    spread_u.relay_third()
+    for copy in gain_out:
+        copy.wait_recv()
+    gain_sum = gain_all[0]
+    for index in range(1, 8):
+        gain_sum = gain_sum + gain_all[index]
+    gains_out[...] = gain_sum
+    spread_c.relay_first()
+    spread_c.relay_second()
+    spread_u.arrived(0, 7, 8, 9)
+    save_units = pltpu.make_async_copy(units_all, units_out, local_sem.at[0])
+    save_units.start()
+    spread_c.relay_third()
+    spread_c.arrived(0, 7, 8, 9)
+    save_columns = pltpu.make_async_copy(columns_all, columns_out, local_sem.at[1])
+    save_columns.start()
+    for copy in units_copies + layer_copies + qkv_copies + output_copies + gain_copies + gain_out:
+        copy.wait_send()
+    sums.sent()
+    output_pairs.sent()
+    spread_u.sent()
+    spread_c.sent()
+    save_units.wait()
+    save_columns.wait()
+
+
+def place_kernel(
+    devices_fsdp,
+    units_all,
+    columns_all,
+    out_query,
+    out_key,
+    out_value,
+    out_output,
+    out_gate,
+    out_up,
+    out_down,
+    columns,
+    outputs,
+    natural,
+    gate,
+    up,
+    down,
+    sems,
+):
+    shard = out_query.shape[0]
+    cols = columns_all.shape[2]
+    lines = shard // 8
+    units = units_all.shape[1] // 3
+    part = units // devices_fsdp
+    span = part * 8
+    saves = []
+
+    def save(source, target):
+        copy = pltpu.make_async_copy(source, target, sems.at[len(saves)])
+        copy.start()
+        saves.append(copy)
+
+    for index in range(8):
+        piece = units_all[index, 2 * units : 3 * units, :].astype(jnp.float32)
+        for tile in range(devices_fsdp):
+            down[index * part : (index + 1) * part, tile * shard : (tile + 1) * shard] = piece[
+                tile * part : (tile + 1) * part, :
+            ]
+    save(down, out_down)
+    for which, (target, out) in enumerate(((gate, out_gate), (up, out_up))):
+        for index in range(8):
+            piece = units_all[index, which * units : (which + 1) * units, :].astype(jnp.float32)
+            for tile in range(devices_fsdp):
+                first = tile * span + index * part
+                natural[first : first + part, :] = piece[tile * part : (tile + 1) * part, :]
+        for first in range(0, span * devices_fsdp, 128):
+            target[:, first : first + 128] = natural[first : first + 128, :].T
+        save(target, out)
+    for index in range(8):
+        at = slice(index * cols, (index + 1) * cols)
+        for which in range(3):
+            columns[which, :, at] = columns_all[
+                index, which * shard : (which + 1) * shard, :
+            ].astype(jnp.float32)
+        for tile in range(8):
+            first = 3 * shard + tile * lines
+            outputs[index * lines : (index + 1) * lines, tile * cols : (tile + 1) * cols] = (
+                columns_all[index, first : first + lines, :].astype(jnp.float32)
+            )
+    save(columns.at[0], out_query)
+    save(columns.at[1], out_key)
+    save(columns.at[2], out_value)
+    save(outputs, out_output)
+    for copy in saves:
+        copy.wait()
+
+
+def heads_plan(
+    patches,
+    cotangent,
+    deal_table,
+    prompt_len,
+    w_query,
+    w_key,
+    w_value,
+    w_output,
+    w_gate,
+    w_up,
+    w_down,
+    gain_attn,
+    gain_ffn,
+):
+    local_rows = patches.shape[1]
+    width = patches.shape[2]
+    groups = lax.axis_size("fsdp")
+    rows = local_rows * 8
+    cols = width // 8
+    shard = width // groups
+    part = w_down.shape[0] // 8
+    units = part * groups
+    tiles = rows // TILE
+    blocks = deal_table.shape[0]
+    block_len = rows // blocks
+    per_segment = CONT_LEN // TILE
+    slots = jnp.arange(deal_table.shape[0], dtype=jnp.int32)
+    slot_of = jnp.sum(
+        jnp.where(deal_table[None, :] == slots[:, None], slots[None, :], 0), axis=1
+    ).astype(jnp.int32)
+    smem = pl.BlockSpec(memory_space=pltpu.SMEM)
+    vmem = pl.BlockSpec(memory_space=pltpu.VMEM)
+    anywhere = pl.BlockSpec(memory_space=pl.ANY)
+    low, full = jnp.bfloat16, jnp.float32
+
+    def shaped(kind, *dims):
+        return jax.ShapeDtypeStruct(dims, kind)
+
+    def room(kind, *dims):
+        return pltpu.VMEM(dims, kind)
+
+    (
+        qkv,
+        normed,
+        attn_t,
+        lse,
+        w_qkv,
+        gains,
+        grad_units,
+        grad_output,
+        layer_sums,
+        hidden,
+        grad_hidden,
+        gain_part,
+        grad_attn,
+    ) = pl.pallas_call(
+        functools.partial(forward_kernel, per_segment, groups),
+        out_shape=(
+            shaped(low, blocks, block_len, 3 * cols),
+            shaped(low, rows, width),
+            shaped(full, tiles, cols, TILE),
+            shaped(full, tiles, 1, 2 * TILE),
+            shaped(low, width, 3 * cols),
+            shaped(full, 16, width),
+            shaped(low, groups, 3 * units, shard),
+            shaped(low, groups, 8, shard // 8, width),
+            shaped(low, 4, local_rows, width),
+            shaped(full, local_rows, width),
+            shaped(full, local_rows, width),
+            shaped(full, 1, width),
+            shaped(low, blocks, block_len, cols),
+        ),
+        in_specs=[smem] * 3
+        + [vmem] * 2
+        + [anywhere] * 4
+        + [vmem] * 2
+        + [anywhere]
+        + [vmem] * 2,
+        out_specs=(vmem, anywhere) + (vmem,) * 11,
+        scratch_shapes=[
+            room(low, rows, width),
+            room(low, rows, width),
+            room(low, rows, width),
+            room(low, width, 3 * cols),
+            room(low, groups, 8, shard // 8, width),
+            room(low, units, width),
+            room(low, units, width),
+            room(low, units, width),
+            room(low, groups, part, width),
+            room(low, units, shard),
+            room(low, units, shard),
+            room(full, 16, shard),
+            room(full, 16, width),
+            room(low, blocks, block_len, cols),
+            room(low, blocks, block_len, cols),
+            room(low, tiles, cols, TILE),
+            room(low, blocks, block_len, cols),
+            room(low, rows, cols),
+            room(low, local_rows, width),
+            room(low, local_rows, width),
+            room(low, units, rows),
+            room(low, units, rows),
+            room(low, units, rows),
+            room(low, 4, 2, local_rows, width),
+            room(low, 4, 2, local_rows, width),
+            room(full, 2, local_rows, width),
+            room(low, 4, local_rows, width),
+            room(low, 4, local_rows, width),
+            room(full, groups, units, shard),
+            room(low, local_rows, width),
+            room(low, local_rows, width),
+            room(low, rows, cols),
+            dma(9),
+            pltpu.SemaphoreType.DMA((8, groups - 1)),
+            pltpu.SemaphoreType.DMA((8, groups - 1)),
+        ]
+        + [dma(10)] * 8
+        + [dma(7)] * 4
+        + [dma(4)] * 4,
+        compiler_params=pltpu.CompilerParams(
+            collective_id=0, has_side_effects=True, vmem_limit_bytes=66_000_000
+        ),
+        name="forward",
+    )(
+        slot_of,
+        deal_table,
+        prompt_len,
+        patches[0],
+        cotangent[0],
+        w_query,
+        w_key,
+        w_value,
+        w_output.reshape(8, shard // 8, width),
+        w_gate,
+        w_up,
+        w_down.reshape(8, part, width),
+        gain_attn[None],
+        gain_ffn[None],
+    )
+
+    layer, grad_rows, units_all, columns_all, gains_sum = pl.pallas_call(
+        functools.partial(backward_kernel, per_segment, groups),
+        out_shape=(
+            shaped(low, local_rows, width),
+            shaped(full, local_rows, width),
+            shaped(low, 8, 3 * units, shard),
+            shaped(low, 8, 4 * shard, cols),
+            shaped(full, 8, shard),
+        ),
+        in_specs=[smem] * 3 + [vmem] * 14,
+        out_specs=(vmem, vmem, anywhere, anywhere, vmem),
+        scratch_shapes=[
+            room(low, rows, 3 * cols),
+            room(low, blocks, block_len, cols),
+            room(low, blocks, block_len, cols),
+            room(low, blocks, block_len, cols),
+            room(low, blocks, block_len, cols),
+            room(low, tiles, cols, TILE),
+            room(full, rows, cols),
+            room(full, rows, cols),
+            room(low, groups, 3 * units, shard),
+            room(low, 3 * units, shard),
+            room(low, 8, 3 * units, shard),
+            room(low, 4, local_rows, width),
+            room(low, 4, groups, shard // 8, width),
+            room(low, 4, groups, shard // 8, width),
+            room(low, 4, groups, shard // 8, width),
+            room(low, 4, groups, shard // 8, width),
+            room(low, groups, shard // 8, width),
+            room(low, groups, shard // 8, width),
+            room(low, 4, local_rows, width),
+            room(low, 4, local_rows, width),
+            room(full, local_rows, width),
+            room(low, 4, local_rows, width),
+            room(low, 4, local_rows, width),
+            room(low, 3 * cols, rows),
+            room(low, groups, 3 * cols, shard),
+            room(low, groups, 3 * cols, shard),
+            room(low, 4 * shard, cols),
+            room(low, 8, 4 * shard, cols),
+            room(full, groups, 8, shard),
+            room(full, groups, 8, shard),
+            room(full, 8, shard),
+            room(full, 8, 8, shard),
+            dma(2),
+            dma(groups - 1),
+            dma(groups - 1),
+            dma(4),
+            dma(4),
+            dma(4),
+            dma(4),
+            dma(4),
+            dma(4),
+            pltpu.SemaphoreType.DMA((2, groups - 1)),
+            pltpu.SemaphoreType.DMA((2, groups - 1)),
+            dma(4),
+            dma(4),
+            dma(4),
+            dma(4),
+            dma(10),
+            dma(10),
+            dma(10),
+            dma(10),
+            dma(groups - 1),
+            dma(groups - 1),
+            dma(7),
+            dma(7),
+        ],
+        compiler_params=pltpu.CompilerParams(
+            collective_id=1, has_side_effects=True, vmem_limit_bytes=66_000_000
+        ),
+        name="backward",
+    )(
+        slot_of,
+        deal_table,
+        prompt_len,
+        qkv,
+        grad_attn,
+        attn_t,
+        lse,
+        normed,
+        w_qkv,
+        gains,
+        patches[0],
+        grad_hidden,
+        hidden,
+        layer_sums,
+        grad_units,
+        grad_output,
+        gain_part,
+    )
+
+    weights = pl.pallas_call(
+        functools.partial(place_kernel, groups),
+        out_shape=tuple(shaped(full, shard, width) for _ in range(4))
+        + tuple(shaped(full, shard, 8 * units) for _ in range(2))
+        + (shaped(full, 8 * part, width),),
+        in_specs=[vmem, vmem],
+        out_specs=(anywhere,) * 7,
+        scratch_shapes=[
+            room(full, 3, shard, width),
+            room(full, shard, width),
+            room(full, 8 * units, shard),
+            room(full, shard, 8 * units),
+            room(full, shard, 8 * units),
+            room(full, 8 * part, width),
+            dma(7),
+        ],
+        name="place",
+    )(units_all, columns_all)
+    return (layer[None], grad_rows[None]) + tuple(weights) + (gains_sum[0], gains_sum[1])
+
+
 def solution(mesh):
+    if mesh.shape["ctx"] == 8:
+        per_device = heads_plan
+    else:
+        per_device = rows_plan
     placed = (
         P("fsdp", "ctx", None),
         P("fsdp", "ctx", None),

time: 1430 us -> 262 us (0.18)
  waiting for transfers between devices: 1120 us -> 0 us
  Pallas kernels: 0 us -> 251 us
  matrix products: 127 us -> 0 us
  local copies, waits for them, and re-layouts: 77.5 us -> 5.55 us
  blocking collectives: 44.8 us -> 0 us
  other arithmetic: 37.4 us -> 1.28 us
    reduce_scatter x9 -> x0, waiting for transfers between devices: 584 us -> none  [the longest x1 105 us: per_device(): lax.psum_scatter(grad_w_down.astype(jnp.bfloat16), 'fsdp', scatter_dimens...]
    all_gather x9 -> x0, waiting for transfers between devices: 463 us -> none  [the longest x1 103 us: per_device(): lax.all_gather(w_gate, 'fsdp', axis=0, tiled=True)]
    pallas_call x0 -> x3, Pallas kernels: none -> 251 us  [the longest x1 142 us: heads_plan(): pl.pallas_call(functools.partial(forward_kernel, per_segment, groups), ou...]
    dot_general x35 -> x0, matrix products: 127 us -> none  [the longest x1 20.8 us: per_device(): jnp.dot(grad_down_in, full_down.T, preferred_element_type=jnp.float32)]
    psum x1 -> x0, waiting for transfers between devices: 72.4 us -> none  [per_device(): lax.psum(shards[0].astype(jnp.bfloat16), 'ctx').astype(jnp.float32)]
    reshape x2 -> x0, local copies, waits for them, and re-layouts: 23.7 us -> none  [split_blocks(): return array.reshape(block_count, key_rows, HEADS, HEAD)]
    all_gather x2 -> x0, blocking collectives: 22 us -> none  [the longest x1 12.6 us: per_device(): lax.all_gather(gain_attn, 'fsdp', axis=0, tiled=True)]
    while x2 -> x0, local copies, waits for them, and re-layouts: 19.5 us -> none  [per_device(): lax.scan(forward_block, start_state, (split_blocks(key_all), split_blocks...]
  transfers between devices with their start and end apart: 19 -> 0, of which waited for: 18 -> 0; matrix products, arithmetic and copies ran while one was open for 10% -> 0% of each run, Pallas kernels for 0% -> 0%
where the time goes in v2:
time: 262 us; the launch traced here: 259 us
  Pallas kernels  251 us (96%)
  local copies, waits for them, and re-layouts  5.55 us (2%)
    pallas_call x1, Pallas kernels, heads_plan(): pl.pallas_call(functools.partial(forward_kernel, per_segment, groups), ou...  142 us
    pallas_call x1, Pallas kernels, heads_plan(): pl.pallas_call(functools.partial(backward_kernel, per_segment, groups), o...  101 us
    pallas_call x1, Pallas kernels, heads_plan(): pl.pallas_call(functools.partial(place_kernel, groups), out_shape=tuple((...  8.71 us

profile of v2, /device:TPU:0, one launch (start us, length us, event | category | flops | bytes accessed | tf_op | source)
XLA Modules:
  0.0 259.3 jit_solution(14269932994604719512)
XLA Ops:
  1.3 1.3 select_reduce_fusion.slot_of
  2.6 1.2 broadcast_in_dim.29.gain_attn
  3.8 1.2 broadcast_in_dim.30.gain_ffn
  5.0 141.8 %forward.1 = (bf16[16,128,384]{2,1,0:T(8,128)(2,1)}, bf16[2048,1024]{1,0:T(8,128)(2,1)}, f32[8,128,256]{2,1,0:T(8,128)}, f32[8,1,512]{2,1,0:T(1,128)}, bf16[1024...) custom-call(s32[16]{0:T(128)} %select_reduce_fusion.slot_of, ...), custom_call_target="tpu_custom_call" | custom-call | tf_op jit(solution)/shard_map/forward/pallas_call | solution.py:1554
  146.9 100.6 %backward.1 = (bf16[256,1024]{1,0:T(8,128)(2,1)}, f32[256,1024]{1,0:T(8,128)}, bf16[8,1056,256]{2,1,0:T(8,128)(2,1)}, bf16[8,1024,128]{2,1,0:T(8,128)(2,1)}, f32[8,256]{1,0:T(8,128)}) custom-call(s32[16]{0:T(128)} %select_reduce_fusion.slot_of, s32[16]{0:T(128)} %block_of.3, s32[1]{0:T(128)S(6)} %copy.26.length_ref, ...), custom_call_target="tpu_custom_call" | custom-call | tf_op jit(solution)/shard_map/backward/pallas_call | solution.py:1639
  247.4 1.3 fusion
  248.8 0.0 copy-start.1
  248.8 0.0 copy-start
  248.8 8.7 %place.1 = (f32[256,1024]{1,0:T(8,128)}, f32[256,1024]{1,0:T(8,128)}, f32[256,1024]{1,0:T(8,128)}, f32[256,1024]{1,0:T(8,128)}, f32[256,2816]{1,0:T(8,128)}, /*index=5*/f32[256,2816]{1,0:T(8,128)}, f32[704,1024]{1,0:T(8,128)}) custom-call(bf16[8,1056,256]{2,1,0:T(8,128)(2,1)} %get-tuple-element.51.units_all, bf16[8,1024,128]{2,1,0:T(8,128)(2,1)} %get-tuple-element.52.columns_all), custom_call_target="tpu_custom_call" | custom-call | tf_op jit(solution)/shard_map/place/pallas_call | solution.py:1731
  257.5 0.0 copy-done.1
  257.5 0.8 copy.27
  258.3 0.0 copy-done
  258.3 1.0 copy.28
Async XLA Ops:
  248.8 8.7 %copy-start.1 = (bf16[256,1024]{1,0:T(8,128)(2,1)S(1)}, bf16[256,1024]{1,0:T(8,128)(2,1)}, u32[]{:S(2)}) copy-start(bf16[256,1024]{1,0:T(8,128)(2,1)} %get-tuple-element.49) | copy-start | bytes 1572868
  248.8 9.5 %copy-start = (f32[256,1024]{1,0:T(8,128)S(1)}, f32[256,1024]{1,0:T(8,128)}, u32[]{:S(2)}) copy-start(f32[256,1024]{1,0:T(8,128)} %get-tuple-element.50) | copy-start | bytes 3145732

commit v3 on v2

--- a/solution.py
+++ b/solution.py
@@ -407,10 +407,8 @@
 def attend_forward(
     per_segment,
     slot_of,
-    block_of,
     length_ref,
     qkv,
-    attn,
     attn_t,
     lse,
     query,
@@ -464,7 +462,6 @@
         return unused
 
     tiles_between(rows // TILE, one_tile, between)
-    to_stored(block_of, kept, attn, 0)
 
 
 def attend_backward(
@@ -568,6 +565,18 @@
     def other_group(self, step):
         return lax.rem(self.group + step, self.groups)
 
+    def at_end(self):
+        return lax.rem(self.group, 3) == 0
+
+    def between(self):
+        return lax.rem(self.group, 3) != 0
+
+    def near(self, step):
+        return self.group != {1: 3, 2: 4, 3: 0}[step]
+
+    def heard(self, step):
+        return self.group != {1: 0, 2: 4, 3: 3}[step]
+
     def meet(self):
         barrier = pltpu.get_barrier_semaphore()
         for flip in range(1, 8):
@@ -677,6 +686,69 @@
             self.exchange(pair).wait_send()
             if pair:
                 self.deliver(pair).wait_send()
+
+
+class CrossSum(PairSum):
+    def __init__(self, place, stage, landed, sums, received, passed, send, recv, out_send, out_recv):
+        super().__init__(place, stage, landed, sums, received, send, recv, out_send, out_recv)
+        self.passed = passed
+
+    def half(self, which):
+        count = self.sums.shape[1] // 2
+        return slice(which * count, (which + 1) * count)
+
+    def far(self, which):
+        slot = 3 * which
+        return remote(
+            self.sums.at[3, self.half(which)],
+            self.passed.at[which],
+            self.out_send.at[slot],
+            self.out_recv.at[slot],
+            {"ctx": self.place.peer(2 + 2 * which)},
+        )
+
+    def deliver(self, pair):
+        return remote(
+            self.sums.at[pair],
+            self.received.at[pair - 1],
+            self.out_send.at[pair],
+            self.out_recv.at[pair],
+            {"ctx": self.place.peer(2 * pair)},
+        )
+
+    def finish(self, pair, total):
+        self.sums[pair] = total.astype(jnp.bfloat16)
+
+        @pl.when(pair == 3)
+        def _():
+            self.far(0).start()
+            self.far(1).start()
+
+        for axis in (1, 2):
+            which = 2 - axis
+
+            @pl.when(pair == axis)
+            def _(axis=axis, which=which):
+                at = self.half(which)
+                self.far(which).wait_recv()
+                self.sums[axis, at, :] = (
+                    total[at] + self.passed[which].astype(jnp.float32)
+                ).astype(jnp.bfloat16)
+                self.deliver(axis).start()
+
+    def collect(self):
+        total = self.sums[0].astype(jnp.float32)
+        for pair in (1, 2):
+            self.deliver(pair).wait_recv()
+            total = total + self.received[pair - 1].astype(jnp.float32)
+        return total
+
+    def sent(self):
+        for pair in range(4):
+            self.exchange(pair).wait_send()
+        for which in (0, 1):
+            self.far(which).wait_send()
+            self.deliver(which + 1).wait_send()
 
 
 def halves(count):
@@ -713,7 +785,7 @@
     grad_hidden,
     gain_part,
     grad_attn_out,
-    normed,
+    rows_all,
     grads,
     normed_ffn,
     w_qkv,
@@ -730,9 +802,8 @@
     key,
     value_t,
     kept,
-    attn,
+    attn_all,
     attn_rows,
-    own_ffn,
     inner_t,
     grad_gate_t,
     grad_up_t,
@@ -741,6 +812,7 @@
     own_sum,
     norm_sums,
     norm_received,
+    norm_passed,
     down_tiles,
     grad_branch,
     grad_rows,
@@ -748,16 +820,19 @@
     local_sem,
     group_send,
     group_recv,
+    pass_send,
     x_send,
     x_recv,
     g_send,
     g_recv,
     o_send,
     o_recv,
-    f_send,
-    f_recv,
-    a_send,
-    a_recv,
+    first_send,
+    first_recv,
+    second_send,
+    second_recv,
+    third_send,
+    third_recv,
     b_send,
     b_recv,
     pair_send,
@@ -788,48 +863,72 @@
     def own_half(ref):
         return lambda half: ref.at[halves(local_rows)(half)]
 
-    spread_x = Spread(place, own_half(patches), rows_half(normed), x_send, x_recv)
+    spread_x = Spread(place, own_half(patches), rows_half(rows_all), x_send, x_recv)
     spread_x.start()
 
     my_cols = rows_of(me, cols)
-    my_shard = rows_of(group, shard)
+    def shard_of(index):
+        return rows_of(index, shard)
+
     group_items = [
-        (w_query.at[:, my_cols], w_qkv.at[my_shard, 0:cols]),
-        (w_key.at[:, my_cols], w_qkv.at[my_shard, cols : 2 * cols]),
-        (w_value.at[:, my_cols], w_qkv.at[my_shard, 2 * cols : 3 * cols]),
-        (gain_stage, gains.at[:, my_shard]),
-        (w_output.at[me], output_all.at[group, me]),
-        (gate_stage, gate_t.at[:, my_shard]),
-        (up_stage, up_t.at[:, my_shard]),
-        (w_down.at[me], down_parts.at[group]),
+        (w_query.at[:, my_cols], lambda to: w_qkv.at[shard_of(to), 0:cols]),
+        (w_key.at[:, my_cols], lambda to: w_qkv.at[shard_of(to), cols : 2 * cols]),
+        (w_value.at[:, my_cols], lambda to: w_qkv.at[shard_of(to), 2 * cols : 3 * cols]),
+        (gain_stage, lambda to: gains.at[:, shard_of(to)]),
+        (w_output.at[me], lambda to: output_all.at[to, me]),
+        (gate_stage, lambda to: gate_t.at[:, shard_of(to)]),
+        (up_stage, lambda to: up_t.at[:, shard_of(to)]),
+        (w_down.at[me], lambda to: down_parts.at[to]),
     ]
 
-    def group_copies(index):
+    def group_copy(index, step):
         source, target = group_items[index]
-        return [
-            remote(
-                source,
-                target,
-                group_send.at[index, step - 1],
-                group_recv.at[index, step - 1],
-                {"fsdp": place.other_group(step)},
-            )
-            for step in range(1, devices_fsdp)
-        ]
+        return remote(
+            source,
+            target(group),
+            group_send.at[index, step - 1],
+            group_recv.at[index, step - 1],
+            {"fsdp": place.other_group(step)},
+        )
+
+    def passed_copy(index):
+        whose = place.other_group(2)
+        held = group_items[index][1](whose)
+        return remote(
+            held,
+            held,
+            pass_send.at[index],
+            group_recv.at[index, 2 * (group // 2)],
+            {"fsdp": devices_fsdp - 1 - whose},
+        )
 
     def local_copy(index):
         source, target = group_items[index]
-        return pltpu.make_async_copy(source, target, local_sem.at[index])
+        return pltpu.make_async_copy(source, target(group), local_sem.at[index])
 
     def send_group(index):
-        for copy in group_copies(index):
-            copy.start()
+        group_copy(index, 2).start()
+        for step in (1, 3):
+            pl.when(place.near(step))(group_copy(index, step).start)
         local_copy(index).start()
 
+    def pass_group(index):
+        @pl.when(place.between())
+        def _():
+            group_copy(index, 2).wait_recv()
+            passed_copy(index).start()
+
     def group_arrived(index):
-        for copy in group_copies(index):
-            copy.wait_recv()
+        pl.when(place.at_end())(group_copy(index, 2).wait_recv)
+        for step in (1, 3):
+            group_copy(index, step).wait_recv()
         local_copy(index).wait()
+
+    def group_sent(index):
+        group_copy(index, 2).wait_send()
+        for step in (1, 3):
+            pl.when(place.near(step))(group_copy(index, step).wait_send)
+        pl.when(place.between())(passed_copy(index).wait_send)
 
     for index in (0, 1, 2):
         send_group(index)
@@ -856,8 +955,10 @@
     send_group(6)
     send_group(7)
 
-    normed[rows_of(me), :] = patches[...]
+    rows_all[rows_of(me), :] = patches[...]
     grads[rows_of(me), :] = cotangent[...]
+    for index in (0, 1, 2, 3):
+        pass_group(index)
     spread_x.relay_first()
     spread_x.relay_second()
     spread_g = Spread(place, own_half(cotangent), rows_half(grads), g_send, g_recv)
@@ -870,18 +971,16 @@
 
     def project(block, unused):
         at = rows_of(block)
-        values = normed[at, :].astype(jnp.float32)
+        values = rows_all[at, :].astype(jnp.float32)
         low = rms_forward(values, gain_one)[0].astype(jnp.bfloat16)
-        normed[at, :] = low
+        normed_ffn[at, :] = low
         store_tile(qkv, block, dot_f32(low, w_qkv[...], 1, 0).astype(jnp.bfloat16))
         return unused
 
     spread_x.sent()
     lax.fori_loop(0, 8, project, 0)
-    save_normed = pltpu.make_async_copy(normed, normed_out, local_sem.at[8])
+    save_normed = pltpu.make_async_copy(normed_ffn, normed_out, local_sem.at[8])
     save_normed.start()
-
-    group_arrived(4)
 
     def output_half(block, half):
         if half is None:
@@ -889,33 +988,92 @@
         lines = output_all.shape[2]
         return output_all.at[:, block, halves(lines)(half)]
 
+    pass_group(4)
+    group_arrived(4)
+    pass_group(5)
     spread_o = Spread(place, lambda half: output_half(me, half), output_half, o_send, o_recv)
+    spread_o.start()
+
+    def attn_spread(first, count, send, recv):
+        def part(half):
+            return slice(
+                first + (count // 2 if half == 1 else 0),
+                first + (count // 2 if half == 0 else count),
+            )
+
+        return Spread(
+            place,
+            lambda half: kept.at[part(half)],
+            lambda block, half: attn_all.at[part(half), :, rows_of(block, cols)],
+            send,
+            recv,
+        )
+
+    half_blocks = kept.shape[0] // 2
+    attn_first = attn_spread(0, half_blocks, first_send, first_recv)
+    attn_second = attn_spread(half_blocks, half_blocks // 2, second_send, second_recv)
+    attn_third = attn_spread(half_blocks * 3 // 2, half_blocks // 2, third_send, third_recv)
+
+    def after_two():
+        spread_g.relay_first()
 
     def after_prompt():
-        spread_g.relay_first()
+        attn_first.start()
+        pass_group(6)
+
+    def after_more():
         spread_g.relay_second()
-        spread_o.start()
+        spread_o.relay_first()
 
     def after_half():
+        attn_second.start()
+        spread_o.relay_second()
         spread_g.relay_third()
-        spread_o.relay_first()
-        spread_o.relay_second()
+
+    def after_most():
+        pass_group(7)
+        attn_first.relay_first()
+        attn_first.relay_second()
+        spread_o.relay_third()
 
     attend_forward(
         per_segment,
         slot_of,
-        block_of,
         length_ref,
         qkv,
-        attn,
         attn_t,
         lse,
         query,
         key,
         value_t,
         kept,
-        {per_segment: after_prompt, per_segment + per_segment // 2: after_half},
-    )
+        {
+            per_segment // 2: after_two,
+            per_segment: after_prompt,
+            per_segment + 1: after_more,
+            per_segment + per_segment // 2: after_half,
+            2 * per_segment - 1: after_most,
+        },
+    )
+    attn_third.start()
+    attn_all[:, :, my_cols] = kept[...]
+    attn_first.relay_third()
+    attn_second.relay_first()
+    attn_second.relay_second()
+    for index in (5, 6, 7):
+        group_arrived(index)
+    down[...] = jnp.concatenate(
+        [down_parts[index].astype(jnp.float32) for index in range(devices_fsdp)], axis=0
+    ).astype(jnp.bfloat16)
+    attn_third.relay_first()
+    attn_second.relay_third()
+    attn_third.relay_second()
+    save_normed.wait()
+    spread_g.arrived(0, 7, 8, 9)
+    spread_o.arrived(0, 7, 8, 9)
+    attn_third.relay_third()
+    for spread in (attn_first, attn_second, attn_third):
+        spread.arrived(0, 7, 8, 9)
 
     def swap(source, target, send, recv):
         return [
@@ -923,38 +1081,35 @@
             for flip in range(1, 8)
         ]
 
-    to_rows = swap(
-        lambda flip: attn.at[rows_of(place.peer(flip))], attn_rows.at[:, my_cols], a_send, a_recv
-    )
-    for copy in to_rows:
-        copy.start()
-    attn_rows[:, my_cols] = attn[rows_of(me), :]
-    spread_o.relay_third()
-    for index in (5, 6, 7):
-        group_arrived(index)
-    down[...] = jnp.concatenate(
-        [down_parts[index].astype(jnp.float32) for index in range(devices_fsdp)], axis=0
-    ).astype(jnp.bfloat16)
-    spread_g.arrived(0, 7, 8, 9)
-    spread_o.arrived(0, 7, 8, 9)
-    for copy in to_rows:
-        copy.wait_recv()
-
-    full_output = output_all[...].reshape(width, width)
+    def attn_of(block):
+        held = attn_all.shape[0] // 8
+        return jnp.concatenate(
+            [attn_all[block_of[block * held + index]] for index in range(held)], axis=0
+        )
+
     gain_two = gains[8:9, :]
-    hidden[...] = patches[...].astype(jnp.float32) + dot_f32(attn_rows[...], full_output, 1, 0)
-    own_ffn[...] = rms_forward(hidden[...], gain_two)[0].astype(jnp.bfloat16)
-    spread_f = Spread(place, own_half(own_ffn), rows_half(normed_ffn), f_send, f_recv)
-    spread_f.start()
-    normed_ffn[rows_of(me), :] = own_ffn[...]
-
-    sums = PairSum(
-        place, stage, landed, norm_sums, norm_received, pair_send, pair_recv, out_send, out_recv
-    )
+    sums = CrossSum(
+        place,
+        stage,
+        landed,
+        norm_sums,
+        norm_received,
+        norm_passed,
+        pair_send,
+        pair_recv,
+        out_send,
+        out_recv,
+    )
+
+    def hidden_of(block, attn):
+        return rows_all[rows_of(block), :].astype(jnp.float32) + dot_f32(
+            attn, output_all[...].reshape(width, width), 1, 0
+        )
 
     def feed(block):
         at = rows_of(block)
-        low = normed_ffn[at, :]
+        low = rms_forward(hidden_of(block, attn_of(block)), gain_two)[0].astype(jnp.bfloat16)
+        normed_ffn[at, :] = low
         grad_out = grads[at, :]
         gate = dot_f32(low, gate_t[...], 1, 1)
         up_proj = dot_f32(low, up_t[...], 1, 1)
@@ -975,26 +1130,8 @@
             dot_f32(gate_low, gate_t[...], 1, 0) + dot_f32(up_low, up_t[...], 1, 0),
         )
 
-    def one_pair(pair, unused):
-        @pl.when(pair == 0)
-        def _():
-            spread_f.arrived(0)
-
-        @pl.when(pair == 1)
-        def _():
-            spread_f.relay_first()
-            spread_f.relay_second()
-            spread_f.arrived(7)
-
-        @pl.when(pair == 2)
-        def _():
-            spread_f.arrived(8)
-
-        @pl.when(pair == 3)
-        def _():
-            spread_f.relay_third()
-            spread_f.arrived(9)
-
+    def one_pair(step, unused):
+        pair = 3 - step
         layer, norm = feed(sums.theirs(pair))
         stage[pair, 0] = layer.astype(jnp.bfloat16)
         stage[pair, 1] = norm.astype(jnp.bfloat16)
@@ -1004,15 +1141,12 @@
         own_sum[1] = norm
         sums.exchange(pair).wait_recv()
         layer_sums[pair] = (own_sum[0] + landed[pair, 0].astype(jnp.float32)).astype(jnp.bfloat16)
-        norm_sums[pair] = (own_sum[1] + landed[pair, 1].astype(jnp.float32)).astype(jnp.bfloat16)
-
-        @pl.when(pair > 0)
-        def _():
-            sums.deliver(pair).start()
-
+        sums.finish(pair, own_sum[1] + landed[pair, 1].astype(jnp.float32))
         return unused
 
     lax.fori_loop(0, 4, one_pair, 0)
+    attn_rows[...] = attn_of(me)
+    hidden[...] = hidden_of(me, attn_rows[...])
 
     def units_tile(tile, unused):
         at = rows_of(tile, shard)
@@ -1034,10 +1168,7 @@
             axis=0,
         ).astype(jnp.bfloat16)
 
-    total = norm_sums[0].astype(jnp.float32)
-    for pair in range(1, 4):
-        sums.deliver(pair).wait_recv()
-        total = total + norm_received[pair].astype(jnp.float32)
+    total = sums.collect()
     values = hidden[...]
     factor = lax.rsqrt(jnp.mean(values * values, axis=-1, keepdims=True) + epsilon)
     scaled = total * gain_two
@@ -1075,14 +1206,13 @@
         copy.wait_recv()
     grad_attn_out[...] = grad_attn[...].reshape(grad_attn_out.shape)
 
-    save_normed.wait()
     for index in range(8):
-        for copy in group_copies(index):
-            copy.wait_send()
+        group_sent(index)
     spread_g.sent()
     spread_o.sent()
-    spread_f.sent()
-    for copy in to_rows + to_heads:
+    for spread in (attn_first, attn_second, attn_third):
+        spread.sent()
+    for copy in to_heads:
         copy.wait_send()
     sums.sent()
 
@@ -1121,8 +1251,9 @@
     grad_key,
     grad_value,
     units_landed,
+    units_far,
+    units_near,
     units_stage,
-    units_all,
     layer_received,
     output_stage,
     output_landed,
@@ -1135,11 +1266,11 @@
     own_sum,
     norm_sums,
     norm_received,
+    norm_passed,
     grad_qkv_t,
     qkv_parts,
     qkv_landed,
     columns_stage,
-    columns_all,
     gain_stage,
     gain_landed,
     gain_total,
@@ -1147,6 +1278,7 @@
     local_sem,
     units_send,
     units_recv,
+    far_sem,
     layer_send,
     layer_recv,
     wo_send,
@@ -1191,11 +1323,56 @@
             for step in range(1, devices_fsdp)
         ]
 
-    units_copies = over_groups(lambda to: grad_units.at[to], units_landed, units_send, units_recv)
-    for copy in units_copies:
-        copy.start()
-    sums = PairSum(
-        place, stage, landed, norm_sums, norm_received, pair_send, pair_recv, out_send, out_recv
+    def units_copy(step, source):
+        return remote(
+            source,
+            units_landed.at[group],
+            units_send.at[step - 1],
+            units_recv.at[step - 1],
+            {"fsdp": place.other_group(step)},
+        )
+
+    def units_direct(step):
+        return units_copy(step, grad_units.at[place.other_group(step)])
+
+    units_far_copy = remote(
+        grad_units.at[devices_fsdp - 1 - group],
+        units_far,
+        far_sem.at[0],
+        far_sem.at[1],
+        {"fsdp": 1 + group // 3},
+    )
+    units_sum_copy = units_copy(2, units_near)
+
+    @pl.when(place.at_end())
+    def _():
+        units_far_copy.start()
+        units_direct(2).start()
+
+    for step in (1, 3):
+        pl.when(place.near(step))(units_direct(step).start)
+
+    def units_between():
+        @pl.when(place.between())
+        def _():
+            units_far_copy.wait_recv()
+            units_near[...] = (
+                grad_units[place.other_group(2)].astype(jnp.float32)
+                + units_far[...].astype(jnp.float32)
+            ).astype(jnp.bfloat16)
+            units_sum_copy.start()
+
+    sums = CrossSum(
+        place,
+        stage,
+        landed,
+        norm_sums,
+        norm_received,
+        norm_passed,
+        pair_send,
+        pair_recv,
+        out_send,
+        out_recv,
     )
     output_pairs = PairSum(
         place,
@@ -1251,51 +1428,8 @@
         key_t,
         grad_key,
         grad_value,
-        {per_segment: after_prompt},
-    )
-
-    def one_pair(pair, unused):
-        stage[pair] = dot_f32(grad_qkv[rows_of(sums.theirs(pair)), :], w_qkv[...], 1, 1).astype(
-            jnp.bfloat16
-        )
-        sums.exchange(pair).start()
-        return unused
-
-    lax.fori_loop(0, 4, one_pair, 0)
-
-    def sum_pair(step, unused):
-        pair = 3 - step
-        own_sum[...] = dot_f32(grad_qkv[rows_of(sums.mine(pair)), :], w_qkv[...], 1, 1)
-        sums.exchange(pair).wait_recv()
-        norm_sums[pair] = (own_sum[...] + landed[pair].astype(jnp.float32)).astype(jnp.bfloat16)
-
-        @pl.when(pair > 0)
-        def _():
-            sums.deliver(pair).start()
-
-        return unused
-
-    lax.fori_loop(0, 4, sum_pair, 0)
-
-    def turn(tile, unused):
-        at = rows_of(tile, TILE)
-        grad_qkv_t[:, at] = grad_qkv[at, :].T
-        return unused
-
-    lax.fori_loop(0, grad_qkv.shape[0] // TILE, turn, 0)
-
-    def weight_tile(tile, unused):
-        qkv_parts[tile] = dot_f32(grad_qkv_t[...], normed[:, rows_of(tile, shard)], 1, 0).astype(
-            jnp.bfloat16
-        )
-        return unused
-
-    lax.fori_loop(0, devices_fsdp, weight_tile, 0)
-    qkv_copies = over_groups(
-        lambda to: qkv_parts.at[to], qkv_landed, group_send.at[0], group_recv.at[0]
-    )
-    for copy in qkv_copies:
-        copy.start()
+        {per_segment: after_prompt, per_segment + 2: units_between},
+    )
 
     total = output_sums[0].astype(jnp.float32)
     for pair in range(1, 4):
@@ -1307,6 +1441,45 @@
     )
     for copy in output_copies:
         copy.start()
+
+    def turn(tile, unused):
+        at = rows_of(tile, TILE)
+        grad_qkv_t[:, at] = grad_qkv[at, :].T
+        return unused
+
+    lax.fori_loop(0, grad_qkv.shape[0] // TILE, turn, 0)
+
+    def weight_tile(tile, unused):
+        qkv_parts[tile] = dot_f32(grad_qkv_t[...], normed[:, rows_of(tile, shard)], 1, 0).astype(
+            jnp.bfloat16
+        )
+        return unused
+
+    lax.fori_loop(0, devices_fsdp, weight_tile, 0)
+    qkv_copies = over_groups(
+        lambda to: qkv_parts.at[to], qkv_landed, group_send.at[0], group_recv.at[0]
+    )
+    for copy in qkv_copies:
+        copy.start()
+
+    def one_pair(step, unused):
+        pair = 3 - step
+        stage[pair] = dot_f32(grad_qkv[rows_of(sums.theirs(pair)), :], w_qkv[...], 1, 1).astype(
+            jnp.bfloat16
+        )
+        sums.exchange(pair).start()
+        return unused
+
+    lax.fori_loop(0, 4, one_pair, 0)
+
+    def sum_pair(step, unused):
+        pair = 3 - step
+        own_sum[...] = dot_f32(grad_qkv[rows_of(sums.mine(pair)), :], w_qkv[...], 1, 1)
+        sums.exchange(pair).wait_recv()
+        sums.finish(pair, own_sum[...] + landed[pair].astype(jnp.float32))
+        return unused
+
+    lax.fori_loop(0, 4, sum_pair, 0)
 
     def group_sum(own, landed_ref, copies):
         landed_ref[group] = own
@@ -1317,9 +1490,19 @@
             total = total + landed_ref[index].astype(jnp.float32)
         return total
 
-    units_stage[...] = group_sum(grad_units[group], units_landed, units_copies).astype(
-        jnp.bfloat16
-    )
+    units_landed[group] = grad_units[group]
+
+    @pl.when(place.at_end())
+    def _():
+        units_landed[devices_fsdp - 1 - group] = jnp.zeros_like(grad_units[group])
+
+    units_direct(2).wait_recv()
+    for step in (1, 3):
+        pl.when(place.heard(step))(units_direct(step).wait_recv)
+    units_total = units_landed[0].astype(jnp.float32)
+    for index in range(1, devices_fsdp):
+        units_total = units_total + units_landed[index].astype(jnp.float32)
+    units_stage[...] = units_total.astype(jnp.bfloat16)
 
     def half_of(ref, lines):
         def region(block, half):
@@ -1333,12 +1516,13 @@
     spread_u = Spread(
         place,
         own_of(units_stage, 3 * units),
-        half_of(units_all, 3 * units),
+        half_of(units_out, 3 * units),
         u_send,
         u_recv,
     )
     spread_u.start()
-    units_all[me] = units_stage[...]
+    save_units = pltpu.make_async_copy(units_stage, units_out.at[me], local_sem.at[0])
+    save_units.start()
 
     total = layer_sums[0].astype(jnp.float32)
     for pair, copy in enumerate(layer_copies):
@@ -1346,10 +1530,7 @@
         total = total + layer_received[pair + 1].astype(jnp.float32)
     layer[...] = (hidden[...] + total).astype(jnp.bfloat16)
 
-    total = norm_sums[0].astype(jnp.float32)
-    for pair in range(1, 4):
-        sums.deliver(pair).wait_recv()
-        total = total + norm_received[pair].astype(jnp.float32)
+    total = sums.collect()
     values = patches[...].astype(jnp.float32)
     gain_one = gains[0:1, :]
     factor = lax.rsqrt(jnp.mean(values * values, axis=-1, keepdims=True) + epsilon)
@@ -1398,10 +1579,11 @@
             :, index * cols : (index + 1) * cols
         ]
     spread_c = Spread(
-        place, own_of(columns_stage, 4 * shard), half_of(columns_all, 4 * shard), c_send, c_recv
+        place, own_of(columns_stage, 4 * shard), half_of(columns_out, 4 * shard), c_send, c_recv
     )
     spread_c.start()
-    columns_all[me] = columns_stage[...]
+    save_columns = pltpu.make_async_copy(columns_stage, columns_out.at[me], local_sem.at[1])
+    save_columns.start()
     spread_u.relay_third()
     for copy in gain_out:
         copy.wait_recv()
@@ -1412,13 +1594,13 @@
     spread_c.relay_first()
     spread_c.relay_second()
     spread_u.arrived(0, 7, 8, 9)
-    save_units = pltpu.make_async_copy(units_all, units_out, local_sem.at[0])
-    save_units.start()
     spread_c.relay_third()
     spread_c.arrived(0, 7, 8, 9)
-    save_columns = pltpu.make_async_copy(columns_all, columns_out, local_sem.at[1])
-    save_columns.start()
-    for copy in units_copies + layer_copies + qkv_copies + output_copies + gain_copies + gain_out:
+    for step in (1, 3):
+        pl.when(place.near(step))(units_direct(step).wait_send)
+    units_direct(2).wait_send()
+    pl.when(place.at_end())(units_far_copy.wait_send)
+    for copy in layer_copies + qkv_copies + output_copies + gain_copies + gain_out:
         copy.wait_send()
     sums.sent()
     output_pairs.sent()
@@ -1593,8 +1775,7 @@
             room(low, blocks, block_len, cols),
             room(low, tiles, cols, TILE),
             room(low, blocks, block_len, cols),
-            room(low, rows, cols),
-            room(low, local_rows, width),
+            room(low, blocks, block_len, width),
             room(low, local_rows, width),
             room(low, units, rows),
             room(low, units, rows),
@@ -1603,7 +1784,8 @@
             room(low, 4, 2, local_rows, width),
             room(full, 2, local_rows, width),
             room(low, 4, local_rows, width),
-            room(low, 4, local_rows, width),
+            room(low, 2, local_rows, width),
+            room(low, 2, local_rows // 2, width),
             room(full, groups, units, shard),
             room(low, local_rows, width),
             room(low, local_rows, width),
@@ -1611,9 +1793,10 @@
             dma(9),
             pltpu.SemaphoreType.DMA((8, groups - 1)),
             pltpu.SemaphoreType.DMA((8, groups - 1)),
+            dma(8),
         ]
-        + [dma(10)] * 8
-        + [dma(7)] * 4
+        + [dma(10)] * 12
+        + [dma(7)] * 2
         + [dma(4)] * 4,
         compiler_params=pltpu.CompilerParams(
             collective_id=0, has_side_effects=True, vmem_limit_bytes=66_000_000
@@ -1658,7 +1841,8 @@
             room(full, rows, cols),
             room(low, groups, 3 * units, shard),
             room(low, 3 * units, shard),
-            room(low, 8, 3 * units, shard),
+            room(low, 3 * units, shard),
+            room(low, 3 * units, shard),
             room(low, 4, local_rows, width),
             room(low, 4, groups, shard // 8, width),
             room(low, 4, groups, shard // 8, width),
@@ -1670,12 +1854,12 @@
             room(low, 4, local_rows, width),
             room(full, local_rows, width),
             room(low, 4, local_rows, width),
-            room(low, 4, local_rows, width),
+            room(low, 2, local_rows, width),
+            room(low, 2, local_rows // 2, width),
             room(low, 3 * cols, rows),
             room(low, groups, 3 * cols, shard),
             room(low, groups, 3 * cols, shard),
             room(low, 4 * shard, cols),
-            room(low, 8, 4 * shard, cols),
             room(full, groups, 8, shard),
             room(full, groups, 8, shard),
             room(full, 8, shard),
@@ -1683,6 +1867,7 @@
             dma(2),
             dma(groups - 1),
             dma(groups - 1),
+            dma(2),
             dma(4),
             dma(4),
             dma(4),
@@ -1750,7 +1935,7 @@
 
 
 def solution(mesh):
-    if mesh.shape["ctx"] == 8:
+    if mesh.shape["ctx"] == 8 and mesh.shape["fsdp"] == 4:
         per_device = heads_plan
     else:
         per_device = rows_plan

time: 262 us -> 245 us (0.935)
  Pallas kernels: 251 us -> 236 us
    pallas_call x1, Pallas kernels: 142 us -> 126 us  [heads_plan(): pl.pallas_call(functools.partial(forward_kernel, per_segment, groups), ou...]
where the time goes in v3:
time: 245 us; the launch traced here: 244 us
  Pallas kernels  236 us (96%)
  local copies, waits for them, and re-layouts  5.55 us (2%)
    pallas_call x1, Pallas kernels, heads_plan(): pl.pallas_call(functools.partial(forward_kernel, per_segment, groups), ou...  126 us
    pallas_call x1, Pallas kernels, heads_plan(): pl.pallas_call(functools.partial(backward_kernel, per_segment, groups), o...  102 us
    pallas_call x1, Pallas kernels, heads_plan(): pl.pallas_call(functools.partial(place_kernel, groups), out_shape=tuple((...  8.71 us

profile of v3, /device:TPU:0, one launch (start us, length us, event | category | flops | bytes accessed | tf_op | source)
XLA Modules:
  0.0 244.4 jit_solution(16677448015102715443)
XLA Ops:
  1.3 1.3 select_reduce_fusion.slot_of
  2.6 1.2 broadcast_in_dim.29.gain_attn
  3.8 1.2 broadcast_in_dim.30.gain_ffn
  5.0 125.5 %forward.1 = (bf16[16,128,384]{2,1,0:T(8,128)(2,1)}, bf16[2048,1024]{1,0:T(8,128)(2,1)}, f32[8,128,256]{2,1,0:T(8,128)}, f32[8,1,512]{2,1,0:T(1,128)}, bf16[1024...) custom-call(s32[16]{0:T(128)} %select_reduce_fusion.slot_of, ...), custom_call_target="tpu_custom_call" | custom-call | tf_op jit(solution)/shard_map/forward/pallas_call | solution.py:1736
  130.5 102.0 %backward.1 = (bf16[256,1024]{1,0:T(8,128)(2,1)}, f32[256,1024]{1,0:T(8,128)}, bf16[8,1056,256]{2,1,0:T(8,128)(2,1)}, bf16[8,1024,128]{2,1,0:T(8,128)(2,1)}, f32[8,256]{1,0:T(8,128)}) custom-call(s32[16]{0:T(128)} %select_reduce_fusion.slot_of, s32[16]{0:T(128)} %block_of.3, s32[1]{0:T(128)S(6)} %copy.26.length_ref, ...), custom_call_target="tpu_custom_call" | custom-call | tf_op jit(solution)/shard_map/backward/pallas_call | solution.py:1822
  232.5 1.3 fusion
  233.9 0.0 copy-start.1
  233.9 0.0 copy-start
  233.9 8.7 %place.1 = (f32[256,1024]{1,0:T(8,128)}, f32[256,1024]{1,0:T(8,128)}, f32[256,1024]{1,0:T(8,128)}, f32[256,1024]{1,0:T(8,128)}, f32[256,2816]{1,0:T(8,128)}, /*index=5*/f32[256,2816]{1,0:T(8,128)}, f32[704,1024]{1,0:T(8,128)}) custom-call(bf16[8,1056,256]{2,1,0:T(8,128)(2,1)} %get-tuple-element.51.units_all, bf16[8,1024,128]{2,1,0:T(8,128)(2,1)} %get-tuple-element.52.columns_all), custom_call_target="tpu_custom_call" | custom-call | tf_op jit(solution)/shard_map/place/pallas_call | solution.py:1916
  242.6 0.0 copy-done.1
  242.6 0.8 copy.27
  243.4 0.0 copy-done
  243.4 1.0 copy.28
Async XLA Ops:
  233.9 8.7 %copy-start.1 = (bf16[256,1024]{1,0:T(8,128)(2,1)S(1)}, bf16[256,1024]{1,0:T(8,128)(2,1)}, u32[]{:S(2)}) copy-start(bf16[256,1024]{1,0:T(8,128)(2,1)} %get-tuple-element.49) | copy-start | bytes 1572868
  233.9 9.5 %copy-start = (f32[256,1024]{1,0:T(8,128)S(1)}, f32[256,1024]{1,0:T(8,128)}, u32[]{:S(2)}) copy-start(f32[256,1024]{1,0:T(8,128)} %get-tuple-element.50) | copy-start | bytes 3145732

commit v4 on v3

--- a/solution.py
+++ b/solution.py
@@ -479,8 +479,7 @@
     value,
     grad,
     key_t,
-    grad_key,
-    grad_value,
+    grad_sums,
     between,
 ):
     rows = qkv.shape[0] * qkv.shape[1]
@@ -491,8 +490,7 @@
     to_logical(slot_of, grad_attn, 0, grad)
     for tile in range(rows // TILE):
         key_t[tile] = load_tile(key, tile).T
-    grad_key[...] = jnp.zeros_like(grad_key)
-    grad_value[...] = jnp.zeros_like(grad_value)
+    grad_sums[...] = jnp.zeros_like(grad_sums)
     masks = head_masks()
 
     def one_tile(tile, unused):
@@ -510,15 +508,15 @@
         log_total = lse[tile]
 
         def step(key_tile, grad_query, kind):
-            keys_at = pl.ds(pl.multiple_of(key_tile * TILE, TILE), TILE)
+            keys_at = pl.ds(pl.multiple_of(key_tile * 2 * HEAD, 2 * HEAD), 2 * HEAD)
             scores = dot_f32(load_tile(key, key_tile), both, 1, 1)
             if kind != "full":
                 scores = jnp.where(tile_mask(kind, key_tile, length), scores, masked_value)
             probs = jnp.exp(scores - log_total)
             grad_probs = dot_f32(load_tile(value, key_tile), both_grad, 1, 1)
             grad_scores = (probs * (grad_probs - delta)).astype(jnp.bfloat16)
-            grad_value[keys_at, :] += dot_f32(probs.astype(jnp.bfloat16), both_grad, 1, 0)
-            grad_key[keys_at, :] += dot_f32(grad_scores, both, 1, 0)
+            grad_sums[1, :, keys_at] += dot_f32(probs.astype(jnp.bfloat16), both_grad, 1, 0)
+            grad_sums[0, :, keys_at] += dot_f32(grad_scores, both, 1, 0)
             return grad_query + dot_f32(key_t[key_tile], grad_scores, 1, 0)
 
         grad_query = over_keys(
@@ -530,8 +528,10 @@
         return unused
 
     tiles_between(rows // TILE, one_tile, between)
-    key[...] = grad_key[...].astype(jnp.bfloat16).reshape(key.shape)
-    value[...] = grad_value[...].astype(jnp.bfloat16).reshape(value.shape)
+    for tile in range(rows // TILE):
+        at = slice(tile * 2 * HEAD, (tile + 1) * 2 * HEAD)
+        store_tile(key, tile, grad_sums[0, :, at].astype(jnp.bfloat16))
+        store_tile(value, tile, grad_sums[1, :, at].astype(jnp.bfloat16))
     to_stored(block_of, query, grad_qkv, 0)
     to_stored(block_of, key, grad_qkv, 2 * HEAD)
     to_stored(block_of, value, grad_qkv, 4 * HEAD)
@@ -649,6 +649,7 @@
 class PairSum:
     def __init__(self, place, stage, landed, sums, received, send, recv, out_send, out_recv):
         self.place = place
+        self.slot = lambda pair: pair
         self.stage, self.landed, self.sums, self.received = stage, landed, sums, received
         self.send, self.recv, self.out_send, self.out_recv = send, recv, out_send, out_recv
 
@@ -663,10 +664,13 @@
     def theirs(self, pair):
         return self.mine(pair) + 1 - 2 * self.place.core
 
+    def staged(self, pair):
+        return self.stage.at[self.slot(pair)]
+
     def exchange(self, pair):
         return remote(
-            self.stage.at[pair],
-            self.landed.at[pair],
+            self.staged(pair),
+            self.landed.at[self.slot(pair)],
             self.send.at[pair],
             self.recv.at[pair],
             {"ctx": self.place.peer(1)},
@@ -688,9 +692,17 @@
                 self.deliver(pair).wait_send()
 
 
+class OutputSum(PairSum):
+    def staged(self, pair):
+        return self.stage.at[:, self.theirs(pair)]
+
+
 class CrossSum(PairSum):
-    def __init__(self, place, stage, landed, sums, received, passed, send, recv, out_send, out_recv):
+    def __init__(
+        self, place, slot, stage, landed, sums, received, passed, send, recv, out_send, out_recv
+    ):
         super().__init__(place, stage, landed, sums, received, send, recv, out_send, out_recv)
+        self.slot = slot
         self.passed = passed
 
     def half(self, which):
@@ -744,8 +756,6 @@
         return total
 
     def sent(self):
-        for pair in range(4):
-            self.exchange(pair).wait_send()
         for which in (0, 1):
             self.far(which).wait_send()
             self.deliver(which + 1).wait_send()
@@ -755,7 +765,7 @@
     return lambda half: pl.ds(0 if half in (None, 0) else count // 2, count if half is None else count // 2)
 
 
-def forward_kernel(
+def layer_kernel(
     per_segment,
     devices_fsdp,
     slot_of,
@@ -772,22 +782,24 @@
     w_down,
     gain_attn,
     gain_ffn,
+    normed_out,
+    layer,
+    grad_patches,
+    units_out,
+    columns_out,
+    gains_out,
     qkv,
-    normed_out,
     attn_t,
     lse,
-    qkv_out,
-    gains_out,
     grad_units,
     grad_output,
     layer_sums,
     hidden,
     grad_hidden,
-    gain_part,
-    grad_attn_out,
     rows_all,
     grads,
     normed_ffn,
+    attn_all,
     w_qkv,
     output_all,
     gate_t,
@@ -802,22 +814,36 @@
     key,
     value_t,
     kept,
-    attn_all,
+    grad,
     attn_rows,
-    inner_t,
-    grad_gate_t,
-    grad_up_t,
+    units_t,
     stage,
     landed,
     own_sum,
     norm_sums,
     norm_received,
     norm_passed,
-    down_tiles,
     grad_branch,
     grad_rows,
     grad_attn,
+    units_landed,
+    units_far,
+    units_near,
+    units_stage,
+    output_landed,
+    output_sums,
+    output_received,
+    output_total,
+    output_group,
+    qkv_landed,
+    columns_stage,
+    gain_parts,
+    gain_landed,
+    gain_total,
+    gain_all,
     local_sem,
+    save_sem,
+    unit_sem,
     group_send,
     group_recv,
     pass_send,
@@ -833,12 +859,35 @@
     second_recv,
     third_send,
     third_recv,
+    u_send,
+    u_recv,
+    c_send,
+    c_recv,
     b_send,
     b_recv,
+    gain_out_send,
+    gain_out_recv,
     pair_send,
     pair_recv,
     out_send,
     out_recv,
+    back_pair_send,
+    back_pair_recv,
+    back_out_send,
+    back_out_recv,
+    wo_send,
+    wo_recv,
+    wo_out_send,
+    wo_out_recv,
+    layer_send,
+    layer_recv,
+    units_send,
+    units_recv,
+    gain_send,
+    gain_recv,
+    far_sem,
+    late_send,
+    late_recv,
 ):
     place = Place(devices_fsdp)
     me, group = place.me, place.group
@@ -847,6 +896,29 @@
     shard = w_query.shape[0]
     part = w_down.shape[1]
     units = part * devices_fsdp
+    span = part * 8
+    held = qkv.shape[0] // 8
+
+    def unit_range(index):
+        return span * index // 128 * 128, -(-span * (index + 1) // 128) * 128
+
+    def unit_copies(weight, target, first):
+        copies = []
+        for index in range(devices_fsdp):
+            low, high = unit_range(index)
+            copies.append(
+                pltpu.make_async_copy(
+                    weight.at[:, low:high],
+                    target.at[index // 2, index % 2, :, 0 : high - low],
+                    unit_sem.at[first + index],
+                )
+            )
+        return copies
+
+    gate_copies = unit_copies(w_gate, stage, 0)
+    up_copies = unit_copies(w_up, landed, devices_fsdp)
+    for copy in gate_copies + up_copies:
+        copy.start()
     place.meet()
 
     def rows_of(block, count=local_rows):
@@ -937,37 +1009,50 @@
     send_group(3)
     send_group(4)
 
-    def pick_units(weight, target):
-        span = part * 8
+    def pick_units(copies, source, target):
         pieces = []
         for index in range(devices_fsdp):
-            low = span * index // 128 * 128
-            high = -(-span * (index + 1) // 128) * 128
+            low, high = unit_range(index)
             unit = lax.broadcasted_iota(jnp.int32, (part, high - low), 0)
             column = lax.broadcasted_iota(jnp.int32, (part, high - low), 1)
             chosen = (column + low == unit + span * index + part * me).astype(jnp.bfloat16)
-            pieces.append(dot_f32(chosen, weight[:, low:high], 1, 1))
+            copies[index].wait()
+            pieces.append(
+                dot_f32(chosen, source[index // 2, index % 2, :, 0 : high - low], 1, 1)
+            )
         target[...] = jnp.concatenate(pieces, axis=0).astype(jnp.bfloat16)
 
-    pick_units(w_gate, gate_stage)
-    pick_units(w_up, up_stage)
+    pick_units(gate_copies, stage, gate_stage)
+    pick_units(up_copies, landed, up_stage)
     send_group(5)
     send_group(6)
     send_group(7)
 
     rows_all[rows_of(me), :] = patches[...]
-    grads[rows_of(me), :] = cotangent[...]
+    load_grads = pltpu.make_async_copy(cotangent, grads.at[rows_of(me)], save_sem.at[0])
+    load_grads.start()
+    spread_x.relay_first()
     for index in (0, 1, 2, 3):
         pass_group(index)
-    spread_x.relay_first()
     spread_x.relay_second()
     spread_g = Spread(place, own_half(cotangent), rows_half(grads), g_send, g_recv)
     spread_g.start()
     spread_x.relay_third()
+    pass_group(4)
     spread_x.arrived(0, 7, 8, 9)
     for index in (0, 1, 2, 3):
         group_arrived(index)
     gain_one = gains[0:1, :]
+
+    def output_half(block, half):
+        if half is None:
+            return output_all.at[:, block]
+        lines = output_all.shape[2]
+        return output_all.at[:, block, halves(lines)(half)]
+
+    group_arrived(4)
+    spread_o = Spread(place, lambda half: output_half(me, half), output_half, o_send, o_recv)
+    spread_o.start()
 
     def project(block, unused):
         at = rows_of(block)
@@ -981,18 +1066,7 @@
     lax.fori_loop(0, 8, project, 0)
     save_normed = pltpu.make_async_copy(normed_ffn, normed_out, local_sem.at[8])
     save_normed.start()
-
-    def output_half(block, half):
-        if half is None:
-            return output_all.at[:, block]
-        lines = output_all.shape[2]
-        return output_all.at[:, block, halves(lines)(half)]
-
-    pass_group(4)
-    group_arrived(4)
-    pass_group(5)
-    spread_o = Spread(place, lambda half: output_half(me, half), output_half, o_send, o_recv)
-    spread_o.start()
+    spread_g.relay_first()
 
     def attn_spread(first, count, send, recv):
         def part(half):
@@ -1015,26 +1089,19 @@
     attn_third = attn_spread(half_blocks * 3 // 2, half_blocks // 2, third_send, third_recv)
 
     def after_two():
-        spread_g.relay_first()
-
-    def after_prompt():
-        attn_first.start()
-        pass_group(6)
+        pass_group(5)
 
     def after_more():
         spread_g.relay_second()
-        spread_o.relay_first()
+        pass_group(6)
 
     def after_half():
         attn_second.start()
-        spread_o.relay_second()
-        spread_g.relay_third()
+        spread_o.relay_first()
 
     def after_most():
         pass_group(7)
-        attn_first.relay_first()
-        attn_first.relay_second()
-        spread_o.relay_third()
+        spread_o.relay_second()
 
     attend_forward(
         per_segment,
@@ -1049,7 +1116,7 @@
         kept,
         {
             per_segment // 2: after_two,
-            per_segment: after_prompt,
+            per_segment: attn_first.start,
             per_segment + 1: after_more,
             per_segment + per_segment // 2: after_half,
             2 * per_segment - 1: after_most,
@@ -1057,18 +1124,23 @@
     )
     attn_third.start()
     attn_all[:, :, my_cols] = kept[...]
-    attn_first.relay_third()
-    attn_second.relay_first()
-    attn_second.relay_second()
+    spread_g.relay_third()
+    attn_first.relay_first()
+    attn_first.relay_second()
+    spread_o.relay_third()
     for index in (5, 6, 7):
         group_arrived(index)
     down[...] = jnp.concatenate(
         [down_parts[index].astype(jnp.float32) for index in range(devices_fsdp)], axis=0
     ).astype(jnp.bfloat16)
+    attn_second.relay_first()
+    attn_second.relay_second()
+    attn_first.relay_third()
     attn_third.relay_first()
+    attn_third.relay_second()
     attn_second.relay_third()
-    attn_third.relay_second()
     save_normed.wait()
+    load_grads.wait()
     spread_g.arrived(0, 7, 8, 9)
     spread_o.arrived(0, 7, 8, 9)
     attn_third.relay_third()
@@ -1082,7 +1154,6 @@
         ]
 
     def attn_of(block):
-        held = attn_all.shape[0] // 8
         return jnp.concatenate(
             [attn_all[block_of[block * held + index]] for index in range(held)], axis=0
         )
@@ -1090,6 +1161,7 @@
     gain_two = gains[8:9, :]
     sums = CrossSum(
         place,
+        lambda pair: lax.rem(pair, 2),
         stage,
         landed,
         norm_sums,
@@ -1122,9 +1194,9 @@
         grad_up = grad_inner * activated
         gate_low = grad_gate.astype(jnp.bfloat16)
         up_low = grad_up.astype(jnp.bfloat16)
-        inner_t[:, at] = inner.T.astype(jnp.bfloat16)
-        grad_gate_t[:, at] = grad_gate.T.astype(jnp.bfloat16)
-        grad_up_t[:, at] = grad_up.T.astype(jnp.bfloat16)
+        units_t[0:units, at] = inner.T.astype(jnp.bfloat16)
+        units_t[units : 2 * units, at] = grad_gate.T.astype(jnp.bfloat16)
+        units_t[2 * units : 3 * units, at] = grad_up.T.astype(jnp.bfloat16)
         return (
             dot_f32(inner_low, down[...], 1, 0),
             dot_f32(gate_low, gate_t[...], 1, 0) + dot_f32(up_low, up_t[...], 1, 0),
@@ -1132,66 +1204,116 @@
 
     def one_pair(step, unused):
         pair = 3 - step
+        slot = lax.rem(pair, 2)
         layer, norm = feed(sums.theirs(pair))
-        stage[pair, 0] = layer.astype(jnp.bfloat16)
-        stage[pair, 1] = norm.astype(jnp.bfloat16)
+
+        @pl.when(step > 1)
+        def _():
+            sums.exchange(pair + 2).wait_send()
+
+        stage[slot, 0] = layer.astype(jnp.bfloat16)
+        stage[slot, 1] = norm.astype(jnp.bfloat16)
         sums.exchange(pair).start()
         layer, norm = feed(sums.mine(pair))
         own_sum[0] = layer
         own_sum[1] = norm
         sums.exchange(pair).wait_recv()
-        layer_sums[pair] = (own_sum[0] + landed[pair, 0].astype(jnp.float32)).astype(jnp.bfloat16)
-        sums.finish(pair, own_sum[1] + landed[pair, 1].astype(jnp.float32))
+        layer_sums[pair] = (
+            (own_sum[0] + landed[slot, 0].astype(jnp.float32))
+            .astype(jnp.bfloat16)
+            .reshape(layer_sums.shape[1:])
+        )
+        sums.finish(pair, own_sum[1] + landed[slot, 1].astype(jnp.float32))
         return unused
 
     lax.fori_loop(0, 4, one_pair, 0)
+    for pair in (1, 0):
+        sums.exchange(pair).wait_send()
     attn_rows[...] = attn_of(me)
     hidden[...] = hidden_of(me, attn_rows[...])
+    load_normed = pltpu.make_async_copy(normed_out, rows_all, local_sem.at[8])
+    load_normed.start()
 
     def units_tile(tile, unused):
         at = rows_of(tile, shard)
         low = normed_ffn[:, at]
-        grad_units[tile, 0:units, :] = dot_f32(grad_gate_t[...], low, 1, 0).astype(jnp.bfloat16)
-        grad_units[tile, units : 2 * units, :] = dot_f32(grad_up_t[...], low, 1, 0).astype(
+        grad_units[tile, 0 : 2 * units, :] = dot_f32(units_t[units : 3 * units, :], low, 1, 0).astype(
             jnp.bfloat16
         )
-        down_tiles[tile] = dot_f32(inner_t[...], grads[:, at], 1, 0)
+        down_tile = dot_f32(units_t[0:units, :], grads[:, at], 1, 0)
+        for half in (0, 1):
+            own_sum[half, 0 : units // 2, at] = down_tile[half * units // 2 : (half + 1) * units // 2]
         return unused
 
     lax.fori_loop(0, devices_fsdp, units_tile, 0)
     for index in range(devices_fsdp):
+        first = index % 2 * part
         grad_units[index, 2 * units : 3 * units, :] = jnp.concatenate(
             [
-                down_tiles[tile, index * part : (index + 1) * part, :]
+                own_sum[index // 2, first : first + part, tile * shard : (tile + 1) * shard]
                 for tile in range(devices_fsdp)
             ],
             axis=0,
         ).astype(jnp.bfloat16)
 
+    def units_copy(step, source):
+        return remote(
+            source,
+            units_landed.at[group],
+            units_send.at[step - 1],
+            units_recv.at[step - 1],
+            {"fsdp": place.other_group(step)},
+        )
+
+    def units_direct(step):
+        return units_copy(step, grad_units.at[place.other_group(step)])
+
+    units_far_copy = remote(
+        grad_units.at[devices_fsdp - 1 - group],
+        units_far,
+        far_sem.at[0],
+        far_sem.at[1],
+        {"fsdp": 1 + group // 3},
+    )
+    units_sum_copy = units_copy(2, units_near)
+
+    @pl.when(place.at_end())
+    def _():
+        units_far_copy.start()
+        units_direct(2).start()
+
+    for step in (1, 3):
+        pl.when(place.near(step))(units_direct(step).start)
+
     total = sums.collect()
     values = hidden[...]
     factor = lax.rsqrt(jnp.mean(values * values, axis=-1, keepdims=True) + epsilon)
     scaled = total * gain_two
-    gain_part[...] = jnp.sum(total * values * factor, axis=0, keepdims=True)
+    gain_part = jnp.sum(total * values * factor, axis=0, keepdims=True)
     whole = (
-        cotangent[...].astype(jnp.float32)
+        grads[rows_of(me), :].astype(jnp.float32)
         + factor * scaled
         - values * (factor * factor * factor) * jnp.mean(scaled * values, axis=-1, keepdims=True)
     )
     grad_hidden[...] = whole
     grad_branch[...] = whole.astype(jnp.bfloat16)
-    grad_rows[...] = dot_f32(grad_branch[...], output_all[...].reshape(width, width), 1, 1).astype(
-        jnp.bfloat16
+    grad_rows[...] = (
+        dot_f32(grad_branch[...], output_all[...].reshape(width, width), 1, 1)
+        .astype(jnp.bfloat16)
+        .reshape(grad_rows.shape)
     )
     to_heads = swap(
-        lambda flip: grad_rows.at[:, rows_of(place.peer(flip), cols)],
-        grad_attn.at[rows_of(me)],
+        lambda flip: grad_rows.at[:, :, rows_of(place.peer(flip), cols)],
+        grad_attn.at[pl.ds(me * held, held)],
         b_send,
         b_recv,
     )
+    for spread in (spread_g, spread_o, attn_first, attn_second, attn_third):
+        spread.sent()
+    sums.sent()
     for copy in to_heads:
         copy.start()
-    grad_attn[rows_of(me), :] = grad_rows[:, my_cols]
+    grad_attn[pl.ds(me * held, held)] = grad_rows[:, :, my_cols]
 
     for index in range(devices_fsdp):
         piece = attn_rows[:, index * shard : (index + 1) * shard].T
@@ -1200,116 +1322,12 @@
             .astype(jnp.bfloat16)
             .reshape(8, shard // 8, width)
         )
-    qkv_out[...] = w_qkv[...]
-    gains_out[...] = gains[...]
     for copy in to_heads:
         copy.wait_recv()
-    grad_attn_out[...] = grad_attn[...].reshape(grad_attn_out.shape)
-
     for index in range(8):
         group_sent(index)
-    spread_g.sent()
-    spread_o.sent()
-    for spread in (attn_first, attn_second, attn_third):
-        spread.sent()
     for copy in to_heads:
         copy.wait_send()
-    sums.sent()
-
-
-def backward_kernel(
-    per_segment,
-    devices_fsdp,
-    slot_of,
-    block_of,
-    length_ref,
-    qkv,
-    grad_attn,
-    attn_t,
-    lse,
-    normed,
-    w_qkv,
-    gains,
-    patches,
-    grad_hidden,
-    hidden,
-    layer_sums,
-    grad_units,
-    grad_output,
-    gain_part,
-    layer,
-    grad_patches,
-    units_out,
-    columns_out,
-    gains_out,
-    grad_qkv,
-    query,
-    key,
-    value,
-    grad,
-    key_t,
-    grad_key,
-    grad_value,
-    units_landed,
-    units_far,
-    units_near,
-    units_stage,
-    layer_received,
-    output_stage,
-    output_landed,
-    output_sums,
-    output_received,
-    output_total,
-    output_group,
-    stage,
-    landed,
-    own_sum,
-    norm_sums,
-    norm_received,
-    norm_passed,
-    grad_qkv_t,
-    qkv_parts,
-    qkv_landed,
-    columns_stage,
-    gain_stage,
-    gain_landed,
-    gain_total,
-    gain_all,
-    local_sem,
-    units_send,
-    units_recv,
-    far_sem,
-    layer_send,
-    layer_recv,
-    wo_send,
-    wo_recv,
-    wo_out_send,
-    wo_out_recv,
-    group_send,
-    group_recv,
-    pair_send,
-    pair_recv,
-    out_send,
-    out_recv,
-    u_send,
-    u_recv,
-    c_send,
-    c_recv,
-    gain_send,
-    gain_recv,
-    gain_out_send,
-    gain_out_recv,
-):
-    place = Place(devices_fsdp)
-    me, group = place.me, place.group
-    local_rows, width = patches.shape
-    shard = width // devices_fsdp
-    cols = width // 8
-    units = grad_units.shape[1] // 3
-    place.meet()
-
-    def rows_of(block, count=local_rows):
-        return pl.ds(pl.multiple_of(block * count, count), count)
 
     def over_groups(source, target, send, recv):
         return [
@@ -1323,35 +1341,6 @@
             for step in range(1, devices_fsdp)
         ]
 
-    def units_copy(step, source):
-        return remote(
-            source,
-            units_landed.at[group],
-            units_send.at[step - 1],
-            units_recv.at[step - 1],
-            {"fsdp": place.other_group(step)},
-        )
-
-    def units_direct(step):
-        return units_copy(step, grad_units.at[place.other_group(step)])
-
-    units_far_copy = remote(
-        grad_units.at[devices_fsdp - 1 - group],
-        units_far,
-        far_sem.at[0],
-        far_sem.at[1],
-        {"fsdp": 1 + group // 3},
-    )
-    units_sum_copy = units_copy(2, units_near)
-
-    @pl.when(place.at_end())
-    def _():
-        units_far_copy.start()
-        units_direct(2).start()
-
-    for step in (1, 3):
-        pl.when(place.near(step))(units_direct(step).start)
-
     def units_between():
         @pl.when(place.between())
         def _():
@@ -1364,19 +1353,20 @@
 
     sums = CrossSum(
         place,
+        lambda pair: (pair // 2, lax.rem(pair, 2)),
         stage,
         landed,
         norm_sums,
         norm_received,
         norm_passed,
-        pair_send,
-        pair_recv,
-        out_send,
-        out_recv,
-    )
-    output_pairs = PairSum(
+        back_pair_send,
+        back_pair_recv,
+        back_out_send,
+        back_out_recv,
+    )
+    output_pairs = OutputSum(
         place,
-        output_stage,
+        grad_output,
         output_landed,
         output_sums,
         output_received,
@@ -1386,12 +1376,11 @@
         wo_out_recv,
     )
     for pair in range(4):
-        output_stage[pair] = grad_output[:, output_pairs.theirs(pair)]
         output_pairs.exchange(pair).start()
     layer_copies = [
         remote(
             layer_sums.at[pair],
-            layer_received.at[pair],
+            attn_all.at[pair * held : (pair + 1) * held],
             layer_send.at[pair],
             layer_recv.at[pair],
             {"ctx": sums.mine(pair)},
@@ -1420,15 +1409,14 @@
         grad_attn,
         attn_t,
         lse,
-        grad_qkv,
+        grads,
         query,
         key,
-        value,
+        kept,
         grad,
-        key_t,
-        grad_key,
-        grad_value,
-        {per_segment: after_prompt, per_segment + 2: units_between},
+        value_t,
+        own_sum,
+        {per_segment // 2: units_between, per_segment: after_prompt},
     )
 
     total = output_sums[0].astype(jnp.float32)
@@ -1437,36 +1425,41 @@
         total = total + output_received[pair].astype(jnp.float32)
     output_total[...] = total.astype(jnp.bfloat16)
     output_copies = over_groups(
-        lambda to: output_total.at[to], output_group, group_send.at[1], group_recv.at[1]
+        lambda to: output_total.at[to], output_group, late_send.at[1], late_recv.at[1]
     )
     for copy in output_copies:
         copy.start()
 
     def turn(tile, unused):
         at = rows_of(tile, TILE)
-        grad_qkv_t[:, at] = grad_qkv[at, :].T
+        units_t[0 : 3 * cols, at] = grads[at, 0 : 3 * cols].T
         return unused
 
-    lax.fori_loop(0, grad_qkv.shape[0] // TILE, turn, 0)
+    lax.fori_loop(0, grads.shape[0] // TILE, turn, 0)
+    load_normed.wait()
 
     def weight_tile(tile, unused):
-        qkv_parts[tile] = dot_f32(grad_qkv_t[...], normed[:, rows_of(tile, shard)], 1, 0).astype(
-            jnp.bfloat16
-        )
+        at = rows_of(tile, shard)
+        normed_ffn[0 : 3 * cols, at] = dot_f32(
+            units_t[0 : 3 * cols, :], rows_all[:, at], 1, 0
+        ).astype(jnp.bfloat16)
         return unused
+
+    def qkv_parts(to):
+        return normed_ffn.at[0 : 3 * cols, rows_of(to, shard)]
 
     lax.fori_loop(0, devices_fsdp, weight_tile, 0)
     qkv_copies = over_groups(
-        lambda to: qkv_parts.at[to], qkv_landed, group_send.at[0], group_recv.at[0]
+        qkv_parts, qkv_landed, late_send.at[0], late_recv.at[0]
     )
     for copy in qkv_copies:
         copy.start()
 
     def one_pair(step, unused):
         pair = 3 - step
-        stage[pair] = dot_f32(grad_qkv[rows_of(sums.theirs(pair)), :], w_qkv[...], 1, 1).astype(
-            jnp.bfloat16
-        )
+        stage[pair // 2, lax.rem(pair, 2)] = dot_f32(
+            grads[rows_of(sums.theirs(pair)), 0 : 3 * cols], w_qkv[...], 1, 1
+        ).astype(jnp.bfloat16)
         sums.exchange(pair).start()
         return unused
 
@@ -1474,9 +1467,11 @@
 
     def sum_pair(step, unused):
         pair = 3 - step
-        own_sum[...] = dot_f32(grad_qkv[rows_of(sums.mine(pair)), :], w_qkv[...], 1, 1)
+        own_sum[0] = dot_f32(grads[rows_of(sums.mine(pair)), 0 : 3 * cols], w_qkv[...], 1, 1)
         sums.exchange(pair).wait_recv()
-        sums.finish(pair, own_sum[...] + landed[pair].astype(jnp.float32))
+        sums.finish(
+            pair, own_sum[0] + landed[pair // 2, lax.rem(pair, 2)].astype(jnp.float32)
+        )
         return unused
 
     lax.fori_loop(0, 4, sum_pair, 0)
@@ -1521,38 +1516,42 @@
         u_recv,
     )
     spread_u.start()
-    save_units = pltpu.make_async_copy(units_stage, units_out.at[me], local_sem.at[0])
+    save_units = pltpu.make_async_copy(units_stage, units_out.at[me], save_sem.at[0])
     save_units.start()
 
     total = layer_sums[0].astype(jnp.float32)
     for pair, copy in enumerate(layer_copies):
         copy.wait_recv()
-        total = total + layer_received[pair + 1].astype(jnp.float32)
-    layer[...] = (hidden[...] + total).astype(jnp.bfloat16)
+        at = slice((pair + 1) * held, (pair + 2) * held)
+        total = total + attn_all[at].astype(jnp.float32)
+    grad_rows[...] = (hidden[...].reshape(total.shape) + total).astype(jnp.bfloat16)
+    save_layer = pltpu.make_async_copy(grad_rows, layer, save_sem.at[2])
+    save_layer.start()
 
     total = sums.collect()
     values = patches[...].astype(jnp.float32)
-    gain_one = gains[0:1, :]
     factor = lax.rsqrt(jnp.mean(values * values, axis=-1, keepdims=True) + epsilon)
     scaled = total * gain_one
-    gain_stage[...] = jnp.zeros_like(gain_stage)
+    gain_parts[...] = jnp.zeros_like(gain_parts)
     attn_part = jnp.sum(total * values * factor, axis=0, keepdims=True)
-    ffn_part = gain_part[...]
+    ffn_part = gain_part
     for index in range(devices_fsdp):
         at = slice(index * shard, (index + 1) * shard)
-        gain_stage[index, 0:1, :] = attn_part[:, at]
-        gain_stage[index, 1:2, :] = ffn_part[:, at]
-    gain_copies = over_groups(lambda to: gain_stage.at[to], gain_landed, gain_send, gain_recv)
+        gain_parts[index, 0:1, :] = attn_part[:, at]
+        gain_parts[index, 1:2, :] = ffn_part[:, at]
+    gain_copies = over_groups(lambda to: gain_parts.at[to], gain_landed, gain_send, gain_recv)
     for copy in gain_copies:
         copy.start()
-    grad_patches[...] = (
+    grad_hidden[...] = (
         grad_hidden[...]
         + factor * scaled
         - values * (factor * factor * factor) * jnp.mean(scaled * values, axis=-1, keepdims=True)
     )
+    save_rows = pltpu.make_async_copy(grad_hidden, grad_patches, save_sem.at[3])
+    save_rows.start()
     spread_u.relay_first()
     spread_u.relay_second()
-    gain_total[...] = group_sum(gain_stage[group], gain_landed, gain_copies)
+    gain_total[...] = group_sum(gain_parts[group], gain_landed, gain_copies)
     gain_out = [
         remote(
             gain_total,
@@ -1567,7 +1566,7 @@
         copy.start()
     gain_all[me] = gain_total[...]
 
-    turned = group_sum(qkv_parts[group], qkv_landed, qkv_copies).T.astype(jnp.bfloat16)
+    turned = group_sum(qkv_parts(group)[...], qkv_landed, qkv_copies).T.astype(jnp.bfloat16)
     for index in range(3):
         columns_stage[index * shard : (index + 1) * shard, :] = turned[
             :, index * cols : (index + 1) * cols
@@ -1582,7 +1581,7 @@
         place, own_of(columns_stage, 4 * shard), half_of(columns_out, 4 * shard), c_send, c_recv
     )
     spread_c.start()
-    save_columns = pltpu.make_async_copy(columns_stage, columns_out.at[me], local_sem.at[1])
+    save_columns = pltpu.make_async_copy(columns_stage, columns_out.at[me], save_sem.at[1])
     save_columns.start()
     spread_u.relay_third()
     for copy in gain_out:
@@ -1602,8 +1601,12 @@
     pl.when(place.at_end())(units_far_copy.wait_send)
     for copy in layer_copies + qkv_copies + output_copies + gain_copies + gain_out:
         copy.wait_send()
+    for pair in range(4):
+        sums.exchange(pair).wait_send()
     sums.sent()
     output_pairs.sent()
+    save_layer.wait()
+    save_rows.wait()
     spread_u.sent()
     spread_c.sent()
     save_units.wait()
@@ -1719,48 +1722,31 @@
     def room(kind, *dims):
         return pltpu.VMEM(dims, kind)
 
-    (
-        qkv,
-        normed,
-        attn_t,
-        lse,
-        w_qkv,
-        gains,
-        grad_units,
-        grad_output,
-        layer_sums,
-        hidden,
-        grad_hidden,
-        gain_part,
-        grad_attn,
-    ) = pl.pallas_call(
-        functools.partial(forward_kernel, per_segment, groups),
+    unused, layer, grad_rows, units_all, columns_all, gains_sum = pl.pallas_call(
+        functools.partial(layer_kernel, per_segment, groups),
         out_shape=(
-            shaped(low, blocks, block_len, 3 * cols),
             shaped(low, rows, width),
-            shaped(full, tiles, cols, TILE),
-            shaped(full, tiles, 1, 2 * TILE),
-            shaped(low, width, 3 * cols),
-            shaped(full, 16, width),
-            shaped(low, groups, 3 * units, shard),
-            shaped(low, groups, 8, shard // 8, width),
-            shaped(low, 4, local_rows, width),
+            shaped(low, blocks // 8, block_len, width),
             shaped(full, local_rows, width),
-            shaped(full, local_rows, width),
-            shaped(full, 1, width),
-            shaped(low, blocks, block_len, cols),
+            shaped(low, 8, 3 * units, shard),
+            shaped(low, 8, 4 * shard, cols),
+            shaped(full, 8, shard),
         ),
-        in_specs=[smem] * 3
-        + [vmem] * 2
-        + [anywhere] * 4
-        + [vmem] * 2
-        + [anywhere]
-        + [vmem] * 2,
-        out_specs=(vmem, anywhere) + (vmem,) * 11,
+        in_specs=[smem] * 3 + [vmem] + [anywhere] * 8 + [vmem] * 2,
+        out_specs=(anywhere,) * 5 + (vmem,),
         scratch_shapes=[
+            room(low, blocks, block_len, 3 * cols),
+            room(full, tiles, cols, TILE),
+            room(full, tiles, 1, 2 * TILE),
+            room(low, groups, 3 * units, shard),
+            room(low, groups, 8, shard // 8, width),
+            room(low, 4, blocks // 8, block_len, width),
+            room(full, local_rows, width),
+            room(full, local_rows, width),
             room(low, rows, width),
             room(low, rows, width),
             room(low, rows, width),
+            room(low, blocks, block_len, width),
             room(low, width, 3 * cols),
             room(low, groups, 8, shard // 8, width),
             room(low, units, width),
@@ -1775,33 +1761,85 @@
             room(low, blocks, block_len, cols),
             room(low, tiles, cols, TILE),
             room(low, blocks, block_len, cols),
-            room(low, blocks, block_len, width),
+            room(low, blocks, block_len, cols),
             room(low, local_rows, width),
-            room(low, units, rows),
-            room(low, units, rows),
-            room(low, units, rows),
-            room(low, 4, 2, local_rows, width),
-            room(low, 4, 2, local_rows, width),
+            room(low, 3 * units, rows),
+            room(low, 2, 2, local_rows, width),
+            room(low, 2, 2, local_rows, width),
             room(full, 2, local_rows, width),
             room(low, 4, local_rows, width),
             room(low, 2, local_rows, width),
             room(low, 2, local_rows // 2, width),
-            room(full, groups, units, shard),
             room(low, local_rows, width),
-            room(low, local_rows, width),
-            room(low, rows, cols),
+            room(low, blocks // 8, block_len, width),
+            room(low, blocks, block_len, cols),
+            room(low, groups, 3 * units, shard),
+            room(low, 3 * units, shard),
+            room(low, 3 * units, shard),
+            room(low, 3 * units, shard),
+            room(low, 4, groups, shard // 8, width),
+            room(low, 4, groups, shard // 8, width),
+            room(low, 4, groups, shard // 8, width),
+            room(low, groups, shard // 8, width),
+            room(low, groups, shard // 8, width),
+            room(low, groups, 3 * cols, shard),
+            room(low, 4 * shard, cols),
+            room(full, groups, 8, shard),
+            room(full, groups, 8, shard),
+            room(full, 8, shard),
+            room(full, 8, 8, shard),
             dma(9),
+            dma(4),
+            dma(2 * groups),
             pltpu.SemaphoreType.DMA((8, groups - 1)),
             pltpu.SemaphoreType.DMA((8, groups - 1)),
             dma(8),
-        ]
-        + [dma(10)] * 12
-        + [dma(7)] * 2
-        + [dma(4)] * 4,
+            dma(10),
+            dma(10),
+            dma(10),
+            dma(10),
+            dma(10),
+            dma(10),
+            dma(10),
+            dma(10),
+            dma(10),
+            dma(10),
+            dma(10),
+            dma(10),
+            dma(10),
+            dma(10),
+            dma(10),
+            dma(10),
+            dma(7),
+            dma(7),
+            dma(7),
+            dma(7),
+            dma(4),
+            dma(4),
+            dma(4),
+            dma(4),
+            dma(4),
+            dma(4),
+            dma(4),
+            dma(4),
+            dma(4),
+            dma(4),
+            dma(4),
+            dma(4),
+            dma(4),
+            dma(4),
+            dma(groups - 1),
+            dma(groups - 1),
+            dma(groups - 1),
+            dma(groups - 1),
+            dma(2),
+            pltpu.SemaphoreType.DMA((2, groups - 1)),
+            pltpu.SemaphoreType.DMA((2, groups - 1)),
+        ],
         compiler_params=pltpu.CompilerParams(
-            collective_id=0, has_side_effects=True, vmem_limit_bytes=66_000_000
+            collective_id=0, has_side_effects=True, vmem_limit_bytes=67_000_000
         ),
-        name="forward",
+        name="layer",
     )(
         slot_of,
         deal_table,
@@ -1817,100 +1855,6 @@
         w_down.reshape(8, part, width),
         gain_attn[None],
         gain_ffn[None],
-    )
-
-    layer, grad_rows, units_all, columns_all, gains_sum = pl.pallas_call(
-        functools.partial(backward_kernel, per_segment, groups),
-        out_shape=(
-            shaped(low, local_rows, width),
-            shaped(full, local_rows, width),
-            shaped(low, 8, 3 * units, shard),
-            shaped(low, 8, 4 * shard, cols),
-            shaped(full, 8, shard),
-        ),
-        in_specs=[smem] * 3 + [vmem] * 14,
-        out_specs=(vmem, vmem, anywhere, anywhere, vmem),
-        scratch_shapes=[
-            room(low, rows, 3 * cols),
-            room(low, blocks, block_len, cols),
-            room(low, blocks, block_len, cols),
-            room(low, blocks, block_len, cols),
-            room(low, blocks, block_len, cols),
-            room(low, tiles, cols, TILE),
-            room(full, rows, cols),
-            room(full, rows, cols),
-            room(low, groups, 3 * units, shard),
-            room(low, 3 * units, shard),
-            room(low, 3 * units, shard),
-            room(low, 3 * units, shard),
-            room(low, 4, local_rows, width),
-            room(low, 4, groups, shard // 8, width),
-            room(low, 4, groups, shard // 8, width),
-            room(low, 4, groups, shard // 8, width),
-            room(low, 4, groups, shard // 8, width),
-            room(low, groups, shard // 8, width),
-            room(low, groups, shard // 8, width),
-            room(low, 4, local_rows, width),
-            room(low, 4, local_rows, width),
-            room(full, local_rows, width),
-            room(low, 4, local_rows, width),
-            room(low, 2, local_rows, width),
-            room(low, 2, local_rows // 2, width),
-            room(low, 3 * cols, rows),
-            room(low, groups, 3 * cols, shard),
-            room(low, groups, 3 * cols, shard),
-            room(low, 4 * shard, cols),
-            room(full, groups, 8, shard),
-            room(full, groups, 8, shard),
-            room(full, 8, shard),
-            room(full, 8, 8, shard),
-            dma(2),
-            dma(groups - 1),
-            dma(groups - 1),
-            dma(2),
-            dma(4),
-            dma(4),
-            dma(4),
-            dma(4),
-            dma(4),
-            dma(4),
-            pltpu.SemaphoreType.DMA((2, groups - 1)),
-            pltpu.SemaphoreType.DMA((2, groups - 1)),
-            dma(4),
-            dma(4),
-            dma(4),
-            dma(4),
-            dma(10),
-            dma(10),
-            dma(10),
-            dma(10),
-            dma(groups - 1),
-            dma(groups - 1),
-            dma(7),
-            dma(7),
-        ],
-        compiler_params=pltpu.CompilerParams(
-            collective_id=1, has_side_effects=True, vmem_limit_bytes=66_000_000
-        ),
-        name="backward",
-    )(
-        slot_of,
-        deal_table,
-        prompt_len,
-        qkv,
-        grad_attn,
-        attn_t,
-        lse,
-        normed,
-        w_qkv,
-        gains,
-        patches[0],
-        grad_hidden,
-        hidden,
-        layer_sums,
-        grad_units,
-        grad_output,
-        gain_part,
     )
 
     weights = pl.pallas_call(
@@ -1931,7 +1875,8 @@
         ],
         name="place",
     )(units_all, columns_all)
-    return (layer[None], grad_rows[None]) + tuple(weights) + (gains_sum[0], gains_sum[1])
+    layer = layer.reshape(1, local_rows, width)
+    return (layer, grad_rows[None]) + tuple(weights) + (gains_sum[0], gains_sum[1])
 
 
 def solution(mesh):

time: 245 us -> 228 us (0.931)
  Pallas kernels: 236 us -> 220 us
    pallas_call x2 -> x1, Pallas kernels: 228 us -> 211 us  [heads_plan(): pl.pallas_call(functools.partial(layer_kernel, per_segment, groups), out_...]
where the time goes in v4:
time: 228 us
  Pallas kernels  220 us (96%)
  local copies, waits for them, and re-layouts  5.55 us (2%)
    pallas_call x1, Pallas kernels, heads_plan(): pl.pallas_call(functools.partial(layer_kernel, per_segment, groups), out_...  211 us
    pallas_call x1, Pallas kernels, heads_plan(): pl.pallas_call(functools.partial(place_kernel, groups), out_shape=tuple((...  8.71 us

profile of v4, /device:TPU:0, one launch (start us, length us, event | category | flops | bytes accessed | tf_op | source)
XLA Modules:
  0.0 228.2 jit_solution(13219369502150485186)
XLA Ops:
  1.3 1.3 select_reduce_fusion.slot_of
  2.6 1.2 broadcast_in_dim.26.gain_attn
  3.8 1.2 broadcast_in_dim.27.gain_ffn
  5.0 211.3 %layer.1 = (bf16[2048,1024]{1,0:T(8,128)(2,1)}, bf16[2,128,1024]{2,1,0:T(8,128)(2,1)}, f32[256,1024]{1,0:T(8,128)}, bf16[8,1056,256]{2,1,0:T(8,128)(2,1)}, bf16[...) custom-call(s32[16]{0:T(128)} %select_reduce_fusion.slot_of, s32[16]{0:T(128)} %block_of.1, s32[1]{0:T(128)S(6)} %copy.26.length_ref, ...), custom_call_target="tpu_custom_call" | custom-call | tf_op jit(solution)/shard_map/layer/pallas_call | solution.py:1725
  216.3 1.3 fusion
  217.7 0.0 copy-start.1
  217.7 0.0 copy-start
  217.7 8.7 %place.1 = (f32[256,1024]{1,0:T(8,128)}, f32[256,1024]{1,0:T(8,128)}, f32[256,1024]{1,0:T(8,128)}, f32[256,1024]{1,0:T(8,128)}, f32[256,2816]{1,0:T(8,128)}, /*index=5*/f32[256,2816]{1,0:T(8,128)}, f32[704,1024]{1,0:T(8,128)}) custom-call(bf16[8,1056,256]{2,1,0:T(8,128)(2,1)} %get-tuple-element.25.units_all, bf16[8,1024,128]{2,1,0:T(8,128)(2,1)} %get-tuple-element.26.columns_all), custom_call_target="tpu_custom_call" | custom-call | tf_op jit(solution)/shard_map/place/pallas_call | solution.py:1860
  226.4 0.0 copy-done.1
  226.4 0.8 copy.27
  227.2 0.0 copy-done
  227.2 1.0 copy.28
Async XLA Ops:
  217.7 8.7 %copy-start.1 = (bf16[2,128,1024]{2,1,0:T(8,128)(2,1)S(1)}, bf16[2,128,1024]{2,1,0:T(8,128)(2,1)}, u32[]{:S(2)}) copy-start(bf16[2,128,1024]{2,1,0:T(8,128)(2,1)} %get-tuple-element.23) | copy-start | bytes 1572868
  217.7 9.5 %copy-start = (f32[256,1024]{1,0:T(8,128)S(1)}, f32[256,1024]{1,0:T(8,128)}, u32[]{:S(2)}) copy-start(f32[256,1024]{1,0:T(8,128)} %get-tuple-element.24) | copy-start | bytes 3145732

commit v5 on v4

--- a/solution.py
+++ b/solution.py
@@ -1234,18 +1234,14 @@
     load_normed = pltpu.make_async_copy(normed_out, rows_all, local_sem.at[8])
     load_normed.start()
 
-    def units_tile(tile, unused):
+    def down_part(tile, unused):
         at = rows_of(tile, shard)
-        low = normed_ffn[:, at]
-        grad_units[tile, 0 : 2 * units, :] = dot_f32(units_t[units : 3 * units, :], low, 1, 0).astype(
-            jnp.bfloat16
-        )
         down_tile = dot_f32(units_t[0:units, :], grads[:, at], 1, 0)
         for half in (0, 1):
             own_sum[half, 0 : units // 2, at] = down_tile[half * units // 2 : (half + 1) * units // 2]
         return unused
 
-    lax.fori_loop(0, devices_fsdp, units_tile, 0)
+    lax.fori_loop(0, devices_fsdp, down_part, 0)
     for index in range(devices_fsdp):
         first = index % 2 * part
         grad_units[index, 2 * units : 3 * units, :] = jnp.concatenate(
@@ -1277,13 +1273,20 @@
     )
     units_sum_copy = units_copy(2, units_near)
 
-    @pl.when(place.at_end())
-    def _():
-        units_far_copy.start()
-        units_direct(2).start()
-
-    for step in (1, 3):
-        pl.when(place.near(step))(units_direct(step).start)
+    def units_tile(turn, unused):
+        step = jnp.where(turn < 2, 3 - 2 * turn, 6 - 2 * turn)
+        tile = place.other_group(step)
+        grad_units[tile, 0 : 2 * units, :] = dot_f32(
+            units_t[units : 3 * units, :], normed_ffn[:, rows_of(tile, shard)], 1, 0
+        ).astype(jnp.bfloat16)
+
+        for at, step in ((0, 3), (1, 1)):
+            pl.when((turn == at) & place.near(step))(units_direct(step).start)
+            pl.when((turn == at) & (group == 3 - step // 2 * 3))(units_far_copy.start)
+        pl.when((turn == 2) & place.at_end())(units_direct(2).start)
+        return unused
+
+    lax.fori_loop(0, devices_fsdp, units_tile, 0)
 
     total = sums.collect()
     values = hidden[...]
@@ -1399,6 +1402,52 @@
             ).astype(jnp.bfloat16)
             if pair:
                 output_pairs.deliver(pair).start()
+
+    def half_of(ref, lines):
+        def region(block, half):
+            return ref.at[block] if half is None else ref.at[block, halves(lines)(half)]
+
+        return region
+
+    def own_of(ref, lines):
+        return lambda half: ref if half is None else ref.at[halves(lines)(half)]
+
+    spread_u = Spread(
+        place,
+        own_of(units_stage, 3 * units),
+        half_of(units_out, 3 * units),
+        u_send,
+        u_recv,
+    )
+    save_units = pltpu.make_async_copy(units_stage, units_out.at[me], save_sem.at[0])
+    output_copies = over_groups(
+        lambda to: output_total.at[to], output_group, late_send.at[1], late_recv.at[1]
+    )
+
+    def before_last():
+        total = output_sums[0].astype(jnp.float32)
+        for pair in range(1, 4):
+            output_pairs.deliver(pair).wait_recv()
+            total = total + output_received[pair].astype(jnp.float32)
+        output_total[...] = total.astype(jnp.bfloat16)
+        for copy in output_copies:
+            copy.start()
+        units_landed[group] = grad_units[group]
+
+        @pl.when(place.at_end())
+        def _():
+            units_landed[devices_fsdp - 1 - group] = jnp.zeros_like(grad_units[group])
+
+        units_direct(2).wait_recv()
+        for step in (1, 3):
+            pl.when(place.heard(step))(units_direct(step).wait_recv)
+        units_total = units_landed[0].astype(jnp.float32)
+        for index in range(1, devices_fsdp):
+            units_total = units_total + units_landed[index].astype(jnp.float32)
+        units_stage[...] = units_total.astype(jnp.bfloat16)
+
+        spread_u.start()
+        save_units.start()
 
     attend_backward(
         per_segment,
@@ -1416,19 +1465,12 @@
         grad,
         value_t,
         own_sum,
-        {per_segment // 2: units_between, per_segment: after_prompt},
-    )
-
-    total = output_sums[0].astype(jnp.float32)
-    for pair in range(1, 4):
-        output_pairs.deliver(pair).wait_recv()
-        total = total + output_received[pair].astype(jnp.float32)
-    output_total[...] = total.astype(jnp.bfloat16)
-    output_copies = over_groups(
-        lambda to: output_total.at[to], output_group, late_send.at[1], late_recv.at[1]
-    )
-    for copy in output_copies:
-        copy.start()
+        {
+            per_segment // 2: units_between,
+            per_segment: after_prompt,
+            2 * per_segment - 1: before_last,
+        },
+    )
 
     def turn(tile, unused):
         at = rows_of(tile, TILE)
@@ -1454,6 +1496,7 @@
     )
     for copy in qkv_copies:
         copy.start()
+    spread_u.relay_first()
 
     def one_pair(step, unused):
         pair = 3 - step
@@ -1464,6 +1507,7 @@
         return unused
 
     lax.fori_loop(0, 4, one_pair, 0)
+    spread_u.relay_second()
 
     def sum_pair(step, unused):
         pair = 3 - step
@@ -1485,40 +1529,6 @@
             total = total + landed_ref[index].astype(jnp.float32)
         return total
 
-    units_landed[group] = grad_units[group]
-
-    @pl.when(place.at_end())
-    def _():
-        units_landed[devices_fsdp - 1 - group] = jnp.zeros_like(grad_units[group])
-
-    units_direct(2).wait_recv()
-    for step in (1, 3):
-        pl.when(place.heard(step))(units_direct(step).wait_recv)
-    units_total = units_landed[0].astype(jnp.float32)
-    for index in range(1, devices_fsdp):
-        units_total = units_total + units_landed[index].astype(jnp.float32)
-    units_stage[...] = units_total.astype(jnp.bfloat16)
-
-    def half_of(ref, lines):
-        def region(block, half):
-            return ref.at[block] if half is None else ref.at[block, halves(lines)(half)]
-
-        return region
-
-    def own_of(ref, lines):
-        return lambda half: ref if half is None else ref.at[halves(lines)(half)]
-
-    spread_u = Spread(
-        place,
-        own_of(units_stage, 3 * units),
-        half_of(units_out, 3 * units),
-        u_send,
-        u_recv,
-    )
-    spread_u.start()
-    save_units = pltpu.make_async_copy(units_stage, units_out.at[me], save_sem.at[0])
-    save_units.start()
-
     total = layer_sums[0].astype(jnp.float32)
     for pair, copy in enumerate(layer_copies):
         copy.wait_recv()
@@ -1528,6 +1538,24 @@
     save_layer = pltpu.make_async_copy(grad_rows, layer, save_sem.at[2])
     save_layer.start()
 
+    spread_u.relay_third()
+    turned = group_sum(qkv_parts(group)[...], qkv_landed, qkv_copies).T.astype(jnp.bfloat16)
+    for index in range(3):
+        columns_stage[index * shard : (index + 1) * shard, :] = turned[
+            :, index * cols : (index + 1) * cols
+        ]
+    summed = group_sum(output_total[group], output_group, output_copies).astype(jnp.bfloat16)
+    lines = shard // 8
+    for index in range(8):
+        columns_stage[3 * shard + index * lines : 3 * shard + (index + 1) * lines, :] = summed[
+            :, index * cols : (index + 1) * cols
+        ]
+    spread_c = Spread(
+        place, own_of(columns_stage, 4 * shard), half_of(columns_out, 4 * shard), c_send, c_recv
+    )
+    spread_c.start()
+    save_columns = pltpu.make_async_copy(columns_stage, columns_out.at[me], save_sem.at[1])
+    save_columns.start()
     total = sums.collect()
     values = patches[...].astype(jnp.float32)
     factor = lax.rsqrt(jnp.mean(values * values, axis=-1, keepdims=True) + epsilon)
@@ -1542,6 +1570,7 @@
     gain_copies = over_groups(lambda to: gain_parts.at[to], gain_landed, gain_send, gain_recv)
     for copy in gain_copies:
         copy.start()
+    spread_c.relay_first()
     grad_hidden[...] = (
         grad_hidden[...]
         + factor * scaled
@@ -1549,8 +1578,7 @@
     )
     save_rows = pltpu.make_async_copy(grad_hidden, grad_patches, save_sem.at[3])
     save_rows.start()
-    spread_u.relay_first()
-    spread_u.relay_second()
+    spread_c.relay_second()
     gain_total[...] = group_sum(gain_parts[group], gain_landed, gain_copies)
     gain_out = [
         remote(
@@ -1566,34 +1594,14 @@
         copy.start()
     gain_all[me] = gain_total[...]
 
-    turned = group_sum(qkv_parts(group)[...], qkv_landed, qkv_copies).T.astype(jnp.bfloat16)
-    for index in range(3):
-        columns_stage[index * shard : (index + 1) * shard, :] = turned[
-            :, index * cols : (index + 1) * cols
-        ]
-    summed = group_sum(output_total[group], output_group, output_copies).astype(jnp.bfloat16)
-    lines = shard // 8
-    for index in range(8):
-        columns_stage[3 * shard + index * lines : 3 * shard + (index + 1) * lines, :] = summed[
-            :, index * cols : (index + 1) * cols
-        ]
-    spread_c = Spread(
-        place, own_of(columns_stage, 4 * shard), half_of(columns_out, 4 * shard), c_send, c_recv
-    )
-    spread_c.start()
-    save_columns = pltpu.make_async_copy(columns_stage, columns_out.at[me], save_sem.at[1])
-    save_columns.start()
-    spread_u.relay_third()
+    spread_c.relay_third()
     for copy in gain_out:
         copy.wait_recv()
     gain_sum = gain_all[0]
     for index in range(1, 8):
         gain_sum = gain_sum + gain_all[index]
     gains_out[...] = gain_sum
-    spread_c.relay_first()
-    spread_c.relay_second()
     spread_u.arrived(0, 7, 8, 9)
-    spread_c.relay_third()
     spread_c.arrived(0, 7, 8, 9)
     for step in (1, 3):
         pl.when(place.near(step))(units_direct(step).wait_send)

time: 228 us -> 224 us (0.982)
  Pallas kernels: 220 us -> 216 us
    pallas_call x1, Pallas kernels: 211 us -> 207 us  [heads_plan(): pl.pallas_call(functools.partial(layer_kernel, per_segment, groups), out_...]
where the time goes in v5:
time: 224 us
  Pallas kernels  216 us (96%)
  local copies, waits for them, and re-layouts  5.55 us (2%)
    pallas_call x1, Pallas kernels, heads_plan(): pl.pallas_call(functools.partial(layer_kernel, per_segment, groups), out_...  207 us
    pallas_call x1, Pallas kernels, heads_plan(): pl.pallas_call(functools.partial(place_kernel, groups), out_shape=tuple((...  8.71 us

profile of v5, /device:TPU:0, one launch (start us, length us, event | category | flops | bytes accessed | tf_op | source)
XLA Modules:
  0.0 224.0 jit_solution(16867130360847695650)
XLA Ops:
  1.3 1.3 select_reduce_fusion.slot_of
  2.6 1.2 broadcast_in_dim.26.gain_attn
  3.8 1.2 broadcast_in_dim.27.gain_ffn
  5.0 207.1 %layer.1 = (bf16[2048,1024]{1,0:T(8,128)(2,1)}, bf16[2,128,1024]{2,1,0:T(8,128)(2,1)}, f32[256,1024]{1,0:T(8,128)}, bf16[8,1056,256]{2,1,0:T(8,128)(2,1)}, bf16[...) custom-call(s32[16]{0:T(128)} %select_reduce_fusion.slot_of, s32[16]{0:T(128)} %block_of.1, s32[1]{0:T(128)S(6)} %copy.26.length_ref, ...), custom_call_target="tpu_custom_call" | custom-call | tf_op jit(solution)/shard_map/layer/pallas_call | solution.py:1733
  212.1 1.3 fusion
  213.5 0.0 copy-start.1
  213.5 0.0 copy-start
  213.5 8.7 %place.1 = (f32[256,1024]{1,0:T(8,128)}, f32[256,1024]{1,0:T(8,128)}, f32[256,1024]{1,0:T(8,128)}, f32[256,1024]{1,0:T(8,128)}, f32[256,2816]{1,0:T(8,128)}, /*index=5*/f32[256,2816]{1,0:T(8,128)}, f32[704,1024]{1,0:T(8,128)}) custom-call(bf16[8,1056,256]{2,1,0:T(8,128)(2,1)} %get-tuple-element.25.units_all, bf16[8,1024,128]{2,1,0:T(8,128)(2,1)} %get-tuple-element.26.columns_all), custom_call_target="tpu_custom_call" | custom-call | tf_op jit(solution)/shard_map/place/pallas_call | solution.py:1868
  222.2 0.0 copy-done.1
  222.2 0.8 copy.27
  223.0 0.0 copy-done
  223.0 1.0 copy.28
Async XLA Ops:
  213.5 8.7 %copy-start.1 = (bf16[2,128,1024]{2,1,0:T(8,128)(2,1)S(1)}, bf16[2,128,1024]{2,1,0:T(8,128)(2,1)}, u32[]{:S(2)}) copy-start(bf16[2,128,1024]{2,1,0:T(8,128)(2,1)} %get-tuple-element.23) | copy-start | bytes 1572868
  213.5 9.5 %copy-start = (f32[256,1024]{1,0:T(8,128)S(1)}, f32[256,1024]{1,0:T(8,128)}, u32[]{:S(2)}) copy-start(f32[256,1024]{1,0:T(8,128)} %get-tuple-element.24) | copy-start | bytes 3145732

commit v6 on v5

--- a/solution.py
+++ b/solution.py
@@ -765,10 +765,21 @@
     return lambda half: pl.ds(0 if half in (None, 0) else count // 2, count if half is None else count // 2)
 
 
+def slots_of(block_of):
+    count = block_of.shape[0]
+    held = [block_of[slot] for slot in range(count)]
+    slots = []
+    for block in range(count):
+        found = jnp.int32(0)
+        for slot in range(1, count):
+            found = jnp.where(held[slot] == block, jnp.int32(slot), found)
+        slots.append(found)
+    return slots
+
+
 def layer_kernel(
     per_segment,
     devices_fsdp,
-    slot_of,
     block_of,
     length_ref,
     patches,
@@ -890,6 +901,7 @@
     late_recv,
 ):
     place = Place(devices_fsdp)
+    slot_of = slots_of(block_of)
     me, group = place.me, place.group
     local_rows, width = patches.shape
     cols = width // 8
@@ -1004,8 +1016,8 @@
 
     for index in (0, 1, 2):
         send_group(index)
-    gain_stage[0:8, :] = jnp.broadcast_to(gain_attn[...].astype(jnp.float32), (8, shard))
-    gain_stage[8:16, :] = jnp.broadcast_to(gain_ffn[...].astype(jnp.float32), (8, shard))
+    gain_stage[0:8, :] = jnp.broadcast_to(gain_attn[...].astype(jnp.float32)[None], (8, shard))
+    gain_stage[8:16, :] = jnp.broadcast_to(gain_ffn[...].astype(jnp.float32)[None], (8, shard))
     send_group(3)
     send_group(4)
 
@@ -1625,6 +1637,11 @@
     devices_fsdp,
     units_all,
     columns_all,
+    layer,
+    grad_rows,
+    gains,
+    out_layer,
+    out_rows,
     out_query,
     out_key,
     out_value,
@@ -1632,12 +1649,19 @@
     out_gate,
     out_up,
     out_down,
+    out_gain_attn,
+    out_gain_ffn,
+    units_held,
+    columns_held,
+    layer_held,
+    rows_held,
     columns,
     outputs,
     natural,
     gate,
     up,
     down,
+    load_sems,
     sems,
 ):
     shard = out_query.shape[0]
@@ -1646,39 +1670,59 @@
     units = units_all.shape[1] // 3
     part = units // devices_fsdp
     span = part * 8
+    loads = []
     saves = []
+
+    def load(source, target):
+        copy = pltpu.make_async_copy(source, target, load_sems.at[len(loads)])
+        copy.start()
+        loads.append(copy)
 
     def save(source, target):
         copy = pltpu.make_async_copy(source, target, sems.at[len(saves)])
         copy.start()
         saves.append(copy)
 
+    for which in (2, 0, 1):
+        load(units_all.at[:, which * units : (which + 1) * units], units_held.at[which])
+    load(columns_all, columns_held)
+    load(grad_rows, rows_held)
+    load(layer, layer_held)
+    out_gain_attn[...] = gains[0, :]
+    out_gain_ffn[...] = gains[1, :]
+    loads[0].wait()
     for index in range(8):
-        piece = units_all[index, 2 * units : 3 * units, :].astype(jnp.float32)
+        piece = units_held[2, index].astype(jnp.float32)
         for tile in range(devices_fsdp):
             down[index * part : (index + 1) * part, tile * shard : (tile + 1) * shard] = piece[
                 tile * part : (tile + 1) * part, :
             ]
     save(down, out_down)
     for which, (target, out) in enumerate(((gate, out_gate), (up, out_up))):
+        loads[1 + which].wait()
         for index in range(8):
-            piece = units_all[index, which * units : (which + 1) * units, :].astype(jnp.float32)
+            piece = units_held[which, index].astype(jnp.float32)
             for tile in range(devices_fsdp):
                 first = tile * span + index * part
                 natural[first : first + part, :] = piece[tile * part : (tile + 1) * part, :]
         for first in range(0, span * devices_fsdp, 128):
             target[:, first : first + 128] = natural[first : first + 128, :].T
         save(target, out)
+    loads[4].wait()
+    save(rows_held, out_rows)
+    loads[5].wait()
+    save(layer_held, out_layer)
+    loads[3].wait()
     for index in range(8):
         at = slice(index * cols, (index + 1) * cols)
         for which in range(3):
-            columns[which, :, at] = columns_all[
+            columns[which, :, at] = columns_held[
                 index, which * shard : (which + 1) * shard, :
             ].astype(jnp.float32)
         for tile in range(8):
             first = 3 * shard + tile * lines
             outputs[index * lines : (index + 1) * lines, tile * cols : (tile + 1) * cols] = (
-                columns_all[index, first : first + lines, :].astype(jnp.float32)
+                columns_held[index, first : first + lines, :].astype(jnp.float32)
             )
     save(columns.at[0], out_query)
     save(columns.at[1], out_key)
@@ -1715,10 +1759,6 @@
     blocks = deal_table.shape[0]
     block_len = rows // blocks
     per_segment = CONT_LEN // TILE
-    slots = jnp.arange(deal_table.shape[0], dtype=jnp.int32)
-    slot_of = jnp.sum(
-        jnp.where(deal_table[None, :] == slots[:, None], slots[None, :], 0), axis=1
-    ).astype(jnp.int32)
     smem = pl.BlockSpec(memory_space=pltpu.SMEM)
     vmem = pl.BlockSpec(memory_space=pltpu.VMEM)
     anywhere = pl.BlockSpec(memory_space=pl.ANY)
@@ -1740,7 +1780,7 @@
             shaped(low, 8, 4 * shard, cols),
             shaped(full, 8, shard),
         ),
-        in_specs=[smem] * 3 + [vmem] + [anywhere] * 8 + [vmem] * 2,
+        in_specs=[smem] * 2 + [vmem] + [anywhere] * 8 + [vmem] * 2,
         out_specs=(anywhere,) * 5 + (vmem,),
         scratch_shapes=[
             room(low, blocks, block_len, 3 * cols),
@@ -1849,7 +1889,6 @@
         ),
         name="layer",
     )(
-        slot_of,
         deal_table,
         prompt_len,
         patches[0],
@@ -1861,30 +1900,38 @@
         w_gate,
         w_up,
         w_down.reshape(8, part, width),
-        gain_attn[None],
-        gain_ffn[None],
-    )
-
-    weights = pl.pallas_call(
+        gain_attn,
+        gain_ffn,
+    )
+
+    results = pl.pallas_call(
         functools.partial(place_kernel, groups),
-        out_shape=tuple(shaped(full, shard, width) for _ in range(4))
+        out_shape=(
+            shaped(low, blocks // 8, block_len, width),
+            shaped(full, local_rows, width),
+        )
+        + tuple(shaped(full, shard, width) for _ in range(4))
         + tuple(shaped(full, shard, 8 * units) for _ in range(2))
-        + (shaped(full, 8 * part, width),),
-        in_specs=[vmem, vmem],
-        out_specs=(anywhere,) * 7,
+        + (shaped(full, 8 * part, width), shaped(full, shard), shaped(full, shard)),
+        in_specs=[anywhere] * 4 + [vmem],
+        out_specs=(anywhere,) * 9 + (vmem,) * 2,
         scratch_shapes=[
+            room(low, 3, 8, units, shard),
+            room(low, 8, 4 * shard, cols),
+            room(low, blocks // 8, block_len, width),
+            room(full, local_rows, width),
             room(full, 3, shard, width),
             room(full, shard, width),
             room(full, 8 * units, shard),
             room(full, shard, 8 * units),
             room(full, shard, 8 * units),
             room(full, 8 * part, width),
-            dma(7),
+            dma(6),
+            dma(9),
         ],
         name="place",
-    )(units_all, columns_all)
-    layer = layer.reshape(1, local_rows, width)
-    return (layer, grad_rows[None]) + tuple(weights) + (gains_sum[0], gains_sum[1])
+    )(units_all, columns_all, layer, grad_rows, gains_sum)
+    return (results[0].reshape(1, local_rows, width), results[1][None]) + tuple(results[2:])
 
 
 def solution(mesh):

time: 224 us -> 218 us (0.973)
  local copies, waits for them, and re-layouts: 5.55 us -> 0 us
    broadcast_in_dim x2 -> x0, local copies, waits for them, and re-layouts: 2.44 us -> none  [the longest x1 1.22 us: heads_plan(): gain_ffn[None]]
where the time goes in v6:
time: 218 us
  Pallas kernels  216 us (99%)
    pallas_call x1, Pallas kernels, heads_plan(): pl.pallas_call(functools.partial(layer_kernel, per_segment, groups), out_...  207 us
    pallas_call x1, Pallas kernels, heads_plan(): pl.pallas_call(functools.partial(place_kernel, groups), out_shape=(shaped...  8.93 us

profile of v6, /device:TPU:0, one launch (start us, length us, event | category | flops | bytes accessed | tf_op | source)
XLA Modules:
  0.0 217.9 jit_solution(12097313218165086146)
XLA Ops:
  1.3 207.4 %layer.1 = (bf16[2048,1024]{1,0:T(8,128)(2,1)}, bf16[2,128,1024]{2,1,0:T(8,128)(2,1)}, f32[256,1024]{1,0:T(8,128)}, bf16[8,1056,256]{2,1,0:T(8,128)(2,1)}, bf16[...) custom-call(s32[16]{0:T(128)} %block_of.1, s32[1]{0:T(128)S(6)} %copy.24.length_ref, bf16[256,1024]{1,0:T(8,128)(2,1)} %bitcast.7, ...), custom_call_target="tpu_custom_call" | custom-call | tf_op jit(solution)/shard_map/layer/pallas_call | solution.py:1773
  208.8 8.9 %place.1 = (bf16[2,128,1024]{2,1,0:T(8,128)(2,1)}, f32[256,1024]{1,0:T(8,128)}, f32[256,1024]{1,0:T(8,128)}, f32[256,1024]{1,0:T(8,128)}, f32[256,1024]{1,0:T(8,...) custom-call(bf16[8,1056,256]{2,1,0:T(8,128)(2,1)} %get-tuple-element, ...), custom_call_target="tpu_custom_call" | custom-call | tf_op jit(solution)/shard_map/place/pallas_call | solution.py:1907

commit v7 on v6

--- a/solution.py
+++ b/solution.py
@@ -1049,24 +1049,12 @@
     spread_x.relay_second()
     spread_g = Spread(place, own_half(cotangent), rows_half(grads), g_send, g_recv)
     spread_g.start()
-    spread_x.relay_third()
-    pass_group(4)
-    spread_x.arrived(0, 7, 8, 9)
     for index in (0, 1, 2, 3):
         group_arrived(index)
     gain_one = gains[0:1, :]
 
-    def output_half(block, half):
-        if half is None:
-            return output_all.at[:, block]
-        lines = output_all.shape[2]
-        return output_all.at[:, block, halves(lines)(half)]
-
-    group_arrived(4)
-    spread_o = Spread(place, lambda half: output_half(me, half), output_half, o_send, o_recv)
-    spread_o.start()
-
-    def project(block, unused):
+    def project(flip, unused):
+        block = place.peer(flip)
         at = rows_of(block)
         values = rows_all[at, :].astype(jnp.float32)
         low = rms_forward(values, gain_one)[0].astype(jnp.bfloat16)
@@ -1074,8 +1062,25 @@
         store_tile(qkv, block, dot_f32(low, w_qkv[...], 1, 0).astype(jnp.bfloat16))
         return unused
 
+    lax.fori_loop(0, 3, lambda index, kept: project(2 * index, kept), 0)
+    spread_x.relay_third()
+    pass_group(4)
+
+    def output_half(block, half):
+        if half is None:
+            return output_all.at[:, block]
+        lines = output_all.shape[2]
+        return output_all.at[:, block, halves(lines)(half)]
+
+    group_arrived(4)
+    spread_o = Spread(place, lambda half: output_half(me, half), output_half, o_send, o_recv)
+    spread_o.start()
+
+    spread_x.arrived(0, 7, 8)
+    lax.fori_loop(0, 3, lambda index, kept: project(2 * index + 1, kept), 0)
+    spread_x.arrived(9)
+    lax.fori_loop(6, 8, project, 0)
     spread_x.sent()
-    lax.fori_loop(0, 8, project, 0)
     save_normed = pltpu.make_async_copy(normed_ffn, normed_out, local_sem.at[8])
     save_normed.start()
     spread_g.relay_first()

time: 218 us -> 217 us (level)
  no operation moved by 1% of the time
where the time goes in v7:
time: 217 us
  Pallas kernels  215 us (99%)
    pallas_call x1, Pallas kernels, heads_plan(): pl.pallas_call(functools.partial(layer_kernel, per_segment, groups), out_...  206 us
    pallas_call x1, Pallas kernels, heads_plan(): pl.pallas_call(functools.partial(place_kernel, groups), out_shape=(shaped...  8.93 us

profile of v7, /device:TPU:0, one launch (start us, length us, event | category | flops | bytes accessed | tf_op | source)
XLA Modules:
  0.0 216.7 jit_solution(16876301089896365043)
XLA Ops:
  1.3 206.3 %layer.1 = (bf16[2048,1024]{1,0:T(8,128)(2,1)}, bf16[2,128,1024]{2,1,0:T(8,128)(2,1)}, f32[256,1024]{1,0:T(8,128)}, bf16[8,1056,256]{2,1,0:T(8,128)(2,1)}, bf16[...) custom-call(s32[16]{0:T(128)} %block_of.1, s32[1]{0:T(128)S(6)} %copy.24.length_ref, bf16[256,1024]{1,0:T(8,128)(2,1)} %bitcast.7, ...), custom_call_target="tpu_custom_call" | custom-call | tf_op jit(solution)/shard_map/layer/pallas_call | solution.py:1778
  207.6 8.9 %place.1 = (bf16[2,128,1024]{2,1,0:T(8,128)(2,1)}, f32[256,1024]{1,0:T(8,128)}, f32[256,1024]{1,0:T(8,128)}, f32[256,1024]{1,0:T(8,128)}, f32[256,1024]{1,0:T(8,...) custom-call(bf16[8,1056,256]{2,1,0:T(8,128)(2,1)} %get-tuple-element, ...), custom_call_target="tpu_custom_call" | custom-call | tf_op jit(solution)/shard_map/place/pallas_call | solution.py:1912
